TPU v7x, 256 devices: a whole 4x4x8 slice. The times are simulated.
256 devices in a mesh: src: 64 (over z, x, y_lo), tgt: 4 (over y_hi, core).
Axes of the slice: x: 4, y: 4 (y_hi: 2, y_lo: 2; y = y_hi * 2 + y_lo), z: 8, core: 2. Of those that a mesh axis runs over, the one named last changes fastest.
Arguments:
- src_feat: bfloat16 [131072, 768], P(('src', 'tgt')), may hold values from -6 to 6
- tgt_feat: bfloat16 [8192, 768], P(('tgt', 'src')), may hold values from -6 to 6
- rel_weight: bfloat16 [3, 768, 1024], replicated, may hold values from -0.21875 to 0.21875
- self_weight: bfloat16 [768, 1024], replicated, may hold values from -0.21875 to 0.21875
- adj_weight: bfloat16 [64, 64, 4, 128, 128], P('src', 'tgt'), may hold values from 0 to 0.009521484
- adj_source: int32 [64, 64, 4], P('src', 'tgt'), may hold values from 0 to 47
- adj_count: int32 [64, 64], P('src', 'tgt'), may hold values from 1 to 4
Outputs:
- hidden_out: bfloat16 [8192, 1024], P(('tgt', 'src'))
All inputs are finite; a program needn't handle non-finite values.
Results may differ from a plain program's by a relative error of at most 0.004.
Values may be sent and summed in bfloat16 or wider, within the bound.
No kernel may reach another device: no remote copies, remote signals or barrier semaphores. Data moves between devices by JAX's collectives and lax.ppermute only.
A program may use at most 128 MiB of HBM per device.

v0:
```python
import jax
import jax.numpy as jnp
from jax import lax
from jax.experimental import pallas as pl
from jax.experimental.pallas import tpu as pltpu
from jax.sharding import Mesh, PartitionSpec as P


HID = 1024
BLK = 128
REL = 3
NZ, NX, NY = 8, 4, 2
ROWS = 32
HA = 384
HB = HID - HA
PART = 12
F32 = jnp.float32
BF16 = jnp.bfloat16
SMEM = pl.BlockSpec(memory_space=pltpu.SMEM)
VMEM = pl.BlockSpec(memory_space=pltpu.VMEM)
HOPS = [(dx, dy) for dx in range(NX) for dy in range(NY)]


def transform_rows(f_ref, w_ref, cols, store):
    n = f_ref.shape[0] // BLK
    pairs = n // 2

    def step(i, _):
        r = i // pairs
        p = i - r * pairs
        y = jnp.dot(f_ref[pl.ds(p * 2 * BLK, 2 * BLK), :], w_ref[r, :, cols], preferred_element_type=F32)
        store(r * n + p * 2, y.astype(BF16).reshape(2, BLK, y.shape[1]))
        return 0

    lax.fori_loop(0, REL * pairs, step, 0)


def transform_kernel(f_ref, w_ref, ta_ref, tb_ref):
    def store(at, blocks):
        ta_ref[pl.ds(at, 2)] = blocks[:, :, :HA]
        tb_ref[pl.ds(at, 2)] = blocks[:, :, HA:]

    transform_rows(f_ref, w_ref, slice(0, HID), store)


def transform(feat, weight):
    return pl.pallas_call(
        transform_kernel,
        out_shape=tuple(jax.ShapeDtypeStruct((PART, BLK, n), BF16) for n in (HA, HB)),
        in_specs=[VMEM, VMEM],
        out_specs=(VMEM, VMEM),
        compiler_params=pltpu.CompilerParams(vmem_limit_bytes=24 << 20),
        cost_estimate=pl.CostEstimate(
            flops=2 * feat.size * HID * REL, transcendentals=0, bytes_accessed=8 << 20
        ),
    )(feat, weight)


def fill_table(parts, f_ref, w_ref, t_ref, sems, cols):
    copies = [
        pltpu.make_async_copy(part, t_ref.at[pl.ds(PART * q, PART)], sems.at[q]) for q, part in enumerate(parts)
    ]
    for copy in copies:
        copy.start()

    def store(at, blocks):
        t_ref[pl.ds(PART * len(parts) + at, 2)] = blocks

    transform_rows(f_ref, w_ref, cols, store)
    for copy in copies:
        copy.wait()


def weighted_sum(t, src_ref, cnt_ref, me, adj_ref, t_ref):
    slots = adj_ref.shape[1]
    weights, picked = [], []
    for k in range(slots):
        v = src_ref[t * slots + k]
        r = lax.shift_right_logical(v, 4)
        j = lax.bitwise_and(v, 15)
        q = lax.bitwise_xor(lax.shift_right_logical(j, 2), me)
        w = adj_ref[t, k]
        weights.append(jnp.where(k < cnt_ref[t], w, jnp.zeros_like(w)))
        picked.append(t_ref[q * PART + r * 4 + lax.bitwise_and(j, 3)])
    return jnp.dot(
        jnp.concatenate(weights, axis=1), jnp.concatenate(picked, axis=0), preferred_element_type=F32
    ).astype(BF16)


def sum_a_kernel(src_ref, cnt_ref, pos_ref, f_ref, w_ref, adj_ref, p0, p1, p2, a_ref, t_ref, sems):
    fill_table((p0, p1, p2), f_ref, w_ref, t_ref, sems, slice(0, HA))

    def step(t, _):
        got = weighted_sum(t, src_ref, cnt_ref, pos_ref[0], adj_ref, t_ref)
        a_ref[pl.ds(pl.multiple_of(t * BLK, BLK), BLK), :] = got
        return 0

    lax.fori_loop(0, adj_ref.shape[0], step, 0)


def hop_rows(pos_ref, dx, dy):
    x = lax.bitwise_and(pos_ref[1] + dx, NX - 1)
    y = lax.bitwise_xor(pos_ref[2], dy)
    return pl.multiple_of((x * NY + y) * ROWS, ROWS)


def sum_b_kernel(src_ref, cnt_ref, pos_ref, f_ref, w_ref, adj_ref, p0, p1, p2, *refs):
    b_refs, both, t_ref, sems = refs[:-3], refs[-3], refs[-2], refs[-1]
    fill_table((p0, p1, p2), f_ref, w_ref, t_ref, sems, slice(HA, HID))

    def step(z, _):
        for odd in range(2):
            both[odd * BLK : (odd + 1) * BLK, :] = weighted_sum(
                z * 2 + odd, src_ref, cnt_ref, pos_ref[0], adj_ref, t_ref
            )
        for (dx, dy), b_ref in zip(HOPS, b_refs):
            b_ref[pl.ds(pl.multiple_of(z * ROWS, ROWS), ROWS), :] = both[pl.ds(hop_rows(pos_ref, dx, dy), ROWS), :]
        return 0

    lax.fori_loop(0, NZ, step, 0)


def aggregate(kernel, outs, width, scratch, small, parts):
    return pl.pallas_call(
        kernel,
        out_shape=outs,
        in_specs=[SMEM] * 3 + [VMEM] * 3 + [pl.BlockSpec(memory_space=pl.ANY)] * 3,
        out_specs=jax.tree.map(lambda _: VMEM, outs),
        scratch_shapes=scratch
        + [pltpu.VMEM((4 * PART, BLK, width), BF16), pltpu.SemaphoreType.DMA((3,))],
        compiler_params=pltpu.CompilerParams(vmem_limit_bytes=32 << 20),
        cost_estimate=pl.CostEstimate(flops=6 * width << 20, transcendentals=0, bytes_accessed=16 << 20),
    )(*small, *parts)


def exchange(x, axes):
    return lax.all_to_all(x, axes, 0, 0, tiled=True)


def hop(x, dx, dy):
    pairs = [(i * NY + j, (i + dx) % NX * NY + (j ^ dy)) for i in range(NX) for j in range(NY)]
    return lax.ppermute(x, ("x", "yl"), pairs)


def layer(src_feat, tgt_feat, rel_weight, self_weight, adj_weight, adj_source, adj_count):
    swap = [(0, 1), (1, 0)]
    far = lax.ppermute(src_feat, "yh", swap)
    near = lax.ppermute(src_feat, "core", swap)
    diag = lax.ppermute(far, "core", swap)
    pos = jnp.stack(
        [lax.axis_index("yh") * 2 + lax.axis_index("core"), lax.axis_index("x"), lax.axis_index("yl")]
    ).astype(jnp.int32)
    parts = []
    for feat in (src_feat, near, far):
        parts.append(transform(feat, rel_weight))
    small = (adj_source.reshape(-1), adj_count.reshape(-1), pos, diag, rel_weight, adj_weight[0])
    outs = jax.ShapeDtypeStruct((NZ * 256, HA), BF16)
    out_a = aggregate(sum_a_kernel, outs, HA, [], small, [p[0] for p in parts])
    outs = tuple(jax.ShapeDtypeStruct((256, HB), BF16) for _ in HOPS)
    out_b = aggregate(sum_b_kernel, outs, HB, [pltpu.VMEM((256, HB), BF16)], small, [p[1] for p in parts])
    got_a = exchange(out_a.reshape(NZ, 256, HA), "z")
    got_b = [out_b[0]] + [hop(b, dx, dy) for b, (dx, dy) in zip(out_b[1:], HOPS[1:])]
    sum_a = got_a.astype(F32).sum(0).astype(BF16).reshape(NX * NY, ROWS, HA)
    sum_b = sum(b.astype(F32) for b in got_b).astype(BF16).reshape(NZ, ROWS, HB)
    last_a = exchange(sum_a, ("x", "yl"))
    last_b = exchange(sum_b, "z")
    end_a = last_a.astype(F32).sum(0)
    end_b = last_b.astype(F32).sum(0)
    summed = jnp.concatenate([end_a, end_b], axis=1)
    self_term = jnp.dot(tgt_feat, self_weight, preferred_element_type=F32)
    return jax.nn.relu(summed + self_term).astype(BF16)


def solution(mesh):
    fine = Mesh(mesh.devices.reshape(NZ, NX, NY, 2, 2), ("z", "x", "yl", "yh", "core"))
    src, tgt = ("z", "x", "yl"), ("yh", "core")
    return jax.shard_map(
        layer,
        mesh=fine,
        in_specs=(
            P(src + tgt, None),
            P(tgt + src, None),
            P(),
            P(),
            P(src, tgt, None, None, None),
            P(src, tgt, None),
            P(src, tgt),
        ),
        out_specs=P(tgt + src, None),
        check_vma=False,
    )
```

profile of v0, /device:TPU:16, one launch (start us, length us, event | category | flops | bytes accessed | tf_op | source)
XLA Modules:
  0.0 146.7 jit_solution(265126415697180870)
XLA Ops:
  0.0 2.0 %collective-permute-start = (bf16[512,768]{1,0:T(8,128)(2,1)}, bf16[512,768]{1,0:T(8,128)(2,1)S(1)}, u32[]{:S(2)}, u32[]{:S(2)}) collective-permute-start(bf16[512,768]{1,0:T(8,128)(2,1)} %f_ref.1), channel_id=1, source_target_pairs={{0,2},{2,0},{1,3},{3,1},{4,6},{6,4},{5,7},{7,5},{8,10},{10,8},{9,1... | collective-permute-start | bytes 2359304 | tf_op jit(solution)/shard_map/ppermute | solution.py:147
  2.9 18.1 %collective-permute-done.f_ref = bf16[512,768]{1,0:T(8,128)(2,1)S(1)} collective-permute-done((bf16[512,768]{1,0:T(8,128)(2,1)}, bf16[512,768]{1,0:T(8,128)(2,1)S(1)}, u32[]{:S(2)}, u32[]{:S(2)}) %collective-permute-start) | collective-permute-done | bytes 786464 | tf_op jit(solution)/shard_map/ppermute | solution.py:147
  21.1 2.3 %copy-done.1 = bf16[3,768,1024]{2,1,0:T(8,128)(2,1)S(1)} copy-done((bf16[3,768,1024]{2,1,0:T(8,128)(2,1)S(1)}, bf16[3,768,1024]{2,1,0:T(8,128)(2,1)}, u32[]{:S(2)}) %copy-start.1) | copy-done | bytes 4718616
  24.6 3.5 %shard_map.73 = (bf16[12,128,384]{2,1,0:T(8,128)(2,1)S(1)}, bf16[12,128,640]{2,1,0:T(8,128)(2,1)S(1)}) custom-call(bf16[512,768]{1,0:T(8,128)(2,1)S(1)} %copy-done.7, bf16[3,768,1024]{2,1,0:T(8,128)(2,1)S(1)} %copy-done.1), custom_call_target="tpu_custom_call" | custom-call | flops 2415919104 | bytes 8388608 | tf_op jit(solution)/shard_map/pallas_call | solution.py:47
  28.0 1.3 copy-done.8
  29.3 3.5 %shard_map.75 = (bf16[12,128,384]{2,1,0:T(8,128)(2,1)S(1)}, bf16[12,128,640]{2,1,0:T(8,128)(2,1)S(1)}) custom-call(bf16[512,768]{1,0:T(8,128)(2,1)S(1)} %collective-permute-done.f_ref, bf16[3,768,1024]{2,1,0:T(8,128)(2,1)S(1)} %copy-done.2), custom_call_target="tpu_custom_call" | custom-call | flops 2415919104 | bytes 8388608 | tf_op jit(solution)/shard_map/pallas_call | solution.py:47
  32.8 1.3 copy-done.10
  34.1 4.8 %shard_map.74 = (bf16[12,128,384]{2,1,0:T(8,128)(2,1)S(1)}, bf16[12,128,640]{2,1,0:T(8,128)(2,1)S(1)}) custom-call(bf16[512,768]{1,0:T(8,128)(2,1)} %collective-permute-done.2.f_ref, bf16[3,768,1024]{2,1,0:T(8,128)(2,1)S(1)} %copy-done.2), custom_call_target="tpu_custom_call" | custom-call | flops 2415919104 | bytes 8388608 | tf_op jit(solution)/shard_map/pallas_call | solution.py:47
  40.2 8.4 %shard_map.76 = bf16[2048,384]{1,0:T(8,128)(2,1)} custom-call(s32[64]{0:T(128)S(1)} %reshape.15.src_ref, s32[16]{0:T(128)S(1)} %bitcast.12, s32[3]{0:T(128)S(1)} %pad_add_fusion.pos_ref, bf16[512,768]{1,0:T(8,128)(2,1)S(1)} %collective-permute-done.1.f_ref, bf16[3,768,1024]{2,1,0:T(8,128)(2,1)S(1)} %copy-done.2, bf16[16,4,128,128]{3,2,1,0:T(8,128)(2,1)S(1)} %bitcast.10, ...), custom_call_target="tpu_custom_call" | custom-call | flops 2415919104 | bytes 16777216 | tf_op jit(solution)/shard_map/pallas_call | solution.py:124
  48.7 8.5 %all-to-all-start = ((bf16[8,256,384]{2,1,0:T(8,128)(2,1)}), bf16[8,256,384]{2,1,0:T(8,128)(2,1)}, u32[]{:S(2)}, u32[]{:S(2)}) async-start(bf16[8,256,384]{2,1,0:T(8,128)(2,1)} %bitcast.5), calls=%async_computation | async-start | bytes 3145728 | tf_op jit(solution)/shard_map/all_to_all | solution.py:137
  57.1 2.3 %copy-done.3 = bf16[3,768,1024]{2,1,0:T(8,128)(2,1)S(1)} copy-done((bf16[3,768,1024]{2,1,0:T(8,128)(2,1)S(1)}, bf16[3,768,1024]{2,1,0:T(8,128)(2,1)}, u32[]{:S(2)}) %copy-start.3) | copy-done | bytes 4718616
  59.5 1.6 %copy-done.5 = bf16[1,16,4,128,128]{4,3,2,1,0:T(8,128)(2,1)S(1)} copy-done((bf16[1,16,4,128,128]{4,3,2,1,0:T(8,128)(2,1)S(1)}, bf16[1,16,4,128,128]{4,3,2,1,0:T(8,128)(2,1)}, u32[]{:S(2)}) %copy-start.5) | copy-done | bytes 2097176
  61.1 1.5 %copy-done.9 = bf16[12,128,640]{2,1,0:T(8,128)(2,1)S(1)} copy-done((bf16[12,128,640]{2,1,0:T(8,128)(2,1)S(1)}, bf16[12,128,640]{2,1,0:T(8,128)(2,1)}, u32[]{:S(2)}) %copy-start.9) | copy-done | bytes 1966104
  62.6 1.5 %copy-done.11 = bf16[12,128,640]{2,1,0:T(8,128)(2,1)S(1)} copy-done((bf16[12,128,640]{2,1,0:T(8,128)(2,1)S(1)}, bf16[12,128,640]{2,1,0:T(8,128)(2,1)}, u32[]{:S(2)}) %copy-start.11) | copy-done | bytes 1966104
  64.2 1.5 %copy-done.13 = bf16[12,128,640]{2,1,0:T(8,128)(2,1)S(1)} copy-done((bf16[12,128,640]{2,1,0:T(8,128)(2,1)S(1)}, bf16[12,128,640]{2,1,0:T(8,128)(2,1)}, u32[]{:S(2)}) %copy-start.13) | copy-done | bytes 1966104
  65.7 7.7 %shard_map.77 = (bf16[256,640]{1,0:T(8,128)(2,1)S(1)}, bf16[256,640]{1,0:T(8,128)(2,1)S(1)}, bf16[256,640]{1,0:T(8,128)(2,1)S(1)}, bf16[256,640]{1,0:T(8,128)(2,...) custom-call(s32[64]{0:T(128)S(1)} %reshape.15.src_ref, ...), custom_call_target="tpu_custom_call" | custom-call | flops 4026531840 | bytes 16777216 | tf_op jit(solution)/shard_map/pallas_call | solution.py:124
  73.4 1.4 collective-permute-start.3
  74.8 1.5 %collective-permute-start.4 = (bf16[256,640]{1,0:T(8,128)(2,1)S(1)}, bf16[256,640]{1,0:T(8,128)(2,1)S(1)}, u32[]{:S(2)}, u32[]{:S(2)}) collective-permute-start(bf16[256,640]{1,0:T(8,128)(2,1)S(1)} %get-tuple-element.27), channel_id=1, source_target_pairs={{0,8},{4,12},{8,16},{12,20},{16,24},{20,28},{24,0},{28,4},{1,9},{5... | collective-permute-start | bytes 983048 | tf_op jit(solution)/shard_map/ppermute | solution.py:142
  76.3 1.7 %collective-permute-start.5 = (bf16[256,640]{1,0:T(8,128)(2,1)S(1)}, bf16[256,640]{1,0:T(8,128)(2,1)S(1)}, u32[]{:S(2)}, u32[]{:S(2)}) collective-permute-start(bf16[256,640]{1,0:T(8,128)(2,1)S(1)} %get-tuple-element.28), channel_id=1, source_target_pairs={{0,12},{4,8},{8,20},{12,16},{16,28},{20,24},{24,4},{28,0},{1,13},{... | collective-permute-start | bytes 983048 | tf_op jit(solution)/shard_map/ppermute | solution.py:142
  77.9 1.7 %collective-permute-start.6 = (bf16[256,640]{1,0:T(8,128)(2,1)S(1)}, bf16[256,640]{1,0:T(8,128)(2,1)S(1)}, u32[]{:S(2)}, u32[]{:S(2)}) collective-permute-start(bf16[256,640]{1,0:T(8,128)(2,1)S(1)} %get-tuple-element.29), channel_id=1, source_target_pairs={{0,16},{4,20},{8,24},{12,28},{16,0},{20,4},{24,8},{28,12},{1,17},{... | collective-permute-start | bytes 983048 | tf_op jit(solution)/shard_map/ppermute | solution.py:142
  79.6 2.5 %collective-permute-start.7 = (bf16[256,640]{1,0:T(8,128)(2,1)S(1)}, bf16[256,640]{1,0:T(8,128)(2,1)S(1)}, u32[]{:S(2)}, u32[]{:S(2)}) collective-permute-start(bf16[256,640]{1,0:T(8,128)(2,1)S(1)} %get-tuple-element.30), channel_id=1, source_target_pairs={{0,20},{4,16},{8,28},{12,24},{16,4},{20,0},{24,12},{28,8},{1,21},{... | collective-permute-start | bytes 983048 | tf_op jit(solution)/shard_map/ppermute | solution.py:142
  83.3 2.8 %collective-permute-start.8 = (bf16[256,640]{1,0:T(8,128)(2,1)S(1)}, bf16[256,640]{1,0:T(8,128)(2,1)S(1)}, u32[]{:S(2)}, u32[]{:S(2)}) collective-permute-start(bf16[256,640]{1,0:T(8,128)(2,1)S(1)} %get-tuple-element.31), channel_id=1, source_target_pairs={{0,24},{4,28},{8,0},{12,4},{16,8},{20,12},{24,16},{28,20},{1,25},{... | collective-permute-start | bytes 983048 | tf_op jit(solution)/shard_map/ppermute | solution.py:142
  86.6 1.7 %collective-permute-start.9 = (bf16[256,640]{1,0:T(8,128)(2,1)S(1)}, bf16[256,640]{1,0:T(8,128)(2,1)S(1)}, u32[]{:S(2)}, u32[]{:S(2)}) collective-permute-start(bf16[256,640]{1,0:T(8,128)(2,1)S(1)} %get-tuple-element.32), channel_id=1, source_target_pairs={{0,28},{4,24},{8,4},{12,0},{16,12},{20,8},{24,20},{28,16},{1,29},{... | collective-permute-start | bytes 983048 | tf_op jit(solution)/shard_map/ppermute | solution.py:142
  88.3 5.4 %collective-permute-done.5 = bf16[256,640]{1,0:T(8,128)(2,1)S(1)} collective-permute-done((bf16[256,640]{1,0:T(8,128)(2,1)S(1)}, bf16[256,640]{1,0:T(8,128)(2,1)S(1)}, u32[]{:S(2)}, u32[]{:S(2)}) %collective-permute-start.5) | collective-permute-done | bytes 327712 | tf_op jit(solution)/shard_map/ppermute | solution.py:142
  93.6 12.1 %collective-permute-done.6 = bf16[256,640]{1,0:T(8,128)(2,1)S(1)} collective-permute-done((bf16[256,640]{1,0:T(8,128)(2,1)S(1)}, bf16[256,640]{1,0:T(8,128)(2,1)S(1)}, u32[]{:S(2)}, u32[]{:S(2)}) %collective-permute-start.6) | collective-permute-done | bytes 327712 | tf_op jit(solution)/shard_map/ppermute | solution.py:142
  105.7 9.2 %collective-permute-done.7 = bf16[256,640]{1,0:T(8,128)(2,1)S(1)} collective-permute-done((bf16[256,640]{1,0:T(8,128)(2,1)S(1)}, bf16[256,640]{1,0:T(8,128)(2,1)S(1)}, u32[]{:S(2)}, u32[]{:S(2)}) %collective-permute-start.7) | collective-permute-done | bytes 327712 | tf_op jit(solution)/shard_map/ppermute | solution.py:142
  114.9 1.6 %collective-permute-done.9 = bf16[256,640]{1,0:T(8,128)(2,1)S(1)} collective-permute-done((bf16[256,640]{1,0:T(8,128)(2,1)S(1)}, bf16[256,640]{1,0:T(8,128)(2,1)S(1)}, u32[]{:S(2)}, u32[]{:S(2)}) %collective-permute-start.9) | collective-permute-done | bytes 327712 | tf_op jit(solution)/shard_map/ppermute | solution.py:142
  117.5 6.5 %all-to-all-start.2 = ((bf16[8,32,640]{2,1,0:T(8,128)(2,1)}), bf16[8,32,640]{2,1,0:T(8,128)(2,1)S(1)}, u32[]{:S(2)}, u32[]{:S(2)}) async-start(bf16[8,32,640]{2,1,0:T(8,128)(2,1)} %bitcast.7), calls=%async_computation.2 | async-start | bytes 655360 | tf_op jit(solution)/shard_map/all_to_all | solution.py:137
  124.0 2.3 %reduce_sum.30 = bf16[256,384]{1,0:T(8,128)(2,1)} reduce(bf16[8,256,384]{2,1,0:T(8,128)(2,1)} %all-to-all-done, bf16[]{:T(256)} %constant.20.clone.1), dimensions={0}, to_apply=%region_0.0 | reduce | flops 688128 | bytes 1769474 | tf_op jit(solution)/shard_map/reduce_sum | solution.py:163
  126.4 8.8 %all-to-all-done.2 = bf16[8,32,640]{2,1,0:T(8,128)(2,1)S(1)} async-done(((bf16[8,32,640]{2,1,0:T(8,128)(2,1)}), bf16[8,32,640]{2,1,0:T(8,128)(2,1)S(1)}, u32[]{:S(2)}, u32[]{:S(2)}) %all-to-all-start.2) | async-done | bytes 327712 | tf_op jit(solution)/shard_map/all_to_all | solution.py:137
  135.2 3.7 %all-to-all-start.1 = ((bf16[8,32,384]{2,1,0:T(8,128)(2,1)}), bf16[8,32,384]{2,1,0:T(8,128)(2,1)S(1)}, u32[]{:S(2)}, u32[]{:S(2)}) async-start(bf16[8,32,384]{2,1,0:T(8,128)(2,1)} %bitcast.6), calls=%async_computation.1 | async-start | bytes 393216 | tf_op jit(solution)/shard_map/all_to_all | solution.py:137
  139.0 6.6 %all-to-all-done.1 = bf16[8,32,384]{2,1,0:T(8,128)(2,1)S(1)} async-done(((bf16[8,32,384]{2,1,0:T(8,128)(2,1)}), bf16[8,32,384]{2,1,0:T(8,128)(2,1)S(1)}, u32[]{:S(2)}, u32[]{:S(2)}) %all-to-all-start.1) | async-done | bytes 196640 | tf_op jit(solution)/shard_map/all_to_all | solution.py:137
  (37 shorter events, 7.2 us)
Async XLA Ops:
  0.0 145.6 %copy-start = (bf16[768,1024]{1,0:T(8,128)(2,1)S(1)}, bf16[768,1024]{1,0:T(8,128)(2,1)}, u32[]{:S(2)}) copy-start(bf16[768,1024]{1,0:T(8,128)(2,1)} %param.10) | copy-start | bytes 4718596
  0.0 21.0 %collective-permute-start = (bf16[512,768]{1,0:T(8,128)(2,1)}, bf16[512,768]{1,0:T(8,128)(2,1)S(1)}, u32[]{:S(2)}, u32[]{:S(2)}) collective-permute-start(bf16[512,768]{1,0:T(8,128)(2,1)} %f_ref.1), channel_id=1, source_target_pairs={{0,2},{2,0},{1,3},{3,1},{4,6},{6,4},{5,7},{7,5},{8,10},{10,8},{9,1... | collective-permute-start | bytes 2359304 | tf_op jit(solution)/shard_map/ppermute | solution.py:147
  2.0 32.0 %collective-permute-start.2 = (bf16[512,768]{1,0:T(8,128)(2,1)}, bf16[512,768]{1,0:T(8,128)(2,1)}, u32[]{:S(2)}, u32[]{:S(2)}) collective-permute-start(bf16[512,768]{1,0:T(8,128)(2,1)} %f_ref.1), channel_id=1, source_target_pairs={{0,1},{1,0},{2,3},{3,2},{4,5},{5,4},{6,7},{7,6},{8,9},{9,8},{10,11... | collective-permute-start | bytes 2359304 | tf_op jit(solution)/shard_map/ppermute | solution.py:148
  21.0 19.2 %collective-permute-start.1 = (bf16[512,768]{1,0:T(8,128)(2,1)S(1)}, bf16[512,768]{1,0:T(8,128)(2,1)S(1)}, u32[]{:S(2)}, u32[]{:S(2)}) collective-permute-start(bf16[512,768]{1,0:T(8,128)(2,1)S(1)} %collective-permute-done.f_ref), channel_id=1, source_target_pairs={{0,1},{1,0},{2,3},{3,2},{4,5},{5,4},{6,7},{7,6},{8,9},{9,8},{10,11... | collective-permute-start | bytes 2359304 | tf_op jit(solution)/shard_map/ppermute | solution.py:149
  21.1 2.3 %copy-start.1 = (bf16[3,768,1024]{2,1,0:T(8,128)(2,1)S(1)}, bf16[3,768,1024]{2,1,0:T(8,128)(2,1)}, u32[]{:S(2)}) copy-start(bf16[3,768,1024]{2,1,0:T(8,128)(2,1)} %w_ref.9) | copy-start | bytes 14155780
  23.4 1.1 copy-start.7
  24.6 4.8 %copy-start.2 = (bf16[3,768,1024]{2,1,0:T(8,128)(2,1)S(1)}, bf16[3,768,1024]{2,1,0:T(8,128)(2,1)}, u32[]{:S(2)}) copy-start(bf16[3,768,1024]{2,1,0:T(8,128)(2,1)} %w_ref.9) | copy-start | bytes 14155780
  28.0 1.3 copy-start.8
  32.8 1.3 copy-start.10
  34.1 6.1 %copy-start.4 = (bf16[1,16,4,128,128]{4,3,2,1,0:T(8,128)(2,1)S(1)}, bf16[1,16,4,128,128]{4,3,2,1,0:T(8,128)(2,1)}, u32[]{:S(2)}) copy-start(bf16[1,16,4,128,128]{4,3,2,1,0:T(8,128)(2,1)} %param.11) | copy-start | bytes 6291460
  34.1 6.1 %copy-start.6 = (s32[1,16]{1,0:T(1,128)S(1)}, s32[1,16]{1,0:T(1,128)}, u32[]{:S(2)}) copy-start(s32[1,16]{1,0:T(1,128)} %param.13) | copy-start | bytes 196
  38.9 1.3 copy-start.12
  48.7 68.9 %all-to-all-start = ((bf16[8,256,384]{2,1,0:T(8,128)(2,1)}), bf16[8,256,384]{2,1,0:T(8,128)(2,1)}, u32[]{:S(2)}, u32[]{:S(2)}) async-start(bf16[8,256,384]{2,1,0:T(8,128)(2,1)} %bitcast.5), calls=%async_computation | async-start | bytes 3145728 | tf_op jit(solution)/shard_map/all_to_all | solution.py:137
  57.1 2.3 %copy-start.3 = (bf16[3,768,1024]{2,1,0:T(8,128)(2,1)S(1)}, bf16[3,768,1024]{2,1,0:T(8,128)(2,1)}, u32[]{:S(2)}) copy-start(bf16[3,768,1024]{2,1,0:T(8,128)(2,1)} %w_ref.9) | copy-start | bytes 14155780
  59.5 1.6 %copy-start.5 = (bf16[1,16,4,128,128]{4,3,2,1,0:T(8,128)(2,1)S(1)}, bf16[1,16,4,128,128]{4,3,2,1,0:T(8,128)(2,1)}, u32[]{:S(2)}) copy-start(bf16[1,16,4,128,128]{4,3,2,1,0:T(8,128)(2,1)} %param.11) | copy-start | bytes 6291460
  61.1 1.5 %copy-start.9 = (bf16[12,128,640]{2,1,0:T(8,128)(2,1)S(1)}, bf16[12,128,640]{2,1,0:T(8,128)(2,1)}, u32[]{:S(2)}) copy-start(bf16[12,128,640]{2,1,0:T(8,128)(2,1)} %copy-done.8) | copy-start | bytes 5898244
  62.6 1.5 %copy-start.11 = (bf16[12,128,640]{2,1,0:T(8,128)(2,1)S(1)}, bf16[12,128,640]{2,1,0:T(8,128)(2,1)}, u32[]{:S(2)}) copy-start(bf16[12,128,640]{2,1,0:T(8,128)(2,1)} %copy-done.10) | copy-start | bytes 5898244
  64.1 1.5 %copy-start.13 = (bf16[12,128,640]{2,1,0:T(8,128)(2,1)S(1)}, bf16[12,128,640]{2,1,0:T(8,128)(2,1)}, u32[]{:S(2)}) copy-start(bf16[12,128,640]{2,1,0:T(8,128)(2,1)} %copy-done.12) | copy-start | bytes 5898244
  73.4 9.9 %collective-permute-start.3 = (bf16[256,640]{1,0:T(8,128)(2,1)S(1)}, bf16[256,640]{1,0:T(8,128)(2,1)S(1)}, u32[]{:S(2)}, u32[]{:S(2)}) collective-permute-start(bf16[256,640]{1,0:T(8,128)(2,1)S(1)} %get-tuple-element.26), channel_id=1, source_target_pairs={{0,4},{4,0},{8,12},{12,8},{16,20},{20,16},{24,28},{28,24},{1,5},{5... | collective-permute-start | bytes 983048 | tf_op jit(solution)/shard_map/ppermute | solution.py:142
  74.8 11.8 %collective-permute-start.4 = (bf16[256,640]{1,0:T(8,128)(2,1)S(1)}, bf16[256,640]{1,0:T(8,128)(2,1)S(1)}, u32[]{:S(2)}, u32[]{:S(2)}) collective-permute-start(bf16[256,640]{1,0:T(8,128)(2,1)S(1)} %get-tuple-element.27), channel_id=1, source_target_pairs={{0,8},{4,12},{8,16},{12,20},{16,24},{20,28},{24,0},{28,4},{1,9},{5... | collective-permute-start | bytes 983048 | tf_op jit(solution)/shard_map/ppermute | solution.py:142
  76.3 17.4 %collective-permute-start.5 = (bf16[256,640]{1,0:T(8,128)(2,1)S(1)}, bf16[256,640]{1,0:T(8,128)(2,1)S(1)}, u32[]{:S(2)}, u32[]{:S(2)}) collective-permute-start(bf16[256,640]{1,0:T(8,128)(2,1)S(1)} %get-tuple-element.28), channel_id=1, source_target_pairs={{0,12},{4,8},{8,20},{12,16},{16,28},{20,24},{24,4},{28,0},{1,13},{... | collective-permute-start | bytes 983048 | tf_op jit(solution)/shard_map/ppermute | solution.py:142
  77.9 27.8 %collective-permute-start.6 = (bf16[256,640]{1,0:T(8,128)(2,1)S(1)}, bf16[256,640]{1,0:T(8,128)(2,1)S(1)}, u32[]{:S(2)}, u32[]{:S(2)}) collective-permute-start(bf16[256,640]{1,0:T(8,128)(2,1)S(1)} %get-tuple-element.29), channel_id=1, source_target_pairs={{0,16},{4,20},{8,24},{12,28},{16,0},{20,4},{24,8},{28,12},{1,17},{... | collective-permute-start | bytes 983048 | tf_op jit(solution)/shard_map/ppermute | solution.py:142
  79.6 35.2 %collective-permute-start.7 = (bf16[256,640]{1,0:T(8,128)(2,1)S(1)}, bf16[256,640]{1,0:T(8,128)(2,1)S(1)}, u32[]{:S(2)}, u32[]{:S(2)}) collective-permute-start(bf16[256,640]{1,0:T(8,128)(2,1)S(1)} %get-tuple-element.30), channel_id=1, source_target_pairs={{0,20},{4,16},{8,28},{12,24},{16,4},{20,0},{24,12},{28,8},{1,21},{... | collective-permute-start | bytes 983048 | tf_op jit(solution)/shard_map/ppermute | solution.py:142
  83.3 31.6 %collective-permute-start.8 = (bf16[256,640]{1,0:T(8,128)(2,1)S(1)}, bf16[256,640]{1,0:T(8,128)(2,1)S(1)}, u32[]{:S(2)}, u32[]{:S(2)}) collective-permute-start(bf16[256,640]{1,0:T(8,128)(2,1)S(1)} %get-tuple-element.31), channel_id=1, source_target_pairs={{0,24},{4,28},{8,0},{12,4},{16,8},{20,12},{24,16},{28,20},{1,25},{... | collective-permute-start | bytes 983048 | tf_op jit(solution)/shard_map/ppermute | solution.py:142
  86.6 29.9 %collective-permute-start.9 = (bf16[256,640]{1,0:T(8,128)(2,1)S(1)}, bf16[256,640]{1,0:T(8,128)(2,1)S(1)}, u32[]{:S(2)}, u32[]{:S(2)}) collective-permute-start(bf16[256,640]{1,0:T(8,128)(2,1)S(1)} %get-tuple-element.32), channel_id=1, source_target_pairs={{0,28},{4,24},{8,4},{12,0},{16,12},{20,8},{24,20},{28,16},{1,29},{... | collective-permute-start | bytes 983048 | tf_op jit(solution)/shard_map/ppermute | solution.py:142
  117.5 17.7 %all-to-all-start.2 = ((bf16[8,32,640]{2,1,0:T(8,128)(2,1)}), bf16[8,32,640]{2,1,0:T(8,128)(2,1)S(1)}, u32[]{:S(2)}, u32[]{:S(2)}) async-start(bf16[8,32,640]{2,1,0:T(8,128)(2,1)} %bitcast.7), calls=%async_computation.2 | async-start | bytes 655360 | tf_op jit(solution)/shard_map/all_to_all | solution.py:137
  124.0 21.6 %copy-start.14 = (bf16[32,768]{1,0:T(8,128)(2,1)S(1)}, bf16[32,768]{1,0:T(8,128)(2,1)}, u32[]{:S(2)}) copy-start(bf16[32,768]{1,0:T(8,128)(2,1)} %param.8) | copy-start | bytes 147460
  135.2 10.4 %all-to-all-start.1 = ((bf16[8,32,384]{2,1,0:T(8,128)(2,1)}), bf16[8,32,384]{2,1,0:T(8,128)(2,1)S(1)}, u32[]{:S(2)}, u32[]{:S(2)}) async-start(bf16[8,32,384]{2,1,0:T(8,128)(2,1)} %bitcast.6), calls=%async_computation.1 | async-start | bytes 393216 | tf_op jit(solution)/shard_map/all_to_all | solution.py:137
where the time goes:
time: 147 us
  waiting for transfers between devices  63.3 us (43%)
  starting transfers between devices  34 us (23%)
  Pallas kernels  27.9 us (19%)
  local copies, waits for them, and re-layouts  16.7 us (11%)
  other arithmetic  3.58 us (2%)
    ppermute x7, waiting for transfers between devices, hop(): return lax.ppermute(x, ('x', 'yl'), pairs)  29.8 us
    all_to_all x3, starting transfers between devices, exchange(): return lax.all_to_all(x, axes, 0, 0, tiled=True)  18.7 us
    ppermute x1, waiting for transfers between devices, layer(): far = lax.ppermute(src_feat, 'yh', swap)  18.1 us
    unnamed x31, local copies, waits for them, and re-layouts  16.6 us
    pallas_call x2, Pallas kernels, aggregate(): pl.pallas_call(kernel, out_shape=outs, in_specs=[SMEM] * 3 + [VMEM] * 3 +...  16.1 us
    all_to_all x3, waiting for transfers between devices, exchange(): return lax.all_to_all(x, axes, 0, 0, tiled=True)  15.5 us
    ppermute x7, starting transfers between devices, hop(): return lax.ppermute(x, ('x', 'yl'), pairs)  13.3 us
    pallas_call x3, Pallas kernels, transform(): pl.pallas_call(transform_kernel, out_shape=tuple((jax.ShapeDtypeStruct((P...  11.7 us
  transfers between devices with their start and end apart: 13, of which 9 were waited for; matrix products, arithmetic and copies ran while one was open for 3% of the time, Pallas kernels for 13%

commit v1 on v0

v1 whole, which is shorter than its diff:
```python
import jax
import jax.numpy as jnp
from jax import lax
from jax.experimental import pallas as pl
from jax.experimental.pallas import tpu as pltpu
from jax.sharding import Mesh, PartitionSpec as P


HID = 1024
BLK = 128
REL = 3
NZ, NX, NY = 8, 4, 2
ROWS = 32
HA = 384
HB = HID - HA
PART = 12
F32 = jnp.float32
BF16 = jnp.bfloat16
SMEM = pl.BlockSpec(memory_space=pltpu.SMEM)
VMEM = pl.BlockSpec(memory_space=pltpu.VMEM)
HOPS = [(0, 0), (2, 1), (2, 0), (1, 1), (3, 1), (1, 0), (3, 0), (0, 1)]


def transform_rows(f_ref, w_ref, t_ref, base):
    n = f_ref.shape[0] // BLK
    pairs = n // 2

    def step(i, _):
        r = i // pairs
        p = i - r * pairs
        y = jnp.dot(f_ref[pl.ds(p * 2 * BLK, 2 * BLK), :], w_ref[r], preferred_element_type=F32)
        t_ref[pl.ds(base + r * n + p * 2, 2)] = y.astype(BF16).reshape(2, BLK, HID)
        return 0

    lax.fori_loop(0, REL * pairs, step, 0)


def transform_kernel(f_ref, w_ref, t_ref):
    transform_rows(f_ref, w_ref, t_ref, 0)


def transform(feat, weight):
    return pl.pallas_call(
        transform_kernel,
        out_shape=jax.ShapeDtypeStruct((PART, BLK, HID), BF16),
        in_specs=[VMEM, VMEM],
        out_specs=VMEM,
        compiler_params=pltpu.CompilerParams(vmem_limit_bytes=8 << 20),
        cost_estimate=pl.CostEstimate(
            flops=2 * feat.size * HID * REL, transcendentals=0, bytes_accessed=8 << 20
        ),
    )(feat, weight)


def weighted_sum(t, src_ref, cnt_ref, me, adj_ref, t_ref):
    weights, picked = [], []
    for k in range(adj_ref.shape[1]):
        v = src_ref[k, t]
        r = lax.shift_right_logical(v, 4)
        j = lax.bitwise_and(v, 15)
        q = lax.bitwise_xor(lax.shift_right_logical(j, 2), me)
        w = adj_ref[t, k]
        weights.append(jnp.where(k < cnt_ref[0, t], w, jnp.zeros_like(w)))
        picked.append(t_ref[q * PART + r * 4 + lax.bitwise_and(j, 3)])
    return jnp.dot(
        jnp.concatenate(weights, axis=1), jnp.concatenate(picked, axis=0), preferred_element_type=F32
    ).astype(BF16)


def aggregate_kernel(src_ref, cnt_ref, f_ref, w_ref, adj_ref, p0, p1, p2, a_ref, *refs):
    b_refs, both, t_ref, sems = refs[:-3], refs[-3], refs[-2], refs[-1]
    copies = [
        pltpu.make_async_copy(part, t_ref.at[pl.ds(PART * q, PART)], sems.at[q])
        for q, part in enumerate((p0, p1, p2))
    ]
    for copy in copies:
        copy.start()
    transform_rows(f_ref, w_ref, t_ref, PART * len(copies))
    for copy in copies:
        copy.wait()
    me = lax.axis_index("yh") * 2 + lax.axis_index("core")
    x0, y0 = lax.axis_index("x"), lax.axis_index("yl")

    def step(z, _):
        for odd in range(2):
            got = weighted_sum(z * 2 + odd, src_ref, cnt_ref, me, adj_ref, t_ref)
            a_ref[z, odd * BLK : (odd + 1) * BLK, :] = got[:, :HA]
            both[odd * BLK : (odd + 1) * BLK, :] = got[:, HA:]
        for (dx, dy), b_ref in zip(HOPS, b_refs):
            to = lax.bitwise_and(x0 + dx, NX - 1) * NY + lax.bitwise_xor(y0, dy)
            rows = both[pl.ds(pl.multiple_of(to * ROWS, ROWS), ROWS), :]
            b_ref[pl.ds(pl.multiple_of(z * ROWS, ROWS), ROWS), :] = rows
        return 0

    lax.fori_loop(0, NZ, step, 0)


def aggregate(src, cnt, feat, weight, adj, parts):
    outs = (jax.ShapeDtypeStruct((NZ, 256, HA), BF16),) + tuple(jax.ShapeDtypeStruct((256, HB), BF16) for _ in HOPS)
    return pl.pallas_call(
        aggregate_kernel,
        out_shape=outs,
        in_specs=[SMEM] * 2 + [VMEM] * 3 + [pl.BlockSpec(memory_space=pltpu.HBM)] * 3,
        out_specs=tuple(VMEM for _ in outs),
        scratch_shapes=[
            pltpu.VMEM((256, HB), BF16),
            pltpu.VMEM((4 * PART, BLK, HID), BF16),
            pltpu.SemaphoreType.DMA((3,)),
        ],
        compiler_params=pltpu.CompilerParams(vmem_limit_bytes=24 << 20),
        cost_estimate=pl.CostEstimate(flops=6 << 30, transcendentals=0, bytes_accessed=20 << 20),
    )(src, cnt, feat, weight, adj, *parts)


def exchange(x, axes):
    return lax.all_to_all(x, axes, 0, 0, tiled=True)


def hop(x, dx, dy):
    pairs = [(i * NY + j, (i + dx) % NX * NY + (j ^ dy)) for i in range(NX) for j in range(NY)]
    return lax.ppermute(x, ("x", "yl"), pairs)


def layer(src_feat, tgt_feat, rel_weight, self_weight, adj_weight, adj_source, adj_count):
    swap = [(0, 1), (1, 0)]
    far = lax.ppermute(src_feat, "yh", swap)
    near = lax.ppermute(src_feat, "core", swap)
    diag = lax.ppermute(far, "core", swap)
    parts = []
    for feat in (src_feat, near, far):
        parts.append(transform(feat, rel_weight))
    out_a, *out_b = aggregate(
        jnp.transpose(adj_source[0]), adj_count, diag, rel_weight, adj_weight[0], parts
    )
    got_a = exchange(out_a, "z")
    got_b = [out_b[0]] + [hop(b, dx, dy) for b, (dx, dy) in zip(out_b[1:], HOPS[1:])]
    sum_a = got_a.astype(F32).sum(0).astype(BF16).reshape(NX * NY, ROWS, HA)
    sum_b = sum(b.astype(F32) for b in got_b).astype(BF16).reshape(NZ, ROWS, HB)
    last_a = exchange(sum_a, ("x", "yl"))
    last_b = exchange(sum_b, "z")
    end_a = last_a.astype(F32).sum(0)
    end_b = last_b.astype(F32).sum(0)
    summed = jnp.concatenate([end_a, end_b], axis=1)
    self_term = jnp.dot(tgt_feat, self_weight, preferred_element_type=F32)
    return jax.nn.relu(summed + self_term).astype(BF16)


def solution(mesh):
    fine = Mesh(mesh.devices.reshape(NZ, NX, NY, 2, 2), ("z", "x", "yl", "yh", "core"))
    src, tgt = ("z", "x", "yl"), ("yh", "core")
    return jax.shard_map(
        layer,
        mesh=fine,
        in_specs=(
            P(src + tgt, None),
            P(tgt + src, None),
            P(),
            P(),
            P(src, tgt, None, None, None),
            P(src, tgt, None),
            P(src, tgt),
        ),
        out_specs=P(tgt + src, None),
        check_vma=False,
    )
```

time: 147 us -> 128 us (0.87)
  local copies, waits for them, and re-layouts: 16.7 us -> 4.97 us
  Pallas kernels: 27.9 us -> 20.2 us
    unnamed x31 -> x20, local copies, waits for them, and re-layouts: 16.6 us -> 4.97 us
    pallas_call x5 -> x4, Pallas kernels: 27.9 us -> 20.2 us  [the longest x3 10.4 us: transform(): pl.pallas_call(transform_kernel, out_shape=jax.ShapeDtypeStruct((PART, BL...]
    all_to_all x3, waiting for transfers between devices: 15.5 us -> 17.7 us  [exchange(): return lax.all_to_all(x, axes, 0, 0, tiled=True)]
    ppermute x7, waiting for transfers between devices: 29.8 us -> 27.7 us  [hop(): return lax.ppermute(x, ('x', 'yl'), pairs)]
  transfers between devices with their start and end apart: 13 -> 13, of which waited for: 9 -> 10; matrix products, arithmetic and copies ran while one was open for 3% -> 3% of each run, Pallas kernels for 13% -> 8%
where the time goes in v1:
time: 128 us
  waiting for transfers between devices  64.4 us (50%)
  starting transfers between devices  33.8 us (26%)
  Pallas kernels  20.2 us (16%)
  local copies, waits for them, and re-layouts  4.97 us (4%)
  other arithmetic  3.51 us (3%)
    ppermute x7, waiting for transfers between devices, hop(): return lax.ppermute(x, ('x', 'yl'), pairs)  27.7 us
    all_to_all x3, starting transfers between devices, exchange(): return lax.all_to_all(x, axes, 0, 0, tiled=True)  19.6 us
    ppermute x1, waiting for transfers between devices, layer(): far = lax.ppermute(src_feat, 'yh', swap)  18.9 us
    all_to_all x3, waiting for transfers between devices, exchange(): return lax.all_to_all(x, axes, 0, 0, tiled=True)  17.7 us
    ppermute x7, starting transfers between devices, hop(): return lax.ppermute(x, ('x', 'yl'), pairs)  12.2 us
    pallas_call x3, Pallas kernels, transform(): pl.pallas_call(transform_kernel, out_shape=jax.ShapeDtypeStruct((PART, BL...  10.4 us
    pallas_call x1, Pallas kernels, aggregate(): pl.pallas_call(aggregate_kernel, out_shape=outs, in_specs=[SMEM] * 2 + [V...  9.79 us
    unnamed x20, local copies, waits for them, and re-layouts  4.97 us
  transfers between devices with their start and end apart: 13, of which 10 were waited for; matrix products, arithmetic and copies ran while one was open for 3% of the time, Pallas kernels for 8%

profile of v1, /device:TPU:16, one launch (start us, length us, event | category | flops | bytes accessed | tf_op | source)
XLA Modules:
  0.0 128.0 jit_solution(8230983895839544044)
XLA Ops:
  0.0 2.0 %collective-permute-start = (bf16[512,768]{1,0:T(8,128)(2,1)}, bf16[512,768]{1,0:T(8,128)(2,1)S(1)}, u32[]{:S(2)}, u32[]{:S(2)}) collective-permute-start(bf16[512,768]{1,0:T(8,128)(2,1)} %f_ref.1), channel_id=1, source_target_pairs={{0,2},{2,0},{1,3},{3,1},{4,6},{6,4},{5,7},{7,5},{8,10},{10,8},{9,1... | collective-permute-start | bytes 2359304 | tf_op jit(solution)/shard_map/ppermute | solution.py:126
  2.0 18.9 %collective-permute-done.f_ref = bf16[512,768]{1,0:T(8,128)(2,1)S(1)} collective-permute-done((bf16[512,768]{1,0:T(8,128)(2,1)}, bf16[512,768]{1,0:T(8,128)(2,1)S(1)}, u32[]{:S(2)}, u32[]{:S(2)}) %collective-permute-start) | collective-permute-done | bytes 786464 | tf_op jit(solution)/shard_map/ppermute | solution.py:126
  21.0 2.3 %copy-done.1 = bf16[3,768,1024]{2,1,0:T(8,128)(2,1)S(1)} copy-done((bf16[3,768,1024]{2,1,0:T(8,128)(2,1)S(1)}, bf16[3,768,1024]{2,1,0:T(8,128)(2,1)}, u32[]{:S(2)}) %copy-start.1) | copy-done | bytes 4718616
  23.3 1.1 copy-done.4
  24.5 3.5 %shard_map.73.p0 = bf16[12,128,1024]{2,1,0:T(8,128)(2,1)S(1)} custom-call(bf16[512,768]{1,0:T(8,128)(2,1)S(1)} %copy-done.4, bf16[3,768,1024]{2,1,0:T(8,128)(2,1)S(1)} %copy-done.1), custom_call_target="tpu_custom_call" | custom-call | flops 2415919104 | bytes 8388608 | tf_op jit(solution)/shard_map/pallas_call | solution.py:43
  27.9 3.5 %shard_map.75.p2 = bf16[12,128,1024]{2,1,0:T(8,128)(2,1)S(1)} custom-call(bf16[512,768]{1,0:T(8,128)(2,1)S(1)} %collective-permute-done.f_ref, bf16[3,768,1024]{2,1,0:T(8,128)(2,1)S(1)} %copy-done.2), custom_call_target="tpu_custom_call" | custom-call | flops 2415919104 | bytes 8388608 | tf_op jit(solution)/shard_map/pallas_call | solution.py:43
  31.5 3.5 %shard_map.74.p1 = bf16[12,128,1024]{2,1,0:T(8,128)(2,1)S(1)} custom-call(bf16[512,768]{1,0:T(8,128)(2,1)S(1)} %collective-permute-done.2.f_ref, bf16[3,768,1024]{2,1,0:T(8,128)(2,1)S(1)} %copy-done.2), custom_call_target="tpu_custom_call" | custom-call | flops 2415919104 | bytes 8388608 | tf_op jit(solution)/shard_map/pallas_call | solution.py:43
  35.0 9.8 %shard_map.76 = (bf16[8,256,384]{2,1,0:T(8,128)(2,1)}, bf16[256,640]{1,0:T(8,128)(2,1)S(1)}, bf16[256,640]{1,0:T(8,128)(2,1)S(1)}, bf16[256,640]{1,0:T(8,128)(2,...) custom-call(s32[4,16]{1,0:T(4,128)S(1)} %bitcast.9, ...), custom_call_target="tpu_custom_call" | custom-call | flops 6442450944 | bytes 20971520 | tf_op jit(solution)/shard_map/pallas_call | solution.py:100
  44.8 0.7 copy-done.5
  45.5 0.7 copy-done.6
  46.3 8.5 %all-to-all-start = ((bf16[8,256,384]{2,1,0:T(8,128)(2,1)}), bf16[8,256,384]{2,1,0:T(8,128)(2,1)}, u32[]{:S(2)}, u32[]{:S(2)}) async-start(bf16[8,256,384]{2,1,0:T(8,128)(2,1)} %get-tuple-element.14), calls=%async_computation | async-start | bytes 3145728 | tf_op jit(solution)/shard_map/all_to_all | solution.py:116
  54.7 3.7 %collective-permute-start.3 = (bf16[256,640]{1,0:T(8,128)(2,1)}, bf16[256,640]{1,0:T(8,128)(2,1)S(1)}, u32[]{:S(2)}, u32[]{:S(2)}) collective-permute-start(bf16[256,640]{1,0:T(8,128)(2,1)} %copy-done.6), channel_id=1, source_target_pairs={{0,20},{4,16},{8,28},{12,24},{16,4},{20,0},{24,12},{28,8},{1,21},{... | collective-permute-start | bytes 983048 | tf_op jit(solution)/shard_map/ppermute | solution.py:121
  58.5 0.5 collective-permute-start.4
  59.0 1.7 %collective-permute-start.5 = (bf16[256,640]{1,0:T(8,128)(2,1)S(1)}, bf16[256,640]{1,0:T(8,128)(2,1)S(1)}, u32[]{:S(2)}, u32[]{:S(2)}) collective-permute-start(bf16[256,640]{1,0:T(8,128)(2,1)S(1)} %get-tuple-element.18), channel_id=1, source_target_pairs={{0,12},{4,8},{8,20},{12,16},{16,28},{20,24},{24,4},{28,0},{1,13},{... | collective-permute-start | bytes 983048 | tf_op jit(solution)/shard_map/ppermute | solution.py:121
  60.6 2.5 %collective-permute-start.6 = (bf16[256,640]{1,0:T(8,128)(2,1)S(1)}, bf16[256,640]{1,0:T(8,128)(2,1)S(1)}, u32[]{:S(2)}, u32[]{:S(2)}) collective-permute-start(bf16[256,640]{1,0:T(8,128)(2,1)S(1)} %get-tuple-element.19), channel_id=1, source_target_pairs={{0,28},{4,24},{8,4},{12,0},{16,12},{20,8},{24,20},{28,16},{1,29},{... | collective-permute-start | bytes 983048 | tf_op jit(solution)/shard_map/ppermute | solution.py:121
  63.1 0.3 collective-permute-start.7
  63.4 4.6 %collective-permute-done.3 = bf16[256,640]{1,0:T(8,128)(2,1)S(1)} collective-permute-done((bf16[256,640]{1,0:T(8,128)(2,1)}, bf16[256,640]{1,0:T(8,128)(2,1)S(1)}, u32[]{:S(2)}, u32[]{:S(2)}) %collective-permute-start.3) | collective-permute-done | bytes 327712 | tf_op jit(solution)/shard_map/ppermute | solution.py:121
  68.0 2.8 %collective-permute-start.8 = (bf16[256,640]{1,0:T(8,128)(2,1)S(1)}, bf16[256,640]{1,0:T(8,128)(2,1)S(1)}, u32[]{:S(2)}, u32[]{:S(2)}) collective-permute-start(bf16[256,640]{1,0:T(8,128)(2,1)S(1)} %get-tuple-element.21), channel_id=1, source_target_pairs={{0,24},{4,28},{8,0},{12,4},{16,8},{20,12},{24,16},{28,20},{1,25},{... | collective-permute-start | bytes 983048 | tf_op jit(solution)/shard_map/ppermute | solution.py:121
  70.8 4.0 %collective-permute-done.4 = bf16[256,640]{1,0:T(8,128)(2,1)S(1)} collective-permute-done((bf16[256,640]{1,0:T(8,128)(2,1)}, bf16[256,640]{1,0:T(8,128)(2,1)S(1)}, u32[]{:S(2)}, u32[]{:S(2)}) %collective-permute-start.4) | collective-permute-done | bytes 327712 | tf_op jit(solution)/shard_map/ppermute | solution.py:121
  74.8 0.7 collective-permute-start.9
  75.5 10.1 %collective-permute-done.5 = bf16[256,640]{1,0:T(8,128)(2,1)S(1)} collective-permute-done((bf16[256,640]{1,0:T(8,128)(2,1)S(1)}, bf16[256,640]{1,0:T(8,128)(2,1)S(1)}, u32[]{:S(2)}, u32[]{:S(2)}) %collective-permute-start.5) | collective-permute-done | bytes 327712 | tf_op jit(solution)/shard_map/ppermute | solution.py:121
  85.7 2.7 %collective-permute-done.6 = bf16[256,640]{1,0:T(8,128)(2,1)S(1)} collective-permute-done((bf16[256,640]{1,0:T(8,128)(2,1)S(1)}, bf16[256,640]{1,0:T(8,128)(2,1)S(1)}, u32[]{:S(2)}, u32[]{:S(2)}) %collective-permute-start.6) | collective-permute-done | bytes 327712 | tf_op jit(solution)/shard_map/ppermute | solution.py:121
  88.3 3.4 %collective-permute-done.7 = bf16[256,640]{1,0:T(8,128)(2,1)S(1)} collective-permute-done((bf16[256,640]{1,0:T(8,128)(2,1)S(1)}, bf16[256,640]{1,0:T(8,128)(2,1)S(1)}, u32[]{:S(2)}, u32[]{:S(2)}) %collective-permute-start.7) | collective-permute-done | bytes 327712 | tf_op jit(solution)/shard_map/ppermute | solution.py:121
  91.8 2.7 %collective-permute-done.8 = bf16[256,640]{1,0:T(8,128)(2,1)S(1)} collective-permute-done((bf16[256,640]{1,0:T(8,128)(2,1)S(1)}, bf16[256,640]{1,0:T(8,128)(2,1)S(1)}, u32[]{:S(2)}, u32[]{:S(2)}) %collective-permute-start.8) | collective-permute-done | bytes 327712 | tf_op jit(solution)/shard_map/ppermute | solution.py:121
  94.4 0.1 collective-permute-done.9
  94.6 1.1 add_convert_fusion
  95.6 6.6 %all-to-all-start.2 = ((bf16[8,32,640]{2,1,0:T(8,128)(2,1)}), bf16[8,32,640]{2,1,0:T(8,128)(2,1)S(1)}, u32[]{:S(2)}, u32[]{:S(2)}) async-start(bf16[8,32,640]{2,1,0:T(8,128)(2,1)} %bitcast.4), calls=%async_computation.2 | async-start | bytes 655360 | tf_op jit(solution)/shard_map/all_to_all | solution.py:116
  102.3 2.4 %reduce_sum.30 = bf16[256,384]{1,0:T(8,128)(2,1)} reduce(bf16[8,256,384]{2,1,0:T(8,128)(2,1)} %all-to-all-done, bf16[]{:T(256)} %constant.4.clone.1), dimensions={0}, to_apply=%region_0.0 | reduce | flops 688128 | bytes 1769474 | tf_op jit(solution)/shard_map/reduce_sum | solution.py:137
  104.7 11.1 %all-to-all-done.2 = bf16[8,32,640]{2,1,0:T(8,128)(2,1)S(1)} async-done(((bf16[8,32,640]{2,1,0:T(8,128)(2,1)}), bf16[8,32,640]{2,1,0:T(8,128)(2,1)S(1)}, u32[]{:S(2)}, u32[]{:S(2)}) %all-to-all-start.2) | async-done | bytes 327712 | tf_op jit(solution)/shard_map/all_to_all | solution.py:116
  115.8 4.5 %all-to-all-start.1 = ((bf16[8,32,384]{2,1,0:T(8,128)(2,1)}), bf16[8,32,384]{2,1,0:T(8,128)(2,1)S(1)}, u32[]{:S(2)}, u32[]{:S(2)}) async-start(bf16[8,32,384]{2,1,0:T(8,128)(2,1)} %bitcast.3), calls=%async_computation.1 | async-start | bytes 393216 | tf_op jit(solution)/shard_map/all_to_all | solution.py:116
  120.3 6.6 %all-to-all-done.1 = bf16[8,32,384]{2,1,0:T(8,128)(2,1)S(1)} async-done(((bf16[8,32,384]{2,1,0:T(8,128)(2,1)}), bf16[8,32,384]{2,1,0:T(8,128)(2,1)S(1)}, u32[]{:S(2)}, u32[]{:S(2)}) %all-to-all-start.1) | async-done | bytes 196640 | tf_op jit(solution)/shard_map/all_to_all | solution.py:116
  127.0 1.0 fusion.1
  (23 shorter events, 0.1 us)
Async XLA Ops:
  0.0 127.0 %copy-start = (bf16[768,1024]{1,0:T(8,128)(2,1)S(1)}, bf16[768,1024]{1,0:T(8,128)(2,1)}, u32[]{:S(2)}) copy-start(bf16[768,1024]{1,0:T(8,128)(2,1)} %param.10) | copy-start | bytes 4718596
  0.0 21.0 %collective-permute-start = (bf16[512,768]{1,0:T(8,128)(2,1)}, bf16[512,768]{1,0:T(8,128)(2,1)S(1)}, u32[]{:S(2)}, u32[]{:S(2)}) collective-permute-start(bf16[512,768]{1,0:T(8,128)(2,1)} %f_ref.1), channel_id=1, source_target_pairs={{0,2},{2,0},{1,3},{3,1},{4,6},{6,4},{5,7},{7,5},{8,10},{10,8},{9,1... | collective-permute-start | bytes 2359304 | tf_op jit(solution)/shard_map/ppermute | solution.py:126
  2.0 29.4 %collective-permute-start.2 = (bf16[512,768]{1,0:T(8,128)(2,1)}, bf16[512,768]{1,0:T(8,128)(2,1)S(1)}, u32[]{:S(2)}, u32[]{:S(2)}) collective-permute-start(bf16[512,768]{1,0:T(8,128)(2,1)} %f_ref.1), channel_id=1, source_target_pairs={{0,1},{1,0},{2,3},{3,2},{4,5},{5,4},{6,7},{7,6},{8,9},{9,8},{10,11... | collective-permute-start | bytes 2359304 | tf_op jit(solution)/shard_map/ppermute | solution.py:127
  21.0 13.9 %collective-permute-start.1 = (bf16[512,768]{1,0:T(8,128)(2,1)S(1)}, bf16[512,768]{1,0:T(8,128)(2,1)S(1)}, u32[]{:S(2)}, u32[]{:S(2)}) collective-permute-start(bf16[512,768]{1,0:T(8,128)(2,1)S(1)} %collective-permute-done.f_ref), channel_id=1, source_target_pairs={{0,1},{1,0},{2,3},{3,2},{4,5},{5,4},{6,7},{7,6},{8,9},{9,8},{10,11... | collective-permute-start | bytes 2359304 | tf_op jit(solution)/shard_map/ppermute | solution.py:128
  21.0 2.3 %copy-start.1 = (bf16[3,768,1024]{2,1,0:T(8,128)(2,1)S(1)}, bf16[3,768,1024]{2,1,0:T(8,128)(2,1)}, u32[]{:S(2)}) copy-start(bf16[3,768,1024]{2,1,0:T(8,128)(2,1)} %w_ref.7) | copy-start | bytes 14155780
  23.3 1.1 copy-start.4
  24.5 3.5 %copy-start.2 = (bf16[3,768,1024]{2,1,0:T(8,128)(2,1)S(1)}, bf16[3,768,1024]{2,1,0:T(8,128)(2,1)}, u32[]{:S(2)}) copy-start(bf16[3,768,1024]{2,1,0:T(8,128)(2,1)} %w_ref.7) | copy-start | bytes 14155780
  31.4 3.5 %copy-start.3 = (bf16[1,16,4,128,128]{4,3,2,1,0:T(8,128)(2,1)S(1)}, bf16[1,16,4,128,128]{4,3,2,1,0:T(8,128)(2,1)}, u32[]{:S(2)}) copy-start(bf16[1,16,4,128,128]{4,3,2,1,0:T(8,128)(2,1)} %param.11) | copy-start | bytes 6291460
  31.4 3.5 %copy-start.7 = (s32[1,16,4]{1,2,0:T(4,128)S(1)}, s32[1,16,4]{1,2,0:T(4,128)}, u32[]{:S(2)}) copy-start(s32[1,16,4]{1,2,0:T(4,128)} %param.12) | copy-start | bytes 772
  31.4 3.5 %copy-start.8 = (s32[1,16]{1,0:T(1,128)S(1)}, s32[1,16]{1,0:T(1,128)}, u32[]{:S(2)}) copy-start(s32[1,16]{1,0:T(1,128)} %cnt_ref.1) | copy-start | bytes 196
  44.8 0.7 copy-start.5
  45.5 0.7 copy-start.6
  46.3 49.4 %all-to-all-start = ((bf16[8,256,384]{2,1,0:T(8,128)(2,1)}), bf16[8,256,384]{2,1,0:T(8,128)(2,1)}, u32[]{:S(2)}, u32[]{:S(2)}) async-start(bf16[8,256,384]{2,1,0:T(8,128)(2,1)} %get-tuple-element.14), calls=%async_computation | async-start | bytes 3145728 | tf_op jit(solution)/shard_map/all_to_all | solution.py:116
  54.7 13.3 %collective-permute-start.3 = (bf16[256,640]{1,0:T(8,128)(2,1)}, bf16[256,640]{1,0:T(8,128)(2,1)S(1)}, u32[]{:S(2)}, u32[]{:S(2)}) collective-permute-start(bf16[256,640]{1,0:T(8,128)(2,1)} %copy-done.6), channel_id=1, source_target_pairs={{0,20},{4,16},{8,28},{12,24},{16,4},{20,0},{24,12},{28,8},{1,21},{... | collective-permute-start | bytes 983048 | tf_op jit(solution)/shard_map/ppermute | solution.py:121
  58.5 16.3 %collective-permute-start.4 = (bf16[256,640]{1,0:T(8,128)(2,1)}, bf16[256,640]{1,0:T(8,128)(2,1)S(1)}, u32[]{:S(2)}, u32[]{:S(2)}) collective-permute-start(bf16[256,640]{1,0:T(8,128)(2,1)} %copy-done.5), channel_id=1, source_target_pairs={{0,16},{4,20},{8,24},{12,28},{16,0},{20,4},{24,8},{28,12},{1,17},{... | collective-permute-start | bytes 983048 | tf_op jit(solution)/shard_map/ppermute | solution.py:121
  59.0 26.7 %collective-permute-start.5 = (bf16[256,640]{1,0:T(8,128)(2,1)S(1)}, bf16[256,640]{1,0:T(8,128)(2,1)S(1)}, u32[]{:S(2)}, u32[]{:S(2)}) collective-permute-start(bf16[256,640]{1,0:T(8,128)(2,1)S(1)} %get-tuple-element.18), channel_id=1, source_target_pairs={{0,12},{4,8},{8,20},{12,16},{16,28},{20,24},{24,4},{28,0},{1,13},{... | collective-permute-start | bytes 983048 | tf_op jit(solution)/shard_map/ppermute | solution.py:121
  60.6 27.7 %collective-permute-start.6 = (bf16[256,640]{1,0:T(8,128)(2,1)S(1)}, bf16[256,640]{1,0:T(8,128)(2,1)S(1)}, u32[]{:S(2)}, u32[]{:S(2)}) collective-permute-start(bf16[256,640]{1,0:T(8,128)(2,1)S(1)} %get-tuple-element.19), channel_id=1, source_target_pairs={{0,28},{4,24},{8,4},{12,0},{16,12},{20,8},{24,20},{28,16},{1,29},{... | collective-permute-start | bytes 983048 | tf_op jit(solution)/shard_map/ppermute | solution.py:121
  63.1 28.7 %collective-permute-start.7 = (bf16[256,640]{1,0:T(8,128)(2,1)S(1)}, bf16[256,640]{1,0:T(8,128)(2,1)S(1)}, u32[]{:S(2)}, u32[]{:S(2)}) collective-permute-start(bf16[256,640]{1,0:T(8,128)(2,1)S(1)} %get-tuple-element.20), channel_id=1, source_target_pairs={{0,8},{4,12},{8,16},{12,20},{16,24},{20,28},{24,0},{28,4},{1,9},{5... | collective-permute-start | bytes 983048 | tf_op jit(solution)/shard_map/ppermute | solution.py:121
  68.0 26.4 %collective-permute-start.8 = (bf16[256,640]{1,0:T(8,128)(2,1)S(1)}, bf16[256,640]{1,0:T(8,128)(2,1)S(1)}, u32[]{:S(2)}, u32[]{:S(2)}) collective-permute-start(bf16[256,640]{1,0:T(8,128)(2,1)S(1)} %get-tuple-element.21), channel_id=1, source_target_pairs={{0,24},{4,28},{8,0},{12,4},{16,8},{20,12},{24,16},{28,20},{1,25},{... | collective-permute-start | bytes 983048 | tf_op jit(solution)/shard_map/ppermute | solution.py:121
  74.8 19.8 %collective-permute-start.9 = (bf16[256,640]{1,0:T(8,128)(2,1)S(1)}, bf16[256,640]{1,0:T(8,128)(2,1)S(1)}, u32[]{:S(2)}, u32[]{:S(2)}) collective-permute-start(bf16[256,640]{1,0:T(8,128)(2,1)S(1)} %get-tuple-element.22), channel_id=1, source_target_pairs={{0,4},{4,0},{8,12},{12,8},{16,20},{20,16},{24,28},{28,24},{1,5},{5... | collective-permute-start | bytes 983048 | tf_op jit(solution)/shard_map/ppermute | solution.py:121
  95.6 20.1 %all-to-all-start.2 = ((bf16[8,32,640]{2,1,0:T(8,128)(2,1)}), bf16[8,32,640]{2,1,0:T(8,128)(2,1)S(1)}, u32[]{:S(2)}, u32[]{:S(2)}) async-start(bf16[8,32,640]{2,1,0:T(8,128)(2,1)} %bitcast.4), calls=%async_computation.2 | async-start | bytes 655360 | tf_op jit(solution)/shard_map/all_to_all | solution.py:116
  102.3 24.7 %copy-start.9 = (bf16[32,768]{1,0:T(8,128)(2,1)S(1)}, bf16[32,768]{1,0:T(8,128)(2,1)}, u32[]{:S(2)}) copy-start(bf16[32,768]{1,0:T(8,128)(2,1)} %param.8) | copy-start | bytes 147460
  115.8 11.2 %all-to-all-start.1 = ((bf16[8,32,384]{2,1,0:T(8,128)(2,1)}), bf16[8,32,384]{2,1,0:T(8,128)(2,1)S(1)}, u32[]{:S(2)}, u32[]{:S(2)}) async-start(bf16[8,32,384]{2,1,0:T(8,128)(2,1)} %bitcast.3), calls=%async_computation.1 | async-start | bytes 393216 | tf_op jit(solution)/shard_map/all_to_all | solution.py:116

commit v2 on v1

v2 whole, which is shorter than its diff:
```python
import jax
import jax.numpy as jnp
from jax import lax
from jax.experimental import pallas as pl
from jax.experimental.pallas import tpu as pltpu
from jax.sharding import Mesh, PartitionSpec as P


HID = 1024
BLK = 128
REL = 3
NZ, NX, NY = 8, 4, 2
ROWS = 32
HA = 256
HB = 512
HC = HID - HA - HB
PLACE = (0, 12, 24)
F32 = jnp.float32
BF16 = jnp.bfloat16
SMEM = pl.BlockSpec(memory_space=pltpu.SMEM)
VMEM = pl.BlockSpec(memory_space=pltpu.VMEM)


def transform_rows(f_ref, w_ref, t_ref, base):
    def step(i, _):
        h = i // REL
        r = i - h * REL
        y = jnp.dot(f_ref[pl.ds(h * 2 * BLK, 2 * BLK), :], w_ref[r], preferred_element_type=F32)
        t_ref[pl.ds(base + i * 2, 2)] = y.astype(BF16).reshape(2, BLK, HID)
        return 0

    lax.fori_loop(0, f_ref.shape[0] // (2 * BLK) * REL, step, 0)


def transform_kernel(f_ref, w_ref, t_ref):
    transform_rows(f_ref, w_ref, t_ref, 0)


def transform(feat, weight):
    return pl.pallas_call(
        transform_kernel,
        out_shape=jax.ShapeDtypeStruct((REL * feat.shape[0] // BLK, BLK, HID), BF16),
        in_specs=[VMEM, VMEM],
        out_specs=VMEM,
        compiler_params=pltpu.CompilerParams(vmem_limit_bytes=8 << 20),
        cost_estimate=pl.CostEstimate(
            flops=2 * feat.size * HID * REL, transcendentals=0, bytes_accessed=8 << 20
        ),
    )(feat, weight)


def weighted_sum(t, src_ref, cnt_ref, me, adj_ref, t_ref):
    weights, picked = [], []
    for k in range(adj_ref.shape[1]):
        v = src_ref[k, t]
        r = lax.shift_right_logical(v, 4)
        j = lax.bitwise_and(v, 15)
        half = lax.bitwise_xor(lax.shift_right_logical(j, 1), me * 2)
        w = adj_ref[t, k]
        weights.append(jnp.where(k < cnt_ref[0, t], w, jnp.zeros_like(w)))
        picked.append(t_ref[half * 6 + r * 2 + lax.bitwise_and(j, 1)])
    return jnp.dot(
        jnp.concatenate(weights, axis=1), jnp.concatenate(picked, axis=0), preferred_element_type=F32
    ).astype(BF16)


def aggregate_kernel(src_ref, cnt_ref, f_ref, w_ref, adj_ref, *refs):
    n = len(PLACE)
    parts, a_ref, b_refs, c_refs, (both, t_ref, sems) = refs[:n], refs[n], refs[n + 1 : -5], refs[-5:-3], refs[-3:]
    copies = []
    for q, part in enumerate(parts):
        copies.append(pltpu.make_async_copy(part, t_ref.at[pl.ds(PLACE[q], part.shape[0])], sems.at[q]))
    for copy in copies:
        copy.start()
    transform_rows(f_ref, w_ref, t_ref, 48 - f_ref.shape[0] // BLK * REL)
    for copy in copies:
        copy.wait()
    me = lax.axis_index("yh") * 2 + lax.axis_index("core")
    x0, y0 = lax.axis_index("x"), lax.axis_index("yl")
    b0, b1, b3, b20, b21 = b_refs

    def step(z, _):
        for odd in range(2):
            got = weighted_sum(z * 2 + odd, src_ref, cnt_ref, me, adj_ref, t_ref)
            a_ref[z, odd * BLK : (odd + 1) * BLK, :] = got[:, :HA]
            both[odd * BLK : (odd + 1) * BLK, :] = got[:, HA:]
        at = pl.ds(pl.multiple_of(z * ROWS, ROWS), ROWS)
        for dx in range(NX):
            for dy in range(NY):
                to = lax.bitwise_and(x0 + dx, NX - 1) * NY + lax.bitwise_xor(y0, dy)
                rows = both[pl.ds(pl.multiple_of(to * ROWS, ROWS), ROWS), :]
                if dx == 2:
                    (b20, b21)[dy][at, :] = rows[:, :HB]
                else:
                    (b0, b1, None, b3)[dx][dy, at, :] = rows[:, :HB]
                c_refs[dy][dx, at, :] = rows[:, HB:]
        return 0

    lax.fori_loop(0, NZ, step, 0)


def aggregate(src, cnt, feat, weight, adj, parts):
    shapes = [(NZ, 256, HA)] + [(NY, 256, HB)] * 3 + [(256, HB)] * 2 + [(NX, 256, HC)] * 2
    return pl.pallas_call(
        aggregate_kernel,
        out_shape=tuple(jax.ShapeDtypeStruct(shape, BF16) for shape in shapes),
        in_specs=[SMEM] * 2 + [VMEM] * 3 + [pl.BlockSpec(memory_space=pltpu.HBM)] * len(parts),
        out_specs=tuple(VMEM for _ in shapes),
        scratch_shapes=[
            pltpu.VMEM((256, HB + HC), BF16),
            pltpu.VMEM((48, BLK, HID), BF16),
            pltpu.SemaphoreType.DMA((len(parts),)),
        ],
        compiler_params=pltpu.CompilerParams(vmem_limit_bytes=24 << 20),
        cost_estimate=pl.CostEstimate(flops=6 << 30, transcendentals=0, bytes_accessed=20 << 20),
    )(src, cnt, feat, weight, adj, *parts)


def local(kernel, shapes, *args):
    return pl.pallas_call(
        kernel,
        out_shape=tuple(jax.ShapeDtypeStruct(shape, BF16) for shape in shapes),
        in_specs=[VMEM] * len(args),
        out_specs=tuple(VMEM for _ in shapes),
        compiler_params=pltpu.CompilerParams(vmem_limit_bytes=8 << 20),
    )(*args)


def add(*values):
    total = values[0].astype(F32)
    for value in values[1:]:
        total += value.astype(F32)
    return total.astype(BF16)


def b_relay(b1, b3, left, right, up, down):
    up[0] = add(b1[0], left[...])
    up[1] = b1[1]
    down[0] = b3[0]
    down[1] = add(b3[1], right[...])


def b_meet(b0, left, right, keep, send):
    keep[...] = add(b0[0], left[0], right[0])
    send[...] = add(b0[1], left[1], right[1])


def c_split(c0, other, own, up, low, high, down):
    half = low.shape[0]
    own[...] = add(c0[0], other[0])
    up[...] = add(c0[1], other[1])
    low[...] = add(c0[2, :half], other[2, :half])
    high[...] = add(c0[2, half:], other[2, half:])
    down[...] = add(c0[3], other[3])


def c_relay(up, down, left, right, up_out, down_out):
    half = left.shape[0]
    up_out[:half] = add(up[:half], left[...])
    up_out[half:] = up[half:]
    down_out[:half] = down[:half]
    down_out[half:] = add(down[half:], right[...])


def join(keep, other, own, left, right, out):
    for z in range(NZ):
        rows = slice(z * ROWS, (z + 1) * ROWS)
        out[z, :, :HB] = add(keep[rows], other[rows])
        out[z, :, HB:] = add(own[rows], left[rows], right[rows])


def exchange(x, axes):
    return lax.all_to_all(x, axes, 0, 0, tiled=True)


def along_x(x, d):
    return lax.ppermute(x, "x", [(i, (i + d) % NX) for i in range(NX)])


def layer(src_feat, tgt_feat, rel_weight, self_weight, adj_weight, adj_source, adj_count):
    swap = [(0, 1), (1, 0)]
    far = []
    for f in (src_feat,):
        far.append(lax.ppermute(f, "yh", swap))
    near = lax.ppermute(src_feat, "core", swap)
    t_own = transform(src_feat, rel_weight)
    t_near = transform(near, rel_weight)
    diag, t_far, t_diag = [], [], []
    for f in far:
        diag.append(lax.ppermute(f, "core", swap))
        t_far.append(transform(f, rel_weight))
    for f in diag[:-1]:
        t_diag.append(transform(f, rel_weight))
    out_a, b0, b1, b3, b20, b21, c0, c1 = aggregate(
        jnp.transpose(adj_source[0]),
        adj_count,
        diag[-1],
        rel_weight,
        adj_weight[0],
        [t_own, t_near] + t_far + t_diag,
    )
    b_left, b_right = along_x(b20, 1), along_x(b21, -1)
    c_other = lax.ppermute(c1, "yl", swap)
    got_a = exchange(out_a, "z")
    b_up, b_down = local(b_relay, [(NY, 256, HB)] * 2, b1, b3, b_left, b_right)
    b_left, b_right = along_x(b_up, 1), along_x(b_down, -1)
    shapes = [(256, HC), (256, HC), (BLK, HC), (BLK, HC), (256, HC)]
    c_own, c_up, c_low, c_high, c_down = local(c_split, shapes, c0, c_other)
    c_left, c_right = along_x(c_low, 1), along_x(c_high, -1)
    c_up, c_down = local(c_relay, [(256, HC)] * 2, c_up, c_down, c_left, c_right)
    c_left, c_right = along_x(c_up, 1), along_x(c_down, -1)
    b_keep, b_send = local(b_meet, [(256, HB)] * 2, b0, b_left, b_right)
    b_other = lax.ppermute(b_send, "yl", swap)
    sum_a = got_a.astype(F32).sum(0).astype(BF16).reshape(NX * NY, ROWS, HA)
    last_a = exchange(sum_a, ("x", "yl"))
    (joined,) = local(join, [(NZ, ROWS, HB + HC)], b_keep, b_other, c_own, c_left, c_right)
    last_b = exchange(joined, "z")
    end_a = last_a.astype(F32).sum(0)
    end_b = last_b.astype(F32).sum(0)
    summed = jnp.concatenate([end_a, end_b], axis=1)
    self_term = jnp.dot(tgt_feat, self_weight, preferred_element_type=F32)
    return jax.nn.relu(summed + self_term).astype(BF16)


def solution(mesh):
    fine = Mesh(mesh.devices.reshape(NZ, NX, NY, 2, 2), ("z", "x", "yl", "yh", "core"))
    src, tgt = ("z", "x", "yl"), ("yh", "core")
    return jax.shard_map(
        layer,
        mesh=fine,
        in_specs=(
            P(src + tgt, None),
            P(tgt + src, None),
            P(),
            P(),
            P(src, tgt, None, None, None),
            P(src, tgt, None),
            P(src, tgt),
        ),
        out_specs=P(tgt + src, None),
        check_vma=False,
    )
```

time: 128 us -> 127 us (level)
  waiting for transfers between devices: 64.4 us -> 57.2 us
  starting transfers between devices: 33.8 us -> 38.7 us
  other arithmetic: 3.51 us -> 2.12 us
  Pallas kernels: 20.2 us -> 21.5 us
    ppermute x9 -> x12, waiting for transfers between devices: 46.6 us -> 41 us  [the longest x8 21.7 us: along_x(): return lax.ppermute(x, 'x', [(i, (i + d) % NX) for i in range(NX)])]
    ppermute x9 -> x12, starting transfers between devices: 14.2 us -> 18 us  [the longest x8 13.3 us: along_x(): return lax.ppermute(x, 'x', [(i, (i + d) % NX) for i in range(NX)])]
    all_to_all x3, waiting for transfers between devices: 17.7 us -> 16.2 us  [exchange(): return lax.all_to_all(x, axes, 0, 0, tiled=True)]
    pallas_call x4 -> x9, Pallas kernels: 20.2 us -> 21.5 us  [the longest x3 10.5 us: transform(): pl.pallas_call(transform_kernel, out_shape=jax.ShapeDtypeStruct((REL * fe...]
    unnamed x20 -> x24, local copies, waits for them, and re-layouts: 4.97 us -> 5.81 us
  transfers between devices with their start and end apart: 13 -> 16, of which waited for: 10 -> 8; matrix products, arithmetic and copies ran while one was open for 3% -> 2% of each run, Pallas kernels for 8% -> 9%
where the time goes in v2:
time: 127 us; the launch traced here: 126 us
  waiting for transfers between devices  57.2 us (45%)
  starting transfers between devices  38.7 us (30%)
  Pallas kernels  21.5 us (17%)
  local copies, waits for them, and re-layouts  5.81 us (5%)
  other arithmetic  2.12 us (2%)
    ppermute x8, waiting for transfers between devices, along_x(): return lax.ppermute(x, 'x', [(i, (i + d) % NX) for i in range(NX)])  21.7 us
    all_to_all x3, starting transfers between devices, exchange(): return lax.all_to_all(x, axes, 0, 0, tiled=True)  20.7 us
    ppermute x1, waiting for transfers between devices, layer(): far.append(lax.ppermute(f, 'yh', swap))  18.9 us
    all_to_all x3, waiting for transfers between devices, exchange(): return lax.all_to_all(x, axes, 0, 0, tiled=True)  16.2 us
    ppermute x8, starting transfers between devices, along_x(): return lax.ppermute(x, 'x', [(i, (i + d) % NX) for i in range(NX)])  13.3 us
    pallas_call x3, Pallas kernels, transform(): pl.pallas_call(transform_kernel, out_shape=jax.ShapeDtypeStruct((REL * fe...  10.5 us
    pallas_call x1, Pallas kernels, aggregate(): pl.pallas_call(aggregate_kernel, out_shape=tuple((jax.ShapeDtypeStruct(sh...  9.67 us
    unnamed x24, local copies, waits for them, and re-layouts  5.81 us
  transfers between devices with their start and end apart: 16, of which 8 were waited for; matrix products, arithmetic and copies ran while one was open for 2% of the time, Pallas kernels for 9%

profile of v2, /device:TPU:16, one launch (start us, length us, event | category | flops | bytes accessed | tf_op | source)
XLA Modules:
  0.0 126.5 jit_solution(8229527332427830903)
XLA Ops:
  0.0 2.0 %collective-permute-start = (bf16[512,768]{1,0:T(8,128)(2,1)}, bf16[512,768]{1,0:T(8,128)(2,1)S(1)}, u32[]{:S(2)}, u32[]{:S(2)}) collective-permute-start(bf16[512,768]{1,0:T(8,128)(2,1)} %f_ref.1), channel_id=1, source_target_pairs={{0,2},{2,0},{1,3},{3,1},{4,6},{6,4},{5,7},{7,5},{8,10},{10,8},{9,1... | collective-permute-start | bytes 2359304 | tf_op jit(solution)/shard_map/ppermute | solution.py:184
  2.0 18.9 %collective-permute-done.f_ref = bf16[512,768]{1,0:T(8,128)(2,1)S(1)} collective-permute-done((bf16[512,768]{1,0:T(8,128)(2,1)}, bf16[512,768]{1,0:T(8,128)(2,1)S(1)}, u32[]{:S(2)}, u32[]{:S(2)}) %collective-permute-start) | collective-permute-done | bytes 786464 | tf_op jit(solution)/shard_map/ppermute | solution.py:184
  21.0 2.3 %copy-done.3 = bf16[3,768,1024]{2,1,0:T(8,128)(2,1)S(1)} copy-done((bf16[3,768,1024]{2,1,0:T(8,128)(2,1)S(1)}, bf16[3,768,1024]{2,1,0:T(8,128)(2,1)}, u32[]{:S(2)}) %copy-start.3) | copy-done | bytes 4718616
  23.3 1.1 copy-done.6
  24.5 3.5 %shard_map.73.refs_0_ = bf16[12,128,1024]{2,1,0:T(8,128)(2,1)S(1)} custom-call(bf16[512,768]{1,0:T(8,128)(2,1)S(1)} %copy-done.6, bf16[3,768,1024]{2,1,0:T(8,128)(2,1)S(1)} %copy-done.3), custom_call_target="tpu_custom_call" | custom-call | flops 2415919104 | bytes 8388608 | tf_op jit(solution)/shard_map/pallas_call | solution.py:40
  28.0 3.5 %shard_map.75.refs_2_ = bf16[12,128,1024]{2,1,0:T(8,128)(2,1)S(1)} custom-call(bf16[512,768]{1,0:T(8,128)(2,1)S(1)} %collective-permute-done.f_ref, bf16[3,768,1024]{2,1,0:T(8,128)(2,1)S(1)} %copy-done.4), custom_call_target="tpu_custom_call" | custom-call | flops 2415919104 | bytes 8388608 | tf_op jit(solution)/shard_map/pallas_call | solution.py:40
  31.5 3.5 %shard_map.74.refs_1_ = bf16[12,128,1024]{2,1,0:T(8,128)(2,1)S(1)} custom-call(bf16[512,768]{1,0:T(8,128)(2,1)S(1)} %collective-permute-done.2.f_ref, bf16[3,768,1024]{2,1,0:T(8,128)(2,1)S(1)} %copy-done.4), custom_call_target="tpu_custom_call" | custom-call | flops 2415919104 | bytes 8388608 | tf_op jit(solution)/shard_map/pallas_call | solution.py:40
  35.1 9.7 %shard_map.76 = (bf16[8,256,256]{2,1,0:T(8,128)(2,1)}, bf16[2,256,512]{2,1,0:T(8,128)(2,1)S(1)}, bf16[2,256,512]{2,1,0:T(8,128)(2,1)S(1)}, bf16[2,256,512]{2,1,0...) custom-call(s32[4,16]{1,0:T(4,128)S(1)} %bitcast.8, ...), custom_call_target="tpu_custom_call" | custom-call | flops 6442450944 | bytes 20971520 | tf_op jit(solution)/shard_map/pallas_call | solution.py:104
  44.7 0.8 copy-done.1
  45.5 0.8 copy-done.7
  46.3 0.7 copy-done.8
  47.0 8.5 %all-to-all-start = ((bf16[8,256,256]{2,1,0:T(8,128)(2,1)}), bf16[8,256,256]{2,1,0:T(8,128)(2,1)}, u32[]{:S(2)}, u32[]{:S(2)}) async-start(bf16[8,256,256]{2,1,0:T(8,128)(2,1)} %get-tuple-element.24), calls=%async_computation | async-start | bytes 2097152 | tf_op jit(solution)/shard_map/all_to_all | solution.py:173
  55.5 1.6 %collective-permute-start.3 = (bf16[256,512]{1,0:T(8,128)(2,1)}, bf16[256,512]{1,0:T(8,128)(2,1)S(1)}, u32[]{:S(2)}, u32[]{:S(2)}) collective-permute-start(bf16[256,512]{1,0:T(8,128)(2,1)} %copy-done.8), channel_id=1, source_target_pairs={{0,8},{8,16},{16,24},{24,0},{1,9},{9,17},{17,25},{25,1},{2,10},{10... | collective-permute-start | bytes 786440 | tf_op jit(solution)/shard_map/ppermute | solution.py:177
  57.1 1.7 %collective-permute-start.4 = (bf16[256,512]{1,0:T(8,128)(2,1)S(1)}, bf16[256,512]{1,0:T(8,128)(2,1)S(1)}, u32[]{:S(2)}, u32[]{:S(2)}) collective-permute-start(bf16[256,512]{1,0:T(8,128)(2,1)S(1)} %get-tuple-element.29), channel_id=1, source_target_pairs={{0,24},{8,0},{16,8},{24,16},{1,25},{9,1},{17,9},{25,17},{2,26},{10... | collective-permute-start | bytes 786440 | tf_op jit(solution)/shard_map/ppermute | solution.py:177
  58.8 6.6 %collective-permute-done.3.left = bf16[256,512]{1,0:T(8,128)(2,1)S(1)} collective-permute-done((bf16[256,512]{1,0:T(8,128)(2,1)}, bf16[256,512]{1,0:T(8,128)(2,1)S(1)}, u32[]{:S(2)}, u32[]{:S(2)}) %collective-permute-start.3) | collective-permute-done | bytes 262176 | tf_op jit(solution)/shard_map/ppermute | solution.py:177
  65.6 1.4 %collective-permute-start.5 = (bf16[2,256,512]{2,1,0:T(8,128)(2,1)S(1)}, bf16[2,256,512]{2,1,0:T(8,128)(2,1)S(1)}, u32[]{:S(2)}, u32[]{:S(2)}) collective-permute-start(bf16[2,256,512]{2,1,0:T(8,128)(2,1)S(1)} %get-tuple-element.30), channel_id=1, source_target_pairs={{0,8},{8,16},{16,24},{24,0},{1,9},{9,17},{17,25},{25,1},{2,10},{10... | collective-permute-start | bytes 1572872 | tf_op jit(solution)/shard_map/ppermute | solution.py:177
  66.9 2.0 %collective-permute-start.6 = (bf16[2,256,512]{2,1,0:T(8,128)(2,1)S(1)}, bf16[2,256,512]{2,1,0:T(8,128)(2,1)S(1)}, u32[]{:S(2)}, u32[]{:S(2)}) collective-permute-start(bf16[2,256,512]{2,1,0:T(8,128)(2,1)S(1)} %get-tuple-element.31), channel_id=1, source_target_pairs={{0,24},{8,0},{16,8},{24,16},{1,25},{9,1},{17,9},{25,17},{2,26},{10... | collective-permute-start | bytes 1572872 | tf_op jit(solution)/shard_map/ppermute | solution.py:177
  68.9 1.3 %collective-permute-start.8 = (bf16[4,256,256]{2,1,0:T(8,128)(2,1)}, bf16[4,256,256]{2,1,0:T(8,128)(2,1)S(1)}, u32[]{:S(2)}, u32[]{:S(2)}) collective-permute-start(bf16[4,256,256]{2,1,0:T(8,128)(2,1)} %copy-done.7), channel_id=1, source_target_pairs={{0,4},{4,0},{1,5},{5,1},{2,6},{6,2},{3,7},{7,3},{8,12},{12,8},{9,1... | collective-permute-start | bytes 1572872 | tf_op jit(solution)/shard_map/ppermute | solution.py:203
  70.2 10.0 %collective-permute-done.5.left = bf16[2,256,512]{2,1,0:T(8,128)(2,1)S(1)} collective-permute-done((bf16[2,256,512]{2,1,0:T(8,128)(2,1)S(1)}, bf16[2,256,512]{2,1,0:T(8,128)(2,1)S(1)}, u32[]{:S(2)}, u32[]{:S(2)}) %collective-permute-start.5) | collective-permute-done | bytes 524320 | tf_op jit(solution)/shard_map/ppermute | solution.py:177
  80.4 1.4 %collective-permute-start.7 = (bf16[256,512]{1,0:T(8,128)(2,1)S(1)}, bf16[256,512]{1,0:T(8,128)(2,1)S(1)}, u32[]{:S(2)}, u32[]{:S(2)}) collective-permute-start(bf16[256,512]{1,0:T(8,128)(2,1)S(1)} %get-tuple-element.33), channel_id=1, source_target_pairs={{0,4},{4,0},{1,5},{5,1},{2,6},{6,2},{3,7},{7,3},{8,12},{12,8},{9,1... | collective-permute-start | bytes 786440 | tf_op jit(solution)/shard_map/ppermute | solution.py:213
  82.7 2.8 %collective-permute-start.10 = (bf16[128,256]{1,0:T(8,128)(2,1)S(1)}, bf16[128,256]{1,0:T(8,128)(2,1)S(1)}, u32[]{:S(2)}, u32[]{:S(2)}) collective-permute-start(bf16[128,256]{1,0:T(8,128)(2,1)S(1)} %get-tuple-element.40), channel_id=1, source_target_pairs={{0,24},{8,0},{16,8},{24,16},{1,25},{9,1},{17,9},{25,17},{2,26},{10... | collective-permute-start | bytes 196616 | tf_op jit(solution)/shard_map/ppermute | solution.py:177
  85.5 2.2 %collective-permute-done.9.left = bf16[128,256]{1,0:T(8,128)(2,1)S(1)} collective-permute-done((bf16[128,256]{1,0:T(8,128)(2,1)S(1)}, bf16[128,256]{1,0:T(8,128)(2,1)S(1)}, u32[]{:S(2)}, u32[]{:S(2)}) %collective-permute-start.9) | collective-permute-done | bytes 65568 | tf_op jit(solution)/shard_map/ppermute | solution.py:177
  87.8 1.0 collective-permute-start.11
  88.7 2.4 %collective-permute-start.12 = (bf16[256,256]{1,0:T(8,128)(2,1)S(1)}, bf16[256,256]{1,0:T(8,128)(2,1)S(1)}, u32[]{:S(2)}, u32[]{:S(2)}) collective-permute-start(bf16[256,256]{1,0:T(8,128)(2,1)S(1)} %get-tuple-element.42), channel_id=1, source_target_pairs={{0,24},{8,0},{16,8},{24,16},{1,25},{9,1},{17,9},{25,17},{2,26},{10... | collective-permute-start | bytes 393224 | tf_op jit(solution)/shard_map/ppermute | solution.py:177
  91.2 2.9 %collective-permute-done.11.left = bf16[256,256]{1,0:T(8,128)(2,1)S(1)} collective-permute-done((bf16[256,256]{1,0:T(8,128)(2,1)S(1)}, bf16[256,256]{1,0:T(8,128)(2,1)S(1)}, u32[]{:S(2)}, u32[]{:S(2)}) %collective-permute-start.11) | collective-permute-done | bytes 131104 | tf_op jit(solution)/shard_map/ppermute | solution.py:177
  94.0 0.9 shard_map.81
  94.9 6.7 %all-to-all-start.2 = ((bf16[8,32,768]{2,1,0:T(8,128)(2,1)}), bf16[8,32,768]{2,1,0:T(8,128)(2,1)S(1)}, u32[]{:S(2)}, u32[]{:S(2)}) async-start(bf16[8,32,768]{2,1,0:T(8,128)(2,1)} %shard_map.81), calls=%async_computation.2 | async-start | bytes 786432 | tf_op jit(solution)/shard_map/all_to_all | solution.py:173
  101.6 2.0 %reduce_sum.30 = bf16[256,256]{1,0:T(8,128)(2,1)} reduce(bf16[8,256,256]{2,1,0:T(8,128)(2,1)} %all-to-all-done, bf16[]{:T(256)} %constant.4.clone.1), dimensions={0}, to_apply=%region_0.0 | reduce | flops 458752 | bytes 1179650 | tf_op jit(solution)/shard_map/reduce_sum | solution.py:214
  103.7 9.8 %all-to-all-done.2 = bf16[8,32,768]{2,1,0:T(8,128)(2,1)S(1)} async-done(((bf16[8,32,768]{2,1,0:T(8,128)(2,1)}), bf16[8,32,768]{2,1,0:T(8,128)(2,1)S(1)}, u32[]{:S(2)}, u32[]{:S(2)}) %all-to-all-start.2) | async-done | bytes 393248 | tf_op jit(solution)/shard_map/all_to_all | solution.py:173
  113.5 5.5 %all-to-all-start.1 = ((bf16[8,32,256]{2,1,0:T(8,128)(2,1)}), bf16[8,32,256]{2,1,0:T(8,128)(2,1)S(1)}, u32[]{:S(2)}, u32[]{:S(2)}) async-start(bf16[8,32,256]{2,1,0:T(8,128)(2,1)} %bitcast.3), calls=%async_computation.1 | async-start | bytes 262144 | tf_op jit(solution)/shard_map/all_to_all | solution.py:173
  119.0 6.4 %all-to-all-done.1 = bf16[8,32,256]{2,1,0:T(8,128)(2,1)S(1)} async-done(((bf16[8,32,256]{2,1,0:T(8,128)(2,1)}), bf16[8,32,256]{2,1,0:T(8,128)(2,1)S(1)}, u32[]{:S(2)}, u32[]{:S(2)}) %all-to-all-start.1) | async-done | bytes 131104 | tf_op jit(solution)/shard_map/all_to_all | solution.py:173
  125.4 1.0 fusion.1
  (37 shorter events, 1.4 us)
Async XLA Ops:
  0.0 125.4 %copy-start = (bf16[768,1024]{1,0:T(8,128)(2,1)S(1)}, bf16[768,1024]{1,0:T(8,128)(2,1)}, u32[]{:S(2)}) copy-start(bf16[768,1024]{1,0:T(8,128)(2,1)} %param.10) | copy-start | bytes 4718596
  0.0 21.0 %collective-permute-start = (bf16[512,768]{1,0:T(8,128)(2,1)}, bf16[512,768]{1,0:T(8,128)(2,1)S(1)}, u32[]{:S(2)}, u32[]{:S(2)}) collective-permute-start(bf16[512,768]{1,0:T(8,128)(2,1)} %f_ref.1), channel_id=1, source_target_pairs={{0,2},{2,0},{1,3},{3,1},{4,6},{6,4},{5,7},{7,5},{8,10},{10,8},{9,1... | collective-permute-start | bytes 2359304 | tf_op jit(solution)/shard_map/ppermute | solution.py:184
  2.0 29.5 %collective-permute-start.2 = (bf16[512,768]{1,0:T(8,128)(2,1)}, bf16[512,768]{1,0:T(8,128)(2,1)S(1)}, u32[]{:S(2)}, u32[]{:S(2)}) collective-permute-start(bf16[512,768]{1,0:T(8,128)(2,1)} %f_ref.1), channel_id=1, source_target_pairs={{0,1},{1,0},{2,3},{3,2},{4,5},{5,4},{6,7},{7,6},{8,9},{9,8},{10,11... | collective-permute-start | bytes 2359304 | tf_op jit(solution)/shard_map/ppermute | solution.py:185
  21.0 14.0 %collective-permute-start.1 = (bf16[512,768]{1,0:T(8,128)(2,1)S(1)}, bf16[512,768]{1,0:T(8,128)(2,1)S(1)}, u32[]{:S(2)}, u32[]{:S(2)}) collective-permute-start(bf16[512,768]{1,0:T(8,128)(2,1)S(1)} %collective-permute-done.f_ref), channel_id=1, source_target_pairs={{0,1},{1,0},{2,3},{3,2},{4,5},{5,4},{6,7},{7,6},{8,9},{9,8},{10,11... | collective-permute-start | bytes 2359304 | tf_op jit(solution)/shard_map/ppermute | solution.py:190
  21.0 2.3 %copy-start.3 = (bf16[3,768,1024]{2,1,0:T(8,128)(2,1)S(1)}, bf16[3,768,1024]{2,1,0:T(8,128)(2,1)}, u32[]{:S(2)}) copy-start(bf16[3,768,1024]{2,1,0:T(8,128)(2,1)} %w_ref.7) | copy-start | bytes 14155780
  23.3 1.1 copy-start.6
  24.5 3.5 %copy-start.4 = (bf16[3,768,1024]{2,1,0:T(8,128)(2,1)S(1)}, bf16[3,768,1024]{2,1,0:T(8,128)(2,1)}, u32[]{:S(2)}) copy-start(bf16[3,768,1024]{2,1,0:T(8,128)(2,1)} %w_ref.7) | copy-start | bytes 14155780
  31.5 3.6 %copy-start.5 = (bf16[1,16,4,128,128]{4,3,2,1,0:T(8,128)(2,1)S(1)}, bf16[1,16,4,128,128]{4,3,2,1,0:T(8,128)(2,1)}, u32[]{:S(2)}) copy-start(bf16[1,16,4,128,128]{4,3,2,1,0:T(8,128)(2,1)} %param.11) | copy-start | bytes 6291460
  31.5 3.6 %copy-start.9 = (s32[1,16,4]{1,2,0:T(4,128)S(1)}, s32[1,16,4]{1,2,0:T(4,128)}, u32[]{:S(2)}) copy-start(s32[1,16,4]{1,2,0:T(4,128)} %param.12) | copy-start | bytes 772
  31.5 3.6 %copy-start.10 = (s32[1,16]{1,0:T(1,128)S(1)}, s32[1,16]{1,0:T(1,128)}, u32[]{:S(2)}) copy-start(s32[1,16]{1,0:T(1,128)} %cnt_ref.1) | copy-start | bytes 196
  44.7 0.8 copy-start.1
  45.5 0.8 copy-start.7
  46.3 0.7 copy-start.8
  47.0 47.8 %all-to-all-start = ((bf16[8,256,256]{2,1,0:T(8,128)(2,1)}), bf16[8,256,256]{2,1,0:T(8,128)(2,1)}, u32[]{:S(2)}, u32[]{:S(2)}) async-start(bf16[8,256,256]{2,1,0:T(8,128)(2,1)} %get-tuple-element.24), calls=%async_computation | async-start | bytes 2097152 | tf_op jit(solution)/shard_map/all_to_all | solution.py:173
  55.5 26.5 %copy-start.2 = (bf16[4,256,256]{2,1,0:T(8,128)(2,1)S(1)}, bf16[4,256,256]{2,1,0:T(8,128)(2,1)}, u32[]{:S(2)}) copy-start(bf16[4,256,256]{2,1,0:T(8,128)(2,1)} %copy-done.1) | copy-start | bytes 1572868
  55.5 9.9 %collective-permute-start.3 = (bf16[256,512]{1,0:T(8,128)(2,1)}, bf16[256,512]{1,0:T(8,128)(2,1)S(1)}, u32[]{:S(2)}, u32[]{:S(2)}) collective-permute-start(bf16[256,512]{1,0:T(8,128)(2,1)} %copy-done.8), channel_id=1, source_target_pairs={{0,8},{8,16},{16,24},{24,0},{1,9},{9,17},{17,25},{25,1},{2,10},{10... | collective-permute-start | bytes 786440 | tf_op jit(solution)/shard_map/ppermute | solution.py:177
  57.1 8.4 %collective-permute-start.4 = (bf16[256,512]{1,0:T(8,128)(2,1)S(1)}, bf16[256,512]{1,0:T(8,128)(2,1)S(1)}, u32[]{:S(2)}, u32[]{:S(2)}) collective-permute-start(bf16[256,512]{1,0:T(8,128)(2,1)S(1)} %get-tuple-element.29), channel_id=1, source_target_pairs={{0,24},{8,0},{16,8},{24,16},{1,25},{9,1},{17,9},{25,17},{2,26},{10... | collective-permute-start | bytes 786440 | tf_op jit(solution)/shard_map/ppermute | solution.py:177
  65.6 14.6 %collective-permute-start.5 = (bf16[2,256,512]{2,1,0:T(8,128)(2,1)S(1)}, bf16[2,256,512]{2,1,0:T(8,128)(2,1)S(1)}, u32[]{:S(2)}, u32[]{:S(2)}) collective-permute-start(bf16[2,256,512]{2,1,0:T(8,128)(2,1)S(1)} %get-tuple-element.30), channel_id=1, source_target_pairs={{0,8},{8,16},{16,24},{24,0},{1,9},{9,17},{17,25},{25,1},{2,10},{10... | collective-permute-start | bytes 1572872 | tf_op jit(solution)/shard_map/ppermute | solution.py:177
  66.9 13.2 %collective-permute-start.6 = (bf16[2,256,512]{2,1,0:T(8,128)(2,1)S(1)}, bf16[2,256,512]{2,1,0:T(8,128)(2,1)S(1)}, u32[]{:S(2)}, u32[]{:S(2)}) collective-permute-start(bf16[2,256,512]{2,1,0:T(8,128)(2,1)S(1)} %get-tuple-element.31), channel_id=1, source_target_pairs={{0,24},{8,0},{16,8},{24,16},{1,25},{9,1},{17,9},{25,17},{2,26},{10... | collective-permute-start | bytes 1572872 | tf_op jit(solution)/shard_map/ppermute | solution.py:177
  68.9 13.1 %collective-permute-start.8 = (bf16[4,256,256]{2,1,0:T(8,128)(2,1)}, bf16[4,256,256]{2,1,0:T(8,128)(2,1)S(1)}, u32[]{:S(2)}, u32[]{:S(2)}) collective-permute-start(bf16[4,256,256]{2,1,0:T(8,128)(2,1)} %copy-done.7), channel_id=1, source_target_pairs={{0,4},{4,0},{1,5},{5,1},{2,6},{6,2},{3,7},{7,3},{8,12},{12,8},{9,1... | collective-permute-start | bytes 1572872 | tf_op jit(solution)/shard_map/ppermute | solution.py:203
  80.4 13.6 %collective-permute-start.7 = (bf16[256,512]{1,0:T(8,128)(2,1)S(1)}, bf16[256,512]{1,0:T(8,128)(2,1)S(1)}, u32[]{:S(2)}, u32[]{:S(2)}) collective-permute-start(bf16[256,512]{1,0:T(8,128)(2,1)S(1)} %get-tuple-element.33), channel_id=1, source_target_pairs={{0,4},{4,0},{1,5},{5,1},{2,6},{6,2},{3,7},{7,3},{8,12},{12,8},{9,1... | collective-permute-start | bytes 786440 | tf_op jit(solution)/shard_map/ppermute | solution.py:213
  82.2 5.6 %collective-permute-start.9 = (bf16[128,256]{1,0:T(8,128)(2,1)S(1)}, bf16[128,256]{1,0:T(8,128)(2,1)S(1)}, u32[]{:S(2)}, u32[]{:S(2)}) collective-permute-start(bf16[128,256]{1,0:T(8,128)(2,1)S(1)} %get-tuple-element.39), channel_id=1, source_target_pairs={{0,8},{8,16},{16,24},{24,0},{1,9},{9,17},{17,25},{25,1},{2,10},{10... | collective-permute-start | bytes 196616 | tf_op jit(solution)/shard_map/ppermute | solution.py:177
  82.7 5.1 %collective-permute-start.10 = (bf16[128,256]{1,0:T(8,128)(2,1)S(1)}, bf16[128,256]{1,0:T(8,128)(2,1)S(1)}, u32[]{:S(2)}, u32[]{:S(2)}) collective-permute-start(bf16[128,256]{1,0:T(8,128)(2,1)S(1)} %get-tuple-element.40), channel_id=1, source_target_pairs={{0,24},{8,0},{16,8},{24,16},{1,25},{9,1},{17,9},{25,17},{2,26},{10... | collective-permute-start | bytes 196616 | tf_op jit(solution)/shard_map/ppermute | solution.py:177
  87.8 6.3 %collective-permute-start.11 = (bf16[256,256]{1,0:T(8,128)(2,1)S(1)}, bf16[256,256]{1,0:T(8,128)(2,1)S(1)}, u32[]{:S(2)}, u32[]{:S(2)}) collective-permute-start(bf16[256,256]{1,0:T(8,128)(2,1)S(1)} %get-tuple-element.41), channel_id=1, source_target_pairs={{0,8},{8,16},{16,24},{24,0},{1,9},{9,17},{17,25},{25,1},{2,10},{10... | collective-permute-start | bytes 393224 | tf_op jit(solution)/shard_map/ppermute | solution.py:177
  88.7 5.3 %collective-permute-start.12 = (bf16[256,256]{1,0:T(8,128)(2,1)S(1)}, bf16[256,256]{1,0:T(8,128)(2,1)S(1)}, u32[]{:S(2)}, u32[]{:S(2)}) collective-permute-start(bf16[256,256]{1,0:T(8,128)(2,1)S(1)} %get-tuple-element.42), channel_id=1, source_target_pairs={{0,24},{8,0},{16,8},{24,16},{1,25},{9,1},{17,9},{25,17},{2,26},{10... | collective-permute-start | bytes 393224 | tf_op jit(solution)/shard_map/ppermute | solution.py:177
  94.0 31.4 %copy-start.11 = (bf16[32,768]{1,0:T(8,128)(2,1)S(1)}, bf16[32,768]{1,0:T(8,128)(2,1)}, u32[]{:S(2)}) copy-start(bf16[32,768]{1,0:T(8,128)(2,1)} %param.8) | copy-start | bytes 147460
  94.9 18.6 %all-to-all-start.2 = ((bf16[8,32,768]{2,1,0:T(8,128)(2,1)}), bf16[8,32,768]{2,1,0:T(8,128)(2,1)S(1)}, u32[]{:S(2)}, u32[]{:S(2)}) async-start(bf16[8,32,768]{2,1,0:T(8,128)(2,1)} %shard_map.81), calls=%async_computation.2 | async-start | bytes 786432 | tf_op jit(solution)/shard_map/all_to_all | solution.py:173
  113.5 11.9 %all-to-all-start.1 = ((bf16[8,32,256]{2,1,0:T(8,128)(2,1)}), bf16[8,32,256]{2,1,0:T(8,128)(2,1)S(1)}, u32[]{:S(2)}, u32[]{:S(2)}) async-start(bf16[8,32,256]{2,1,0:T(8,128)(2,1)} %bitcast.3), calls=%async_computation.1 | async-start | bytes 262144 | tf_op jit(solution)/shard_map/all_to_all | solution.py:173

commit v3 on v2

--- a/solution.py
+++ b/solution.py
@@ -66,7 +66,8 @@
 
 def aggregate_kernel(src_ref, cnt_ref, f_ref, w_ref, adj_ref, *refs):
     n = len(PLACE)
-    parts, a_ref, b_refs, c_refs, (both, t_ref, sems) = refs[:n], refs[n], refs[n + 1 : -5], refs[-5:-3], refs[-3:]
+    parts, (a_ref, low, high), b_refs = refs[:n], refs[n : n + 3], refs[n + 3 : -5]
+    c_refs, (both, t_ref, sems) = refs[-5:-3], refs[-3:]
     copies = []
     for q, part in enumerate(parts):
         copies.append(pltpu.make_async_copy(part, t_ref.at[pl.ds(PLACE[q], part.shape[0])], sems.at[q]))
@@ -76,13 +77,19 @@
     for copy in copies:
         copy.wait()
     me = lax.axis_index("yh") * 2 + lax.axis_index("core")
-    x0, y0 = lax.axis_index("x"), lax.axis_index("yl")
+    x0, y0, z0 = lax.axis_index("x"), lax.axis_index("yl"), lax.axis_index("z")
     b0, b1, b3, b20, b21 = b_refs
 
-    def step(z, _):
+    def step(d, _):
+        z = lax.bitwise_and(z0 + d, NZ - 1)
         for odd in range(2):
             got = weighted_sum(z * 2 + odd, src_ref, cnt_ref, me, adj_ref, t_ref)
-            a_ref[z, odd * BLK : (odd + 1) * BLK, :] = got[:, :HA]
+            a_ref[d, odd * BLK : (odd + 1) * BLK, :] = got[:, :HA]
+
+            @pl.when(d == NZ // 2)
+            def _():
+                (low, high)[odd][...] = got[:, :HA]
+
             both[odd * BLK : (odd + 1) * BLK, :] = got[:, HA:]
         at = pl.ds(pl.multiple_of(z * ROWS, ROWS), ROWS)
         for dx in range(NX):
@@ -100,7 +107,7 @@
 
 
 def aggregate(src, cnt, feat, weight, adj, parts):
-    shapes = [(NZ, 256, HA)] + [(NY, 256, HB)] * 3 + [(256, HB)] * 2 + [(NX, 256, HC)] * 2
+    shapes = [(NZ, 256, HA), (BLK, HA), (BLK, HA)] + [(NY, 256, HB)] * 3 + [(256, HB)] * 2 + [(NX, 256, HC)] * 2
     return pl.pallas_call(
         aggregate_kernel,
         out_shape=tuple(jax.ShapeDtypeStruct(shape, BF16) for shape in shapes),
@@ -133,6 +140,35 @@
     return total.astype(BF16)
 
 
+def a_relay(away):
+    def kernel(a, left, right, up, down):
+        if left.shape[0] < up.shape[0]:
+            half = left.shape[0]
+            up[:half] = add(a[away, :half], left[...])
+            up[half:] = a[away, half:]
+            down[:half] = a[NZ - away, :half]
+            down[half:] = add(a[NZ - away, half:], right[...])
+        else:
+            up[...] = add(a[away], left[...])
+            down[...] = add(a[NZ - away], right[...])
+
+    return kernel
+
+
+def a_sum(a, left, right, *outs):
+    x0, y0 = lax.axis_index("x"), lax.axis_index("yl")
+    for dx, out in enumerate(outs):
+        for dy in range(NY):
+            to = lax.bitwise_and(x0 + dx, NX - 1) * NY + lax.bitwise_xor(y0, dy)
+            rows = pl.ds(pl.multiple_of(to * ROWS, ROWS), ROWS)
+            out[dy] = add(a[0, rows, :], left[rows, :], right[rows, :])
+
+
+def a_meet(s0, s1, s2, s3, keep, send):
+    keep[...] = add(s0[0], s1[0], s2[0], s3[0])
+    send[...] = add(s0[1], s1[1], s2[1], s3[1])
+
+
 def b_relay(b1, b3, left, right, up, down):
     up[0] = add(b1[0], left[...])
     up[1] = b1[1]
@@ -171,6 +207,10 @@
 
 def exchange(x, axes):
     return lax.all_to_all(x, axes, 0, 0, tiled=True)
+
+
+def along_z(x, d):
+    return lax.ppermute(x, "z", [(i, (i + d) % NZ) for i in range(NZ)])
 
 
 def along_x(x, d):
@@ -191,7 +231,7 @@
         t_far.append(transform(f, rel_weight))
     for f in diag[:-1]:
         t_diag.append(transform(f, rel_weight))
-    out_a, b0, b1, b3, b20, b21, c0, c1 = aggregate(
+    a, low, high, b0, b1, b3, b20, b21, c0, c1 = aggregate(
         jnp.transpose(adj_source[0]),
         adj_count,
         diag[-1],
@@ -199,23 +239,28 @@
         adj_weight[0],
         [t_own, t_near] + t_far + t_diag,
     )
+    a_left, a_right = along_z(low, 1), along_z(high, -1)
     b_left, b_right = along_x(b20, 1), along_x(b21, -1)
     c_other = lax.ppermute(c1, "yl", swap)
-    got_a = exchange(out_a, "z")
+    for away in (3, 2, 1):
+        up, down = local(a_relay(away), [(256, HA)] * 2, a, a_left, a_right)
+        a_left, a_right = along_z(up, 1), along_z(down, -1)
     b_up, b_down = local(b_relay, [(NY, 256, HB)] * 2, b1, b3, b_left, b_right)
     b_left, b_right = along_x(b_up, 1), along_x(b_down, -1)
     shapes = [(256, HC), (256, HC), (BLK, HC), (BLK, HC), (256, HC)]
     c_own, c_up, c_low, c_high, c_down = local(c_split, shapes, c0, c_other)
     c_left, c_right = along_x(c_low, 1), along_x(c_high, -1)
+    b_keep, b_send = local(b_meet, [(256, HB)] * 2, b0, b_left, b_right)
+    b_other = lax.ppermute(b_send, "yl", swap)
     c_up, c_down = local(c_relay, [(256, HC)] * 2, c_up, c_down, c_left, c_right)
     c_left, c_right = along_x(c_up, 1), along_x(c_down, -1)
-    b_keep, b_send = local(b_meet, [(256, HB)] * 2, b0, b_left, b_right)
-    b_other = lax.ppermute(b_send, "yl", swap)
-    sum_a = got_a.astype(F32).sum(0).astype(BF16).reshape(NX * NY, ROWS, HA)
-    last_a = exchange(sum_a, ("x", "yl"))
+    s0, s1, s2, s3 = local(a_sum, [(NY, ROWS, HA)] * NX, a, a_left, a_right)
+    s1, s2, s3 = along_x(s1, 1), along_x(s2, 2), along_x(s3, 3)
     (joined,) = local(join, [(NZ, ROWS, HB + HC)], b_keep, b_other, c_own, c_left, c_right)
     last_b = exchange(joined, "z")
-    end_a = last_a.astype(F32).sum(0)
+    a_keep, a_send = local(a_meet, [(ROWS, HA)] * 2, s0, s1, s2, s3)
+    a_other = lax.ppermute(a_send, "yl", swap)
+    end_a = a_keep.astype(F32) + a_other.astype(F32)
     end_b = last_b.astype(F32).sum(0)
     summed = jnp.concatenate([end_a, end_b], axis=1)
     self_term = jnp.dot(tgt_feat, self_weight, preferred_element_type=F32)

time: 127 us -> 133 us (1.047)
  starting transfers between devices: 38.7 us -> 45.9 us
  local copies, waits for them, and re-layouts: 5.81 us -> 3.5 us
  waiting for transfers between devices: 57.2 us -> 59.4 us
  other arithmetic: 2.12 us -> 0.06 us
    ppermute x0 -> x9, waiting for transfers between devices: none -> 18.3 us  [the longest x8 15.3 us: along_z(): return lax.ppermute(x, 'z', [(i, (i + d) % NZ) for i in range(NZ)])]
    ppermute x0 -> x9, starting transfers between devices: none -> 16.7 us  [the longest x8 15.8 us: along_z(): return lax.ppermute(x, 'z', [(i, (i + d) % NZ) for i in range(NZ)])]
    all_to_all x3 -> x1, waiting for transfers between devices: 16.2 us -> 0.01 us  [exchange(): return lax.all_to_all(x, axes, 0, 0, tiled=True)]
    all_to_all x3 -> x1, starting transfers between devices: 20.7 us -> 5.82 us  [exchange(): return lax.all_to_all(x, axes, 0, 0, tiled=True)]
    ppermute x8 -> x11, starting transfers between devices: 13.3 us -> 18.7 us  [along_x(): return lax.ppermute(x, 'x', [(i, (i + d) % NX) for i in range(NX)])]
    unnamed x24 -> x16, local copies, waits for them, and re-layouts: 5.81 us -> 3.5 us
    reduce_sum x2 -> x0, other arithmetic: 2.07 us -> none  [the longest x1 2.05 us: layer(): sum_a = got_a.astype(F32).sum(0).astype(BF16).reshape(NX * NY, ROWS, HA)]
    ppermute x8 -> x11, waiting for transfers between devices: 21.7 us -> 22.1 us  [along_x(): return lax.ppermute(x, 'x', [(i, (i + d) % NX) for i in range(NX)])]
  transfers between devices with their start and end apart: 16 -> 26, of which waited for: 8 -> 10; matrix products, arithmetic and copies ran while one was open for 2% -> 0% of each run, Pallas kernels for 9% -> 9%
where the time goes in v3:
time: 133 us; the launch traced here: 132 us
  waiting for transfers between devices  59.4 us (45%)
  starting transfers between devices  45.9 us (35%)
  Pallas kernels  22.3 us (17%)
  local copies, waits for them, and re-layouts  3.5 us (3%)
    ppermute x11, waiting for transfers between devices, along_x(): return lax.ppermute(x, 'x', [(i, (i + d) % NX) for i in range(NX)])  22.1 us
    ppermute x1, waiting for transfers between devices, layer(): far.append(lax.ppermute(f, 'yh', swap))  18.9 us
    ppermute x11, starting transfers between devices, along_x(): return lax.ppermute(x, 'x', [(i, (i + d) % NX) for i in range(NX)])  18.7 us
    ppermute x8, starting transfers between devices, along_z(): return lax.ppermute(x, 'z', [(i, (i + d) % NZ) for i in range(NZ)])  15.8 us
    ppermute x8, waiting for transfers between devices, along_z(): return lax.ppermute(x, 'z', [(i, (i + d) % NZ) for i in range(NZ)])  15.3 us
    pallas_call x3, Pallas kernels, transform(): pl.pallas_call(transform_kernel, out_shape=jax.ShapeDtypeStruct((REL * fe...  10.5 us
    pallas_call x1, Pallas kernels, aggregate(): pl.pallas_call(aggregate_kernel, out_shape=tuple((jax.ShapeDtypeStruct(sh...  10.3 us
    all_to_all x1, starting transfers between devices, exchange(): return lax.all_to_all(x, axes, 0, 0, tiled=True)  5.82 us
  transfers between devices with their start and end apart: 26, of which 10 were waited for; matrix products, arithmetic and copies ran while one was open for 0% of the time, Pallas kernels for 9%

profile of v3, /device:TPU:16, one launch (start us, length us, event | category | flops | bytes accessed | tf_op | source)
XLA Modules:
  0.0 132.4 jit_solution(11817239057246685321)
XLA Ops:
  0.0 2.0 %collective-permute-start = (bf16[512,768]{1,0:T(8,128)(2,1)}, bf16[512,768]{1,0:T(8,128)(2,1)S(1)}, u32[]{:S(2)}, u32[]{:S(2)}) collective-permute-start(bf16[512,768]{1,0:T(8,128)(2,1)} %f_ref.1), channel_id=1, source_target_pairs={{0,2},{2,0},{1,3},{3,1},{4,6},{6,4},{5,7},{7,5},{8,10},{10,8},{9,1... | collective-permute-start | bytes 2359304 | tf_op jit(solution)/shard_map/ppermute | solution.py:224
  2.0 18.9 %collective-permute-done.f_ref = bf16[512,768]{1,0:T(8,128)(2,1)S(1)} collective-permute-done((bf16[512,768]{1,0:T(8,128)(2,1)}, bf16[512,768]{1,0:T(8,128)(2,1)S(1)}, u32[]{:S(2)}, u32[]{:S(2)}) %collective-permute-start) | collective-permute-done | bytes 786464 | tf_op jit(solution)/shard_map/ppermute | solution.py:224
  21.0 2.3 %copy-done.1 = bf16[3,768,1024]{2,1,0:T(8,128)(2,1)S(1)} copy-done((bf16[3,768,1024]{2,1,0:T(8,128)(2,1)S(1)}, bf16[3,768,1024]{2,1,0:T(8,128)(2,1)}, u32[]{:S(2)}) %copy-start.1) | copy-done | bytes 4718616
  24.5 3.5 %shard_map.73.refs_0_ = bf16[12,128,1024]{2,1,0:T(8,128)(2,1)S(1)} custom-call(bf16[512,768]{1,0:T(8,128)(2,1)S(1)} %copy-done.4, bf16[3,768,1024]{2,1,0:T(8,128)(2,1)S(1)} %copy-done.1), custom_call_target="tpu_custom_call" | custom-call | flops 2415919104 | bytes 8388608 | tf_op jit(solution)/shard_map/pallas_call | solution.py:40
  28.0 3.5 %shard_map.75.refs_2_ = bf16[12,128,1024]{2,1,0:T(8,128)(2,1)S(1)} custom-call(bf16[512,768]{1,0:T(8,128)(2,1)S(1)} %collective-permute-done.f_ref, bf16[3,768,1024]{2,1,0:T(8,128)(2,1)S(1)} %copy-done.2), custom_call_target="tpu_custom_call" | custom-call | flops 2415919104 | bytes 8388608 | tf_op jit(solution)/shard_map/pallas_call | solution.py:40
  31.5 3.5 %shard_map.74.refs_1_ = bf16[12,128,1024]{2,1,0:T(8,128)(2,1)S(1)} custom-call(bf16[512,768]{1,0:T(8,128)(2,1)S(1)} %collective-permute-done.2.f_ref, bf16[3,768,1024]{2,1,0:T(8,128)(2,1)S(1)} %copy-done.2), custom_call_target="tpu_custom_call" | custom-call | flops 2415919104 | bytes 8388608 | tf_op jit(solution)/shard_map/pallas_call | solution.py:40
  35.1 10.3 %shard_map.76 = (bf16[8,256,256]{2,1,0:T(8,128)(2,1)S(1)}, bf16[128,256]{1,0:T(8,128)(2,1)S(1)}, bf16[128,256]{1,0:T(8,128)(2,1)S(1)}, bf16[2,256,512]{2,1,0:T(8...) custom-call(s32[4,16]{1,0:T(4,128)S(1)} %bitcast.7, ...), custom_call_target="tpu_custom_call" | custom-call | flops 6442450944 | bytes 20971520 | tf_op jit(solution)/shard_map/pallas_call | solution.py:111
  45.3 1.6 %collective-permute-start.15 = (bf16[256,512]{1,0:T(8,128)(2,1)S(1)}, bf16[256,512]{1,0:T(8,128)(2,1)S(1)}, u32[]{:S(2)}, u32[]{:S(2)}) collective-permute-start(bf16[256,512]{1,0:T(8,128)(2,1)S(1)} %get-tuple-element.56), channel_id=1, source_target_pairs={{0,8},{8,16},{16,24},{24,0},{1,9},{9,17},{17,25},{25,1},{2,10},{10... | collective-permute-start | bytes 786440 | tf_op jit(solution)/shard_map/ppermute | solution.py:217
  46.9 1.7 %collective-permute-start.16 = (bf16[256,512]{1,0:T(8,128)(2,1)S(1)}, bf16[256,512]{1,0:T(8,128)(2,1)S(1)}, u32[]{:S(2)}, u32[]{:S(2)}) collective-permute-start(bf16[256,512]{1,0:T(8,128)(2,1)S(1)} %get-tuple-element.57), channel_id=1, source_target_pairs={{0,24},{8,0},{16,8},{24,16},{1,25},{9,1},{17,9},{25,17},{2,26},{10... | collective-permute-start | bytes 786440 | tf_op jit(solution)/shard_map/ppermute | solution.py:217
  48.6 6.7 %collective-permute-done.15.left = bf16[256,512]{1,0:T(8,128)(2,1)S(1)} collective-permute-done((bf16[256,512]{1,0:T(8,128)(2,1)S(1)}, bf16[256,512]{1,0:T(8,128)(2,1)S(1)}, u32[]{:S(2)}, u32[]{:S(2)}) %collective-permute-start.15) | collective-permute-done | bytes 262176 | tf_op jit(solution)/shard_map/ppermute | solution.py:217
  55.5 1.5 %collective-permute-start.17 = (bf16[2,256,512]{2,1,0:T(8,128)(2,1)S(1)}, bf16[2,256,512]{2,1,0:T(8,128)(2,1)S(1)}, u32[]{:S(2)}, u32[]{:S(2)}) collective-permute-start(bf16[2,256,512]{2,1,0:T(8,128)(2,1)S(1)} %get-tuple-element.58), channel_id=1, source_target_pairs={{0,8},{8,16},{16,24},{24,0},{1,9},{9,17},{17,25},{25,1},{2,10},{10... | collective-permute-start | bytes 1572872 | tf_op jit(solution)/shard_map/ppermute | solution.py:217
  57.0 1.8 %collective-permute-start.18 = (bf16[2,256,512]{2,1,0:T(8,128)(2,1)S(1)}, bf16[2,256,512]{2,1,0:T(8,128)(2,1)S(1)}, u32[]{:S(2)}, u32[]{:S(2)}) collective-permute-start(bf16[2,256,512]{2,1,0:T(8,128)(2,1)S(1)} %get-tuple-element.59), channel_id=1, source_target_pairs={{0,24},{8,0},{16,8},{24,16},{1,25},{9,1},{17,9},{25,17},{2,26},{10... | collective-permute-start | bytes 1572872 | tf_op jit(solution)/shard_map/ppermute | solution.py:217
  60.1 10.2 %collective-permute-done.17.left = bf16[2,256,512]{2,1,0:T(8,128)(2,1)S(1)} collective-permute-done((bf16[2,256,512]{2,1,0:T(8,128)(2,1)S(1)}, bf16[2,256,512]{2,1,0:T(8,128)(2,1)S(1)}, u32[]{:S(2)}, u32[]{:S(2)}) %collective-permute-start.17) | collective-permute-done | bytes 524320 | tf_op jit(solution)/shard_map/ppermute | solution.py:217
  70.5 1.4 %collective-permute-start.19 = (bf16[256,512]{1,0:T(8,128)(2,1)S(1)}, bf16[256,512]{1,0:T(8,128)(2,1)S(1)}, u32[]{:S(2)}, u32[]{:S(2)}) collective-permute-start(bf16[256,512]{1,0:T(8,128)(2,1)S(1)} %get-tuple-element.61), channel_id=1, source_target_pairs={{0,4},{4,0},{1,5},{5,1},{2,6},{6,2},{3,7},{7,3},{8,12},{12,8},{9,1... | collective-permute-start | bytes 786440 | tf_op jit(solution)/shard_map/ppermute | solution.py:254
  73.0 2.3 %collective-permute-start.22 = (bf16[128,256]{1,0:T(8,128)(2,1)S(1)}, bf16[128,256]{1,0:T(8,128)(2,1)S(1)}, u32[]{:S(2)}, u32[]{:S(2)}) collective-permute-start(bf16[128,256]{1,0:T(8,128)(2,1)S(1)} %get-tuple-element.68), channel_id=1, source_target_pairs={{0,24},{8,0},{16,8},{24,16},{1,25},{9,1},{17,9},{25,17},{2,26},{10... | collective-permute-start | bytes 196616 | tf_op jit(solution)/shard_map/ppermute | solution.py:217
  75.3 2.2 %collective-permute-done.21.left = bf16[128,256]{1,0:T(8,128)(2,1)S(1)} collective-permute-done((bf16[128,256]{1,0:T(8,128)(2,1)S(1)}, bf16[128,256]{1,0:T(8,128)(2,1)S(1)}, u32[]{:S(2)}, u32[]{:S(2)}) %collective-permute-start.21) | collective-permute-done | bytes 65568 | tf_op jit(solution)/shard_map/ppermute | solution.py:217
  77.6 1.5 %collective-permute-start.23 = (bf16[256,256]{1,0:T(8,128)(2,1)S(1)}, bf16[256,256]{1,0:T(8,128)(2,1)S(1)}, u32[]{:S(2)}, u32[]{:S(2)}) collective-permute-start(bf16[256,256]{1,0:T(8,128)(2,1)S(1)} %get-tuple-element.69), channel_id=1, source_target_pairs={{0,8},{8,16},{16,24},{24,0},{1,9},{9,17},{17,25},{25,1},{2,10},{10... | collective-permute-start | bytes 393224 | tf_op jit(solution)/shard_map/ppermute | solution.py:217
  79.0 1.9 %collective-permute-start.24 = (bf16[256,256]{1,0:T(8,128)(2,1)S(1)}, bf16[256,256]{1,0:T(8,128)(2,1)S(1)}, u32[]{:S(2)}, u32[]{:S(2)}) collective-permute-start(bf16[256,256]{1,0:T(8,128)(2,1)S(1)} %get-tuple-element.70), channel_id=1, source_target_pairs={{0,24},{8,0},{16,8},{24,16},{1,25},{9,1},{17,9},{25,17},{2,26},{10... | collective-permute-start | bytes 393224 | tf_op jit(solution)/shard_map/ppermute | solution.py:217
  81.0 1.9 %collective-permute-start.3 = (bf16[128,256]{1,0:T(8,128)(2,1)S(1)}, bf16[128,256]{1,0:T(8,128)(2,1)S(1)}, u32[]{:S(2)}, u32[]{:S(2)}) collective-permute-start(bf16[128,256]{1,0:T(8,128)(2,1)S(1)} %get-tuple-element.39), channel_id=1, source_target_pairs={{0,32},{32,64},{64,96},{96,128},{128,160},{160,192},{192,224},{224... | collective-permute-start | bytes 196616 | tf_op jit(solution)/shard_map/ppermute | solution.py:213
  82.8 4.0 %collective-permute-start.4 = (bf16[128,256]{1,0:T(8,128)(2,1)S(1)}, bf16[128,256]{1,0:T(8,128)(2,1)S(1)}, u32[]{:S(2)}, u32[]{:S(2)}) collective-permute-start(bf16[128,256]{1,0:T(8,128)(2,1)S(1)} %get-tuple-element.40), channel_id=1, source_target_pairs={{0,224},{32,0},{64,32},{96,64},{128,96},{160,128},{192,160},{224,1... | collective-permute-start | bytes 196616 | tf_op jit(solution)/shard_map/ppermute | solution.py:213
  87.7 5.8 %all-to-all-start = ((bf16[8,32,768]{2,1,0:T(8,128)(2,1)}), bf16[8,32,768]{2,1,0:T(8,128)(2,1)S(1)}, u32[]{:S(2)}, u32[]{:S(2)}) async-start(bf16[8,32,768]{2,1,0:T(8,128)(2,1)} %shard_map.86), calls=%async_computation | async-start | bytes 786432 | tf_op jit(solution)/shard_map/all_to_all | solution.py:209
  93.5 2.1 %collective-permute-start.5 = (bf16[256,256]{1,0:T(8,128)(2,1)S(1)}, bf16[256,256]{1,0:T(8,128)(2,1)S(1)}, u32[]{:S(2)}, u32[]{:S(2)}) collective-permute-start(bf16[256,256]{1,0:T(8,128)(2,1)S(1)} %get-tuple-element.41), channel_id=1, source_target_pairs={{0,32},{32,64},{64,96},{96,128},{128,160},{160,192},{192,224},{224... | collective-permute-start | bytes 393224 | tf_op jit(solution)/shard_map/ppermute | solution.py:213
  95.6 1.3 collective-permute-start.6
  97.0 8.7 %collective-permute-done.5.left = bf16[256,256]{1,0:T(8,128)(2,1)S(1)} collective-permute-done((bf16[256,256]{1,0:T(8,128)(2,1)S(1)}, bf16[256,256]{1,0:T(8,128)(2,1)S(1)}, u32[]{:S(2)}, u32[]{:S(2)}) %collective-permute-start.5) | collective-permute-done | bytes 131104 | tf_op jit(solution)/shard_map/ppermute | solution.py:213
  105.8 3.2 %collective-permute-start.8 = (bf16[256,256]{1,0:T(8,128)(2,1)S(1)}, bf16[256,256]{1,0:T(8,128)(2,1)S(1)}, u32[]{:S(2)}, u32[]{:S(2)}) collective-permute-start(bf16[256,256]{1,0:T(8,128)(2,1)S(1)} %get-tuple-element.44), channel_id=1, source_target_pairs={{0,224},{32,0},{64,32},{96,64},{128,96},{160,128},{192,160},{224,1... | collective-permute-start | bytes 393224 | tf_op jit(solution)/shard_map/ppermute | solution.py:213
  109.0 3.7 %collective-permute-done.7.left = bf16[256,256]{1,0:T(8,128)(2,1)S(1)} collective-permute-done((bf16[256,256]{1,0:T(8,128)(2,1)S(1)}, bf16[256,256]{1,0:T(8,128)(2,1)S(1)}, u32[]{:S(2)}, u32[]{:S(2)}) %collective-permute-start.7) | collective-permute-done | bytes 131104 | tf_op jit(solution)/shard_map/ppermute | solution.py:213
  112.8 3.2 %collective-permute-start.10 = (bf16[256,256]{1,0:T(8,128)(2,1)S(1)}, bf16[256,256]{1,0:T(8,128)(2,1)S(1)}, u32[]{:S(2)}, u32[]{:S(2)}) collective-permute-start(bf16[256,256]{1,0:T(8,128)(2,1)S(1)} %get-tuple-element.46), channel_id=1, source_target_pairs={{0,224},{32,0},{64,32},{96,64},{128,96},{160,128},{192,160},{224,1... | collective-permute-start | bytes 393224 | tf_op jit(solution)/shard_map/ppermute | solution.py:213
  116.1 2.9 %collective-permute-done.9.left = bf16[256,256]{1,0:T(8,128)(2,1)S(1)} collective-permute-done((bf16[256,256]{1,0:T(8,128)(2,1)S(1)}, bf16[256,256]{1,0:T(8,128)(2,1)S(1)}, u32[]{:S(2)}, u32[]{:S(2)}) %collective-permute-start.9) | collective-permute-done | bytes 131104 | tf_op jit(solution)/shard_map/ppermute | solution.py:213
  120.3 3.2 %collective-permute-start.12 = (bf16[2,32,256]{2,1,0:T(8,128)(2,1)S(1)}, bf16[2,32,256]{2,1,0:T(8,128)(2,1)S(1)}, u32[]{:S(2)}, u32[]{:S(2)}) collective-permute-start(bf16[2,32,256]{2,1,0:T(8,128)(2,1)S(1)} %get-tuple-element.49), channel_id=1, source_target_pairs={{0,16},{8,24},{16,0},{24,8},{1,17},{9,25},{17,1},{25,9},{2,18},{10... | collective-permute-start | bytes 98312 | tf_op jit(solution)/shard_map/ppermute | solution.py:217
  124.5 1.3 collective-permute-done.12.s2
  125.8 1.7 %collective-permute-done.13.s3 = bf16[2,32,256]{2,1,0:T(8,128)(2,1)S(1)} collective-permute-done((bf16[2,32,256]{2,1,0:T(8,128)(2,1)S(1)}, bf16[2,32,256]{2,1,0:T(8,128)(2,1)S(1)}, u32[]{:S(2)}, u32[]{:S(2)}) %collective-permute-start.13) | collective-permute-done | bytes 32800 | tf_op jit(solution)/shard_map/ppermute | solution.py:217
  128.3 3.0 %collective-permute-done.14 = bf16[32,256]{1,0:T(8,128)(2,1)S(1)} collective-permute-done((bf16[32,256]{1,0:T(8,128)(2,1)S(1)}, bf16[32,256]{1,0:T(8,128)(2,1)S(1)}, u32[]{:S(2)}, u32[]{:S(2)}) %collective-permute-start.14) | collective-permute-done | bytes 16416 | tf_op jit(solution)/shard_map/ppermute | solution.py:262
  (53 shorter events, 9.4 us)
Async XLA Ops:
  0.0 131.4 %copy-start = (bf16[768,1024]{1,0:T(8,128)(2,1)S(1)}, bf16[768,1024]{1,0:T(8,128)(2,1)}, u32[]{:S(2)}) copy-start(bf16[768,1024]{1,0:T(8,128)(2,1)} %param.10) | copy-start | bytes 4718596
  0.0 21.0 %collective-permute-start = (bf16[512,768]{1,0:T(8,128)(2,1)}, bf16[512,768]{1,0:T(8,128)(2,1)S(1)}, u32[]{:S(2)}, u32[]{:S(2)}) collective-permute-start(bf16[512,768]{1,0:T(8,128)(2,1)} %f_ref.1), channel_id=1, source_target_pairs={{0,2},{2,0},{1,3},{3,1},{4,6},{6,4},{5,7},{7,5},{8,10},{10,8},{9,1... | collective-permute-start | bytes 2359304 | tf_op jit(solution)/shard_map/ppermute | solution.py:224
  2.0 29.5 %collective-permute-start.2 = (bf16[512,768]{1,0:T(8,128)(2,1)}, bf16[512,768]{1,0:T(8,128)(2,1)S(1)}, u32[]{:S(2)}, u32[]{:S(2)}) collective-permute-start(bf16[512,768]{1,0:T(8,128)(2,1)} %f_ref.1), channel_id=1, source_target_pairs={{0,1},{1,0},{2,3},{3,2},{4,5},{5,4},{6,7},{7,6},{8,9},{9,8},{10,11... | collective-permute-start | bytes 2359304 | tf_op jit(solution)/shard_map/ppermute | solution.py:225
  21.0 14.0 %collective-permute-start.1 = (bf16[512,768]{1,0:T(8,128)(2,1)S(1)}, bf16[512,768]{1,0:T(8,128)(2,1)S(1)}, u32[]{:S(2)}, u32[]{:S(2)}) collective-permute-start(bf16[512,768]{1,0:T(8,128)(2,1)S(1)} %collective-permute-done.f_ref), channel_id=1, source_target_pairs={{0,1},{1,0},{2,3},{3,2},{4,5},{5,4},{6,7},{7,6},{8,9},{9,8},{10,11... | collective-permute-start | bytes 2359304 | tf_op jit(solution)/shard_map/ppermute | solution.py:230
  24.5 3.5 %copy-start.2 = (bf16[3,768,1024]{2,1,0:T(8,128)(2,1)S(1)}, bf16[3,768,1024]{2,1,0:T(8,128)(2,1)}, u32[]{:S(2)}) copy-start(bf16[3,768,1024]{2,1,0:T(8,128)(2,1)} %w_ref.7) | copy-start | bytes 14155780
  31.5 3.6 %copy-start.3 = (bf16[1,16,4,128,128]{4,3,2,1,0:T(8,128)(2,1)S(1)}, bf16[1,16,4,128,128]{4,3,2,1,0:T(8,128)(2,1)}, u32[]{:S(2)}) copy-start(bf16[1,16,4,128,128]{4,3,2,1,0:T(8,128)(2,1)} %param.11) | copy-start | bytes 6291460
  31.5 3.6 %copy-start.5 = (s32[1,16,4]{1,2,0:T(4,128)S(1)}, s32[1,16,4]{1,2,0:T(4,128)}, u32[]{:S(2)}) copy-start(s32[1,16,4]{1,2,0:T(4,128)} %param.12) | copy-start | bytes 772
  31.5 3.6 %copy-start.6 = (s32[1,16]{1,0:T(1,128)S(1)}, s32[1,16]{1,0:T(1,128)}, u32[]{:S(2)}) copy-start(s32[1,16]{1,0:T(1,128)} %cnt_ref.1) | copy-start | bytes 196
  45.3 10.0 %collective-permute-start.15 = (bf16[256,512]{1,0:T(8,128)(2,1)S(1)}, bf16[256,512]{1,0:T(8,128)(2,1)S(1)}, u32[]{:S(2)}, u32[]{:S(2)}) collective-permute-start(bf16[256,512]{1,0:T(8,128)(2,1)S(1)} %get-tuple-element.56), channel_id=1, source_target_pairs={{0,8},{8,16},{16,24},{24,0},{1,9},{9,17},{17,25},{25,1},{2,10},{10... | collective-permute-start | bytes 786440 | tf_op jit(solution)/shard_map/ppermute | solution.py:217
  46.9 8.4 %collective-permute-start.16 = (bf16[256,512]{1,0:T(8,128)(2,1)S(1)}, bf16[256,512]{1,0:T(8,128)(2,1)S(1)}, u32[]{:S(2)}, u32[]{:S(2)}) collective-permute-start(bf16[256,512]{1,0:T(8,128)(2,1)S(1)} %get-tuple-element.57), channel_id=1, source_target_pairs={{0,24},{8,0},{16,8},{24,16},{1,25},{9,1},{17,9},{25,17},{2,26},{10... | collective-permute-start | bytes 786440 | tf_op jit(solution)/shard_map/ppermute | solution.py:217
  55.5 14.8 %collective-permute-start.17 = (bf16[2,256,512]{2,1,0:T(8,128)(2,1)S(1)}, bf16[2,256,512]{2,1,0:T(8,128)(2,1)S(1)}, u32[]{:S(2)}, u32[]{:S(2)}) collective-permute-start(bf16[2,256,512]{2,1,0:T(8,128)(2,1)S(1)} %get-tuple-element.58), channel_id=1, source_target_pairs={{0,8},{8,16},{16,24},{24,0},{1,9},{9,17},{17,25},{25,1},{2,10},{10... | collective-permute-start | bytes 1572872 | tf_op jit(solution)/shard_map/ppermute | solution.py:217
  57.0 13.2 %collective-permute-start.18 = (bf16[2,256,512]{2,1,0:T(8,128)(2,1)S(1)}, bf16[2,256,512]{2,1,0:T(8,128)(2,1)S(1)}, u32[]{:S(2)}, u32[]{:S(2)}) collective-permute-start(bf16[2,256,512]{2,1,0:T(8,128)(2,1)S(1)} %get-tuple-element.59), channel_id=1, source_target_pairs={{0,24},{8,0},{16,8},{24,16},{1,25},{9,1},{17,9},{25,17},{2,26},{10... | collective-permute-start | bytes 1572872 | tf_op jit(solution)/shard_map/ppermute | solution.py:217
  58.8 13.0 %collective-permute-start.20 = (bf16[4,256,256]{2,1,0:T(8,128)(2,1)S(1)}, bf16[4,256,256]{2,1,0:T(8,128)(2,1)S(1)}, u32[]{:S(2)}, u32[]{:S(2)}) collective-permute-start(bf16[4,256,256]{2,1,0:T(8,128)(2,1)S(1)} %get-tuple-element.63), channel_id=1, source_target_pairs={{0,4},{4,0},{1,5},{5,1},{2,6},{6,2},{3,7},{7,3},{8,12},{12,8},{9,1... | collective-permute-start | bytes 1572872 | tf_op jit(solution)/shard_map/ppermute | solution.py:244
  70.5 16.3 %collective-permute-start.19 = (bf16[256,512]{1,0:T(8,128)(2,1)S(1)}, bf16[256,512]{1,0:T(8,128)(2,1)S(1)}, u32[]{:S(2)}, u32[]{:S(2)}) collective-permute-start(bf16[256,512]{1,0:T(8,128)(2,1)S(1)} %get-tuple-element.61), channel_id=1, source_target_pairs={{0,4},{4,0},{1,5},{5,1},{2,6},{6,2},{3,7},{7,3},{8,12},{12,8},{9,1... | collective-permute-start | bytes 786440 | tf_op jit(solution)/shard_map/ppermute | solution.py:254
  72.0 5.6 %collective-permute-start.21 = (bf16[128,256]{1,0:T(8,128)(2,1)S(1)}, bf16[128,256]{1,0:T(8,128)(2,1)S(1)}, u32[]{:S(2)}, u32[]{:S(2)}) collective-permute-start(bf16[128,256]{1,0:T(8,128)(2,1)S(1)} %get-tuple-element.67), channel_id=1, source_target_pairs={{0,8},{8,16},{16,24},{24,0},{1,9},{9,17},{17,25},{25,1},{2,10},{10... | collective-permute-start | bytes 196616 | tf_op jit(solution)/shard_map/ppermute | solution.py:217
  73.0 4.5 %collective-permute-start.22 = (bf16[128,256]{1,0:T(8,128)(2,1)S(1)}, bf16[128,256]{1,0:T(8,128)(2,1)S(1)}, u32[]{:S(2)}, u32[]{:S(2)}) collective-permute-start(bf16[128,256]{1,0:T(8,128)(2,1)S(1)} %get-tuple-element.68), channel_id=1, source_target_pairs={{0,24},{8,0},{16,8},{24,16},{1,25},{9,1},{17,9},{25,17},{2,26},{10... | collective-permute-start | bytes 196616 | tf_op jit(solution)/shard_map/ppermute | solution.py:217
  77.6 9.2 %collective-permute-start.23 = (bf16[256,256]{1,0:T(8,128)(2,1)S(1)}, bf16[256,256]{1,0:T(8,128)(2,1)S(1)}, u32[]{:S(2)}, u32[]{:S(2)}) collective-permute-start(bf16[256,256]{1,0:T(8,128)(2,1)S(1)} %get-tuple-element.69), channel_id=1, source_target_pairs={{0,8},{8,16},{16,24},{24,0},{1,9},{9,17},{17,25},{25,1},{2,10},{10... | collective-permute-start | bytes 393224 | tf_op jit(solution)/shard_map/ppermute | solution.py:217
  79.0 7.8 %collective-permute-start.24 = (bf16[256,256]{1,0:T(8,128)(2,1)S(1)}, bf16[256,256]{1,0:T(8,128)(2,1)S(1)}, u32[]{:S(2)}, u32[]{:S(2)}) collective-permute-start(bf16[256,256]{1,0:T(8,128)(2,1)S(1)} %get-tuple-element.70), channel_id=1, source_target_pairs={{0,24},{8,0},{16,8},{24,16},{1,25},{9,1},{17,9},{25,17},{2,26},{10... | collective-permute-start | bytes 393224 | tf_op jit(solution)/shard_map/ppermute | solution.py:217
  81.0 12.5 %collective-permute-start.3 = (bf16[128,256]{1,0:T(8,128)(2,1)S(1)}, bf16[128,256]{1,0:T(8,128)(2,1)S(1)}, u32[]{:S(2)}, u32[]{:S(2)}) collective-permute-start(bf16[128,256]{1,0:T(8,128)(2,1)S(1)} %get-tuple-element.39), channel_id=1, source_target_pairs={{0,32},{32,64},{64,96},{96,128},{128,160},{160,192},{192,224},{224... | collective-permute-start | bytes 196616 | tf_op jit(solution)/shard_map/ppermute | solution.py:213
  82.8 10.7 %collective-permute-start.4 = (bf16[128,256]{1,0:T(8,128)(2,1)S(1)}, bf16[128,256]{1,0:T(8,128)(2,1)S(1)}, u32[]{:S(2)}, u32[]{:S(2)}) collective-permute-start(bf16[128,256]{1,0:T(8,128)(2,1)S(1)} %get-tuple-element.40), channel_id=1, source_target_pairs={{0,224},{32,0},{64,32},{96,64},{128,96},{160,128},{192,160},{224,1... | collective-permute-start | bytes 196616 | tf_op jit(solution)/shard_map/ppermute | solution.py:213
  87.7 43.7 %all-to-all-start = ((bf16[8,32,768]{2,1,0:T(8,128)(2,1)}), bf16[8,32,768]{2,1,0:T(8,128)(2,1)S(1)}, u32[]{:S(2)}, u32[]{:S(2)}) async-start(bf16[8,32,768]{2,1,0:T(8,128)(2,1)} %shard_map.86), calls=%async_computation | async-start | bytes 786432 | tf_op jit(solution)/shard_map/all_to_all | solution.py:209
  93.5 12.1 %collective-permute-start.5 = (bf16[256,256]{1,0:T(8,128)(2,1)S(1)}, bf16[256,256]{1,0:T(8,128)(2,1)S(1)}, u32[]{:S(2)}, u32[]{:S(2)}) collective-permute-start(bf16[256,256]{1,0:T(8,128)(2,1)S(1)} %get-tuple-element.41), channel_id=1, source_target_pairs={{0,32},{32,64},{64,96},{96,128},{128,160},{160,192},{192,224},{224... | collective-permute-start | bytes 393224 | tf_op jit(solution)/shard_map/ppermute | solution.py:213
  95.6 35.8 %copy-start.7 = (bf16[32,768]{1,0:T(8,128)(2,1)S(1)}, bf16[32,768]{1,0:T(8,128)(2,1)}, u32[]{:S(2)}) copy-start(bf16[32,768]{1,0:T(8,128)(2,1)} %param.8) | copy-start | bytes 147460
  95.6 10.0 %collective-permute-start.6 = (bf16[256,256]{1,0:T(8,128)(2,1)S(1)}, bf16[256,256]{1,0:T(8,128)(2,1)S(1)}, u32[]{:S(2)}, u32[]{:S(2)}) collective-permute-start(bf16[256,256]{1,0:T(8,128)(2,1)S(1)} %get-tuple-element.42), channel_id=1, source_target_pairs={{0,224},{32,0},{64,32},{96,64},{128,96},{160,128},{192,160},{224,1... | collective-permute-start | bytes 393224 | tf_op jit(solution)/shard_map/ppermute | solution.py:213
  105.7 7.0 %collective-permute-start.7 = (bf16[256,256]{1,0:T(8,128)(2,1)S(1)}, bf16[256,256]{1,0:T(8,128)(2,1)S(1)}, u32[]{:S(2)}, u32[]{:S(2)}) collective-permute-start(bf16[256,256]{1,0:T(8,128)(2,1)S(1)} %get-tuple-element.43), channel_id=1, source_target_pairs={{0,32},{32,64},{64,96},{96,128},{128,160},{160,192},{192,224},{224... | collective-permute-start | bytes 393224 | tf_op jit(solution)/shard_map/ppermute | solution.py:213
  105.8 6.9 %collective-permute-start.8 = (bf16[256,256]{1,0:T(8,128)(2,1)S(1)}, bf16[256,256]{1,0:T(8,128)(2,1)S(1)}, u32[]{:S(2)}, u32[]{:S(2)}) collective-permute-start(bf16[256,256]{1,0:T(8,128)(2,1)S(1)} %get-tuple-element.44), channel_id=1, source_target_pairs={{0,224},{32,0},{64,32},{96,64},{128,96},{160,128},{192,160},{224,1... | collective-permute-start | bytes 393224 | tf_op jit(solution)/shard_map/ppermute | solution.py:213
  112.7 6.3 %collective-permute-start.9 = (bf16[256,256]{1,0:T(8,128)(2,1)S(1)}, bf16[256,256]{1,0:T(8,128)(2,1)S(1)}, u32[]{:S(2)}, u32[]{:S(2)}) collective-permute-start(bf16[256,256]{1,0:T(8,128)(2,1)S(1)} %get-tuple-element.45), channel_id=1, source_target_pairs={{0,32},{32,64},{64,96},{96,128},{128,160},{160,192},{192,224},{224... | collective-permute-start | bytes 393224 | tf_op jit(solution)/shard_map/ppermute | solution.py:213
  112.8 6.2 %collective-permute-start.10 = (bf16[256,256]{1,0:T(8,128)(2,1)S(1)}, bf16[256,256]{1,0:T(8,128)(2,1)S(1)}, u32[]{:S(2)}, u32[]{:S(2)}) collective-permute-start(bf16[256,256]{1,0:T(8,128)(2,1)S(1)} %get-tuple-element.46), channel_id=1, source_target_pairs={{0,224},{32,0},{64,32},{96,64},{128,96},{160,128},{192,160},{224,1... | collective-permute-start | bytes 393224 | tf_op jit(solution)/shard_map/ppermute | solution.py:213
  119.1 5.4 %collective-permute-start.11 = (bf16[2,32,256]{2,1,0:T(8,128)(2,1)S(1)}, bf16[2,32,256]{2,1,0:T(8,128)(2,1)S(1)}, u32[]{:S(2)}, u32[]{:S(2)}) collective-permute-start(bf16[2,32,256]{2,1,0:T(8,128)(2,1)S(1)} %get-tuple-element.48), channel_id=1, source_target_pairs={{0,8},{8,16},{16,24},{24,0},{1,9},{9,17},{17,25},{25,1},{2,10},{10... | collective-permute-start | bytes 98312 | tf_op jit(solution)/shard_map/ppermute | solution.py:217
  120.3 5.5 %collective-permute-start.12 = (bf16[2,32,256]{2,1,0:T(8,128)(2,1)S(1)}, bf16[2,32,256]{2,1,0:T(8,128)(2,1)S(1)}, u32[]{:S(2)}, u32[]{:S(2)}) collective-permute-start(bf16[2,32,256]{2,1,0:T(8,128)(2,1)S(1)} %get-tuple-element.49), channel_id=1, source_target_pairs={{0,16},{8,24},{16,0},{24,8},{1,17},{9,25},{17,1},{25,9},{2,18},{10... | collective-permute-start | bytes 98312 | tf_op jit(solution)/shard_map/ppermute | solution.py:217
  123.5 3.9 %collective-permute-start.13 = (bf16[2,32,256]{2,1,0:T(8,128)(2,1)S(1)}, bf16[2,32,256]{2,1,0:T(8,128)(2,1)S(1)}, u32[]{:S(2)}, u32[]{:S(2)}) collective-permute-start(bf16[2,32,256]{2,1,0:T(8,128)(2,1)S(1)} %get-tuple-element.50), channel_id=1, source_target_pairs={{0,24},{8,0},{16,8},{24,16},{1,25},{9,1},{17,9},{25,17},{2,26},{10... | collective-permute-start | bytes 98312 | tf_op jit(solution)/shard_map/ppermute | solution.py:217
  127.5 3.8 %collective-permute-start.14 = (bf16[32,256]{1,0:T(8,128)(2,1)S(1)}, bf16[32,256]{1,0:T(8,128)(2,1)S(1)}, u32[]{:S(2)}, u32[]{:S(2)}) collective-permute-start(bf16[32,256]{1,0:T(8,128)(2,1)S(1)} %get-tuple-element.52), channel_id=1, source_target_pairs={{0,4},{4,0},{1,5},{5,1},{2,6},{6,2},{3,7},{7,3},{8,12},{12,8},{9,1... | collective-permute-start | bytes 49160 | tf_op jit(solution)/shard_map/ppermute | solution.py:262
  (2 other events, 3.5 us)

commit v4 on v3

--- a/solution.py
+++ b/solution.py
@@ -11,8 +11,8 @@
 REL = 3
 NZ, NX, NY = 8, 4, 2
 ROWS = 32
-HA = 256
-HB = 512
+HA = 384
+HB = 384
 HC = HID - HA - HB
 PLACE = (0, 12, 24)
 F32 = jnp.float32
@@ -123,6 +123,15 @@
     )(src, cnt, feat, weight, adj, *parts)
 
 
+def finish(b, keep, other, self_term, out):
+    total = self_term[:, :HA] + (keep[...].astype(F32) + other[...].astype(F32))
+    out[:, :HA] = jnp.maximum(total, 0.0).astype(BF16)
+    total = self_term[:, HA:]
+    for z in range(NZ):
+        total += b[z].astype(F32)
+    out[:, HA:] = jnp.maximum(total, 0.0).astype(BF16)
+
+
 def local(kernel, shapes, *args):
     return pl.pallas_call(
         kernel,
@@ -223,6 +232,7 @@
     for f in (src_feat,):
         far.append(lax.ppermute(f, "yh", swap))
     near = lax.ppermute(src_feat, "core", swap)
+    self_term = jnp.dot(tgt_feat, self_weight, preferred_element_type=F32)
     t_own = transform(src_feat, rel_weight)
     t_near = transform(near, rel_weight)
     diag, t_far, t_diag = [], [], []
@@ -260,11 +270,8 @@
     last_b = exchange(joined, "z")
     a_keep, a_send = local(a_meet, [(ROWS, HA)] * 2, s0, s1, s2, s3)
     a_other = lax.ppermute(a_send, "yl", swap)
-    end_a = a_keep.astype(F32) + a_other.astype(F32)
-    end_b = last_b.astype(F32).sum(0)
-    summed = jnp.concatenate([end_a, end_b], axis=1)
-    self_term = jnp.dot(tgt_feat, self_weight, preferred_element_type=F32)
-    return jax.nn.relu(summed + self_term).astype(BF16)
+    (out,) = local(finish, [(ROWS, HID)], last_b, a_keep, a_other, self_term)
+    return out
 
 
 def solution(mesh):

time: 133 us -> 115 us (0.86)
  waiting for transfers between devices: 59.4 us -> 39.4 us
  Pallas kernels: 22.3 us -> 24.1 us
    ppermute x11, waiting for transfers between devices: 22.1 us -> 9.92 us  [along_x(): return lax.ppermute(x, 'x', [(i, (i + d) % NX) for i in range(NX)])]
    ppermute x8, waiting for transfers between devices: 15.3 us -> 8.78 us  [along_z(): return lax.ppermute(x, 'z', [(i, (i + d) % NZ) for i in range(NZ)])]
    pallas_call x10 -> x11, Pallas kernels: 1.57 us -> 3.31 us  [local(): pl.pallas_call(kernel, out_shape=tuple((jax.ShapeDtypeStruct(shape, BF16)...]
    unnamed x16 -> x20, local copies, waits for them, and re-layouts: 3.5 us -> 4.23 us
  transfers between devices with their start and end apart: 26 -> 26, of which waited for: 10 -> 8; matrix products, arithmetic and copies ran while one was open for 0% -> 0% of each run, Pallas kernels for 9% -> 11%
where the time goes in v4:
time: 115 us; the launch traced here: 114 us
  starting transfers between devices  45.6 us (40%)
  waiting for transfers between devices  39.4 us (34%)
  Pallas kernels  24.1 us (21%)
  local copies, waits for them, and re-layouts  4.23 us (4%)
    ppermute x1, waiting for transfers between devices, layer(): far.append(lax.ppermute(f, 'yh', swap))  18.9 us
    ppermute x11, starting transfers between devices, along_x(): return lax.ppermute(x, 'x', [(i, (i + d) % NX) for i in range(NX)])  17.4 us
    ppermute x8, starting transfers between devices, along_z(): return lax.ppermute(x, 'z', [(i, (i + d) % NZ) for i in range(NZ)])  15.9 us
    pallas_call x3, Pallas kernels, transform(): pl.pallas_call(transform_kernel, out_shape=jax.ShapeDtypeStruct((REL * fe...  10.5 us
    pallas_call x1, Pallas kernels, aggregate(): pl.pallas_call(aggregate_kernel, out_shape=tuple((jax.ShapeDtypeStruct(sh...  10.3 us
    ppermute x11, waiting for transfers between devices, along_x(): return lax.ppermute(x, 'x', [(i, (i + d) % NX) for i in range(NX)])  9.92 us
    ppermute x8, waiting for transfers between devices, along_z(): return lax.ppermute(x, 'z', [(i, (i + d) % NZ) for i in range(NZ)])  8.78 us
    all_to_all x1, starting transfers between devices, exchange(): return lax.all_to_all(x, axes, 0, 0, tiled=True)  5.84 us
  transfers between devices with their start and end apart: 26, of which 8 were waited for; matrix products, arithmetic and copies ran while one was open for 0% of the time, Pallas kernels for 11%

profile of v4, /device:TPU:16, one launch (start us, length us, event | category | flops | bytes accessed | tf_op | source)
XLA Modules:
  0.0 114.0 jit_solution(11001226824382059552)
XLA Ops:
  0.0 2.0 %collective-permute-start = (bf16[512,768]{1,0:T(8,128)(2,1)}, bf16[512,768]{1,0:T(8,128)(2,1)S(1)}, u32[]{:S(2)}, u32[]{:S(2)}) collective-permute-start(bf16[512,768]{1,0:T(8,128)(2,1)} %f_ref.1), channel_id=1, source_target_pairs={{0,2},{2,0},{1,3},{3,1},{4,6},{6,4},{5,7},{7,5},{8,10},{10,8},{9,1... | collective-permute-start | bytes 2359304 | tf_op jit(solution)/shard_map/ppermute | solution.py:233
  2.0 18.9 %collective-permute-done.f_ref = bf16[512,768]{1,0:T(8,128)(2,1)S(1)} collective-permute-done((bf16[512,768]{1,0:T(8,128)(2,1)}, bf16[512,768]{1,0:T(8,128)(2,1)S(1)}, u32[]{:S(2)}, u32[]{:S(2)}) %collective-permute-start) | collective-permute-done | bytes 786464 | tf_op jit(solution)/shard_map/ppermute | solution.py:233
  21.0 2.3 %copy-done.2 = bf16[3,768,1024]{2,1,0:T(8,128)(2,1)S(1)} copy-done((bf16[3,768,1024]{2,1,0:T(8,128)(2,1)S(1)}, bf16[3,768,1024]{2,1,0:T(8,128)(2,1)}, u32[]{:S(2)}) %copy-start.2) | copy-done | bytes 4718616
  24.5 3.5 %shard_map.73.refs_0_ = bf16[12,128,1024]{2,1,0:T(8,128)(2,1)S(1)} custom-call(bf16[512,768]{1,0:T(8,128)(2,1)S(1)} %copy-done.4, bf16[3,768,1024]{2,1,0:T(8,128)(2,1)S(1)} %copy-done.2), custom_call_target="tpu_custom_call" | custom-call | flops 2415919104 | bytes 8388608 | tf_op jit(solution)/shard_map/pallas_call | solution.py:40
  28.0 3.5 %shard_map.75.refs_2_ = bf16[12,128,1024]{2,1,0:T(8,128)(2,1)S(1)} custom-call(bf16[512,768]{1,0:T(8,128)(2,1)S(1)} %collective-permute-done.f_ref, bf16[3,768,1024]{2,1,0:T(8,128)(2,1)S(1)} %copy-done.2), custom_call_target="tpu_custom_call" | custom-call | flops 2415919104 | bytes 8388608 | tf_op jit(solution)/shard_map/pallas_call | solution.py:40
  31.5 3.5 %shard_map.74.refs_1_ = bf16[12,128,1024]{2,1,0:T(8,128)(2,1)S(1)} custom-call(bf16[512,768]{1,0:T(8,128)(2,1)S(1)} %collective-permute-done.2.f_ref, bf16[3,768,1024]{2,1,0:T(8,128)(2,1)S(1)} %copy-done.2), custom_call_target="tpu_custom_call" | custom-call | flops 2415919104 | bytes 8388608 | tf_op jit(solution)/shard_map/pallas_call | solution.py:40
  35.1 10.3 %shard_map.76 = (bf16[8,256,384]{2,1,0:T(8,128)(2,1)S(1)}, bf16[128,384]{1,0:T(8,128)(2,1)S(1)}, bf16[128,384]{1,0:T(8,128)(2,1)S(1)}, bf16[2,256,384]{2,1,0:T(8...) custom-call(s32[4,16]{1,0:T(4,128)S(1)} %bitcast.9, ...), custom_call_target="tpu_custom_call" | custom-call | flops 6442450944 | bytes 20971520 | tf_op jit(solution)/shard_map/pallas_call | solution.py:111
  45.4 1.6 %collective-permute-start.3 = (bf16[256,384]{1,0:T(8,128)(2,1)S(1)}, bf16[256,384]{1,0:T(8,128)(2,1)S(1)}, u32[]{:S(2)}, u32[]{:S(2)}) collective-permute-start(bf16[256,384]{1,0:T(8,128)(2,1)S(1)} %get-tuple-element.41), channel_id=1, source_target_pairs={{0,8},{8,16},{16,24},{24,0},{1,9},{9,17},{17,25},{25,1},{2,10},{10... | collective-permute-start | bytes 589832 | tf_op jit(solution)/shard_map/ppermute | solution.py:226
  47.0 1.7 %collective-permute-start.4 = (bf16[256,384]{1,0:T(8,128)(2,1)S(1)}, bf16[256,384]{1,0:T(8,128)(2,1)S(1)}, u32[]{:S(2)}, u32[]{:S(2)}) collective-permute-start(bf16[256,384]{1,0:T(8,128)(2,1)S(1)} %get-tuple-element.42), channel_id=1, source_target_pairs={{0,24},{8,0},{16,8},{24,16},{1,25},{9,1},{17,9},{25,17},{2,26},{10... | collective-permute-start | bytes 589832 | tf_op jit(solution)/shard_map/ppermute | solution.py:226
  48.7 1.3 %collective-permute-start.8 = (bf16[4,256,256]{2,1,0:T(8,128)(2,1)S(1)}, bf16[4,256,256]{2,1,0:T(8,128)(2,1)S(1)}, u32[]{:S(2)}, u32[]{:S(2)}) collective-permute-start(bf16[4,256,256]{2,1,0:T(8,128)(2,1)S(1)} %get-tuple-element.48), channel_id=1, source_target_pairs={{0,4},{4,0},{1,5},{5,1},{2,6},{6,2},{3,7},{7,3},{8,12},{12,8},{9,1... | collective-permute-start | bytes 1572872 | tf_op jit(solution)/shard_map/ppermute | solution.py:254
  50.0 4.0 %collective-permute-done.3.left = bf16[256,384]{1,0:T(8,128)(2,1)S(1)} collective-permute-done((bf16[256,384]{1,0:T(8,128)(2,1)S(1)}, bf16[256,384]{1,0:T(8,128)(2,1)S(1)}, u32[]{:S(2)}, u32[]{:S(2)}) %collective-permute-start.3) | collective-permute-done | bytes 196640 | tf_op jit(solution)/shard_map/ppermute | solution.py:226
  54.2 1.6 %collective-permute-start.5 = (bf16[2,256,384]{2,1,0:T(8,128)(2,1)S(1)}, bf16[2,256,384]{2,1,0:T(8,128)(2,1)S(1)}, u32[]{:S(2)}, u32[]{:S(2)}) collective-permute-start(bf16[2,256,384]{2,1,0:T(8,128)(2,1)S(1)} %get-tuple-element.43), channel_id=1, source_target_pairs={{0,8},{8,16},{16,24},{24,0},{1,9},{9,17},{17,25},{25,1},{2,10},{10... | collective-permute-start | bytes 1179656 | tf_op jit(solution)/shard_map/ppermute | solution.py:226
  55.7 1.8 %collective-permute-start.6 = (bf16[2,256,384]{2,1,0:T(8,128)(2,1)S(1)}, bf16[2,256,384]{2,1,0:T(8,128)(2,1)S(1)}, u32[]{:S(2)}, u32[]{:S(2)}) collective-permute-start(bf16[2,256,384]{2,1,0:T(8,128)(2,1)S(1)} %get-tuple-element.44), channel_id=1, source_target_pairs={{0,24},{8,0},{16,8},{24,16},{1,25},{9,1},{17,9},{25,17},{2,26},{10... | collective-permute-start | bytes 1179656 | tf_op jit(solution)/shard_map/ppermute | solution.py:226
  57.5 1.9 %collective-permute-start.13 = (bf16[128,384]{1,0:T(8,128)(2,1)S(1)}, bf16[128,384]{1,0:T(8,128)(2,1)S(1)}, u32[]{:S(2)}, u32[]{:S(2)}) collective-permute-start(bf16[128,384]{1,0:T(8,128)(2,1)S(1)} %get-tuple-element.57), channel_id=1, source_target_pairs={{0,32},{32,64},{64,96},{96,128},{128,160},{160,192},{192,224},{224... | collective-permute-start | bytes 294920 | tf_op jit(solution)/shard_map/ppermute | solution.py:222
  59.4 3.9 %collective-permute-start.14 = (bf16[128,384]{1,0:T(8,128)(2,1)S(1)}, bf16[128,384]{1,0:T(8,128)(2,1)S(1)}, u32[]{:S(2)}, u32[]{:S(2)}) collective-permute-start(bf16[128,384]{1,0:T(8,128)(2,1)S(1)} %get-tuple-element.58), channel_id=1, source_target_pairs={{0,224},{32,0},{64,32},{96,64},{128,96},{160,128},{192,160},{224,1... | collective-permute-start | bytes 294920 | tf_op jit(solution)/shard_map/ppermute | solution.py:222
  63.3 2.6 %collective-permute-done.13.left = bf16[128,384]{1,0:T(8,128)(2,1)S(1)} collective-permute-done((bf16[128,384]{1,0:T(8,128)(2,1)S(1)}, bf16[128,384]{1,0:T(8,128)(2,1)S(1)}, u32[]{:S(2)}, u32[]{:S(2)}) %collective-permute-start.13) | collective-permute-done | bytes 98336 | tf_op jit(solution)/shard_map/ppermute | solution.py:222
  66.1 3.3 %collective-permute-start.16 = (bf16[256,384]{1,0:T(8,128)(2,1)S(1)}, bf16[256,384]{1,0:T(8,128)(2,1)S(1)}, u32[]{:S(2)}, u32[]{:S(2)}) collective-permute-start(bf16[256,384]{1,0:T(8,128)(2,1)S(1)} %get-tuple-element.60), channel_id=1, source_target_pairs={{0,224},{32,0},{64,32},{96,64},{128,96},{160,128},{192,160},{224,1... | collective-permute-start | bytes 589832 | tf_op jit(solution)/shard_map/ppermute | solution.py:222
  69.5 1.8 %collective-permute-start.10 = (bf16[128,256]{1,0:T(8,128)(2,1)S(1)}, bf16[128,256]{1,0:T(8,128)(2,1)S(1)}, u32[]{:S(2)}, u32[]{:S(2)}) collective-permute-start(bf16[128,256]{1,0:T(8,128)(2,1)S(1)} %get-tuple-element.53), channel_id=1, source_target_pairs={{0,24},{8,0},{16,8},{24,16},{1,25},{9,1},{17,9},{25,17},{2,26},{10... | collective-permute-start | bytes 196616 | tf_op jit(solution)/shard_map/ppermute | solution.py:226
  71.8 1.4 %collective-permute-start.7 = (bf16[256,384]{1,0:T(8,128)(2,1)S(1)}, bf16[256,384]{1,0:T(8,128)(2,1)S(1)}, u32[]{:S(2)}, u32[]{:S(2)}) collective-permute-start(bf16[256,384]{1,0:T(8,128)(2,1)S(1)} %get-tuple-element.46), channel_id=1, source_target_pairs={{0,4},{4,0},{1,5},{5,1},{2,6},{6,2},{3,7},{7,3},{8,12},{12,8},{9,1... | collective-permute-start | bytes 589832 | tf_op jit(solution)/shard_map/ppermute | solution.py:264
  74.0 2.8 %collective-permute-start.17 = (bf16[256,384]{1,0:T(8,128)(2,1)}, bf16[256,384]{1,0:T(8,128)(2,1)}, u32[]{:S(2)}, u32[]{:S(2)}) collective-permute-start(bf16[256,384]{1,0:T(8,128)(2,1)} %get-tuple-element.61), channel_id=1, source_target_pairs={{0,32},{32,64},{64,96},{96,128},{128,160},{160,192},{192,224},{224... | collective-permute-start | bytes 589832 | tf_op jit(solution)/shard_map/ppermute | solution.py:222
  77.6 3.0 %collective-permute-start.12 = (bf16[256,256]{1,0:T(8,128)(2,1)S(1)}, bf16[256,256]{1,0:T(8,128)(2,1)S(1)}, u32[]{:S(2)}, u32[]{:S(2)}) collective-permute-start(bf16[256,256]{1,0:T(8,128)(2,1)S(1)} %get-tuple-element.55), channel_id=1, source_target_pairs={{0,24},{8,0},{16,8},{24,16},{1,25},{9,1},{17,9},{25,17},{2,26},{10... | collective-permute-start | bytes 393224 | tf_op jit(solution)/shard_map/ppermute | solution.py:226
  80.6 2.9 %collective-permute-done.11.left = bf16[256,256]{1,0:T(8,128)(2,1)S(1)} collective-permute-done((bf16[256,256]{1,0:T(8,128)(2,1)S(1)}, bf16[256,256]{1,0:T(8,128)(2,1)S(1)}, u32[]{:S(2)}, u32[]{:S(2)}) %collective-permute-start.11) | collective-permute-done | bytes 131104 | tf_op jit(solution)/shard_map/ppermute | solution.py:226
  84.3 5.8 %all-to-all-start = ((bf16[8,32,640]{2,1,0:T(8,128)(2,1)}), bf16[8,32,640]{2,1,0:T(8,128)(2,1)S(1)}, u32[]{:S(2)}, u32[]{:S(2)}) async-start(bf16[8,32,640]{2,1,0:T(8,128)(2,1)} %copy-done.1), calls=%async_computation | async-start | bytes 655360 | tf_op jit(solution)/shard_map/all_to_all | solution.py:218
  91.3 2.1 %collective-permute-start.19 = (bf16[256,384]{1,0:T(8,128)(2,1)S(1)}, bf16[256,384]{1,0:T(8,128)(2,1)S(1)}, u32[]{:S(2)}, u32[]{:S(2)}) collective-permute-start(bf16[256,384]{1,0:T(8,128)(2,1)S(1)} %get-tuple-element.63), channel_id=1, source_target_pairs={{0,32},{32,64},{64,96},{96,128},{128,160},{160,192},{192,224},{224... | collective-permute-start | bytes 589832 | tf_op jit(solution)/shard_map/ppermute | solution.py:222
  93.4 1.3 %collective-permute-start.20 = (bf16[256,384]{1,0:T(8,128)(2,1)S(1)}, bf16[256,384]{1,0:T(8,128)(2,1)S(1)}, u32[]{:S(2)}, u32[]{:S(2)}) collective-permute-start(bf16[256,384]{1,0:T(8,128)(2,1)S(1)} %get-tuple-element.64), channel_id=1, source_target_pairs={{0,224},{32,0},{64,32},{96,64},{128,96},{160,128},{192,160},{224,1... | collective-permute-start | bytes 589832 | tf_op jit(solution)/shard_map/ppermute | solution.py:222
  94.7 6.2 %collective-permute-done.19.left = bf16[256,384]{1,0:T(8,128)(2,1)S(1)} collective-permute-done((bf16[256,384]{1,0:T(8,128)(2,1)S(1)}, bf16[256,384]{1,0:T(8,128)(2,1)S(1)}, u32[]{:S(2)}, u32[]{:S(2)}) %collective-permute-start.19) | collective-permute-done | bytes 196640 | tf_op jit(solution)/shard_map/ppermute | solution.py:222
  101.0 1.2 %collective-permute-start.21 = (bf16[2,32,384]{2,1,0:T(8,128)(2,1)S(1)}, bf16[2,32,384]{2,1,0:T(8,128)(2,1)S(1)}, u32[]{:S(2)}, u32[]{:S(2)}) collective-permute-start(bf16[2,32,384]{2,1,0:T(8,128)(2,1)S(1)} %get-tuple-element.66), channel_id=1, source_target_pairs={{0,8},{8,16},{16,24},{24,0},{1,9},{9,17},{17,25},{25,1},{2,10},{10... | collective-permute-start | bytes 147464 | tf_op jit(solution)/shard_map/ppermute | solution.py:226
  102.2 3.0 %collective-permute-start.22 = (bf16[2,32,384]{2,1,0:T(8,128)(2,1)S(1)}, bf16[2,32,384]{2,1,0:T(8,128)(2,1)S(1)}, u32[]{:S(2)}, u32[]{:S(2)}) collective-permute-start(bf16[2,32,384]{2,1,0:T(8,128)(2,1)S(1)} %get-tuple-element.67), channel_id=1, source_target_pairs={{0,16},{8,24},{16,0},{24,8},{1,17},{9,25},{17,1},{25,9},{2,18},{10... | collective-permute-start | bytes 147464 | tf_op jit(solution)/shard_map/ppermute | solution.py:226
  106.4 1.5 %collective-permute-done.22.s2 = bf16[2,32,384]{2,1,0:T(8,128)(2,1)S(1)} collective-permute-done((bf16[2,32,384]{2,1,0:T(8,128)(2,1)S(1)}, bf16[2,32,384]{2,1,0:T(8,128)(2,1)S(1)}, u32[]{:S(2)}, u32[]{:S(2)}) %collective-permute-start.22) | collective-permute-done | bytes 49184 | tf_op jit(solution)/shard_map/ppermute | solution.py:226
  107.8 1.5 %collective-permute-done.23.s3 = bf16[2,32,384]{2,1,0:T(8,128)(2,1)S(1)} collective-permute-done((bf16[2,32,384]{2,1,0:T(8,128)(2,1)S(1)}, bf16[2,32,384]{2,1,0:T(8,128)(2,1)S(1)}, u32[]{:S(2)}, u32[]{:S(2)}) %collective-permute-start.23) | collective-permute-done | bytes 49184 | tf_op jit(solution)/shard_map/ppermute | solution.py:226
  109.3 1.8 %collective-permute-start.24 = (bf16[32,384]{1,0:T(8,128)(2,1)S(1)}, bf16[32,384]{1,0:T(8,128)(2,1)S(1)}, u32[]{:S(2)}, u32[]{:S(2)}) collective-permute-start(bf16[32,384]{1,0:T(8,128)(2,1)S(1)} %get-tuple-element.70), channel_id=1, source_target_pairs={{0,4},{4,0},{1,5},{5,1},{2,6},{6,2},{3,7},{7,3},{8,12},{12,8},{9,1... | collective-permute-start | bytes 73736 | tf_op jit(solution)/shard_map/ppermute | solution.py:272
  111.5 1.8 %collective-permute-done.24.other = bf16[32,384]{1,0:T(8,128)(2,1)S(1)} collective-permute-done((bf16[32,384]{1,0:T(8,128)(2,1)S(1)}, bf16[32,384]{1,0:T(8,128)(2,1)S(1)}, u32[]{:S(2)}, u32[]{:S(2)}) %collective-permute-start.24) | collective-permute-done | bytes 24608 | tf_op jit(solution)/shard_map/ppermute | solution.py:272
  (57 shorter events, 7.9 us)
Async XLA Ops:
  0.0 111.1 %copy-start = (bf16[768,1024]{1,0:T(8,128)(2,1)S(1)}, bf16[768,1024]{1,0:T(8,128)(2,1)}, u32[]{:S(2)}) copy-start(bf16[768,1024]{1,0:T(8,128)(2,1)} %param.10) | copy-start | bytes 4718596
  0.0 21.0 %collective-permute-start = (bf16[512,768]{1,0:T(8,128)(2,1)}, bf16[512,768]{1,0:T(8,128)(2,1)S(1)}, u32[]{:S(2)}, u32[]{:S(2)}) collective-permute-start(bf16[512,768]{1,0:T(8,128)(2,1)} %f_ref.1), channel_id=1, source_target_pairs={{0,2},{2,0},{1,3},{3,1},{4,6},{6,4},{5,7},{7,5},{8,10},{10,8},{9,1... | collective-permute-start | bytes 2359304 | tf_op jit(solution)/shard_map/ppermute | solution.py:233
  2.0 29.5 %collective-permute-start.2 = (bf16[512,768]{1,0:T(8,128)(2,1)}, bf16[512,768]{1,0:T(8,128)(2,1)S(1)}, u32[]{:S(2)}, u32[]{:S(2)}) collective-permute-start(bf16[512,768]{1,0:T(8,128)(2,1)} %f_ref.1), channel_id=1, source_target_pairs={{0,1},{1,0},{2,3},{3,2},{4,5},{5,4},{6,7},{7,6},{8,9},{9,8},{10,11... | collective-permute-start | bytes 2359304 | tf_op jit(solution)/shard_map/ppermute | solution.py:234
  21.0 14.0 %collective-permute-start.1 = (bf16[512,768]{1,0:T(8,128)(2,1)S(1)}, bf16[512,768]{1,0:T(8,128)(2,1)S(1)}, u32[]{:S(2)}, u32[]{:S(2)}) collective-permute-start(bf16[512,768]{1,0:T(8,128)(2,1)S(1)} %collective-permute-done.f_ref), channel_id=1, source_target_pairs={{0,1},{1,0},{2,3},{3,2},{4,5},{5,4},{6,7},{7,6},{8,9},{9,8},{10,11... | collective-permute-start | bytes 2359304 | tf_op jit(solution)/shard_map/ppermute | solution.py:240
  28.0 7.1 %slice-start = ((s8[4718592]{0:T(1024)(128)(4,1)}), s8[4194304]{0:T(1024)(128)(4,1)S(1)}, s32[]{:S(2)}) async-start(s8[4718592]{0:T(1024)(128)(4,1)} %bitcast.6), calls=%async_computation.1 | async-start | bytes 8388608
  31.5 3.6 %slice-start.1 = ((s8[4718592]{0:T(1024)(128)(4,1)}), s8[524288]{0:T(1024)(128)(4,1)S(1)}, s32[]{:S(2)}) async-start(s8[4718592]{0:T(1024)(128)(4,1)} %bitcast.6), calls=%async_computation.2 | async-start | bytes 1048576
  31.5 3.6 %copy-start.3 = (bf16[1,16,4,128,128]{4,3,2,1,0:T(8,128)(2,1)S(1)}, bf16[1,16,4,128,128]{4,3,2,1,0:T(8,128)(2,1)}, u32[]{:S(2)}) copy-start(bf16[1,16,4,128,128]{4,3,2,1,0:T(8,128)(2,1)} %param.11) | copy-start | bytes 6291460
  31.5 3.6 %copy-start.5 = (s32[1,16,4]{1,2,0:T(4,128)S(1)}, s32[1,16,4]{1,2,0:T(4,128)}, u32[]{:S(2)}) copy-start(s32[1,16,4]{1,2,0:T(4,128)} %param.12) | copy-start | bytes 772
  45.4 8.6 %collective-permute-start.3 = (bf16[256,384]{1,0:T(8,128)(2,1)S(1)}, bf16[256,384]{1,0:T(8,128)(2,1)S(1)}, u32[]{:S(2)}, u32[]{:S(2)}) collective-permute-start(bf16[256,384]{1,0:T(8,128)(2,1)S(1)} %get-tuple-element.41), channel_id=1, source_target_pairs={{0,8},{8,16},{16,24},{24,0},{1,9},{9,17},{17,25},{25,1},{2,10},{10... | collective-permute-start | bytes 589832 | tf_op jit(solution)/shard_map/ppermute | solution.py:226
  47.0 7.0 %collective-permute-start.4 = (bf16[256,384]{1,0:T(8,128)(2,1)S(1)}, bf16[256,384]{1,0:T(8,128)(2,1)S(1)}, u32[]{:S(2)}, u32[]{:S(2)}) collective-permute-start(bf16[256,384]{1,0:T(8,128)(2,1)S(1)} %get-tuple-element.42), channel_id=1, source_target_pairs={{0,24},{8,0},{16,8},{24,16},{1,25},{9,1},{17,9},{25,17},{2,26},{10... | collective-permute-start | bytes 589832 | tf_op jit(solution)/shard_map/ppermute | solution.py:226
  48.7 20.6 %collective-permute-start.8 = (bf16[4,256,256]{2,1,0:T(8,128)(2,1)S(1)}, bf16[4,256,256]{2,1,0:T(8,128)(2,1)S(1)}, u32[]{:S(2)}, u32[]{:S(2)}) collective-permute-start(bf16[4,256,256]{2,1,0:T(8,128)(2,1)S(1)} %get-tuple-element.48), channel_id=1, source_target_pairs={{0,4},{4,0},{1,5},{5,1},{2,6},{6,2},{3,7},{7,3},{8,12},{12,8},{9,1... | collective-permute-start | bytes 1572872 | tf_op jit(solution)/shard_map/ppermute | solution.py:254
  54.2 17.2 %collective-permute-start.5 = (bf16[2,256,384]{2,1,0:T(8,128)(2,1)S(1)}, bf16[2,256,384]{2,1,0:T(8,128)(2,1)S(1)}, u32[]{:S(2)}, u32[]{:S(2)}) collective-permute-start(bf16[2,256,384]{2,1,0:T(8,128)(2,1)S(1)} %get-tuple-element.43), channel_id=1, source_target_pairs={{0,8},{8,16},{16,24},{24,0},{1,9},{9,17},{17,25},{25,1},{2,10},{10... | collective-permute-start | bytes 1179656 | tf_op jit(solution)/shard_map/ppermute | solution.py:226
  55.7 15.9 %collective-permute-start.6 = (bf16[2,256,384]{2,1,0:T(8,128)(2,1)S(1)}, bf16[2,256,384]{2,1,0:T(8,128)(2,1)S(1)}, u32[]{:S(2)}, u32[]{:S(2)}) collective-permute-start(bf16[2,256,384]{2,1,0:T(8,128)(2,1)S(1)} %get-tuple-element.44), channel_id=1, source_target_pairs={{0,24},{8,0},{16,8},{24,16},{1,25},{9,1},{17,9},{25,17},{2,26},{10... | collective-permute-start | bytes 1179656 | tf_op jit(solution)/shard_map/ppermute | solution.py:226
  57.5 8.4 %collective-permute-start.13 = (bf16[128,384]{1,0:T(8,128)(2,1)S(1)}, bf16[128,384]{1,0:T(8,128)(2,1)S(1)}, u32[]{:S(2)}, u32[]{:S(2)}) collective-permute-start(bf16[128,384]{1,0:T(8,128)(2,1)S(1)} %get-tuple-element.57), channel_id=1, source_target_pairs={{0,32},{32,64},{64,96},{96,128},{128,160},{160,192},{192,224},{224... | collective-permute-start | bytes 294920 | tf_op jit(solution)/shard_map/ppermute | solution.py:222
  59.4 6.5 %collective-permute-start.14 = (bf16[128,384]{1,0:T(8,128)(2,1)S(1)}, bf16[128,384]{1,0:T(8,128)(2,1)S(1)}, u32[]{:S(2)}, u32[]{:S(2)}) collective-permute-start(bf16[128,384]{1,0:T(8,128)(2,1)S(1)} %get-tuple-element.58), channel_id=1, source_target_pairs={{0,224},{32,0},{64,32},{96,64},{128,96},{160,128},{192,160},{224,1... | collective-permute-start | bytes 294920 | tf_op jit(solution)/shard_map/ppermute | solution.py:222
  66.0 7.2 %collective-permute-start.15 = (bf16[256,384]{1,0:T(8,128)(2,1)S(1)}, bf16[256,384]{1,0:T(8,128)(2,1)S(1)}, u32[]{:S(2)}, u32[]{:S(2)}) collective-permute-start(bf16[256,384]{1,0:T(8,128)(2,1)S(1)} %get-tuple-element.59), channel_id=1, source_target_pairs={{0,32},{32,64},{64,96},{96,128},{128,160},{160,192},{192,224},{224... | collective-permute-start | bytes 589832 | tf_op jit(solution)/shard_map/ppermute | solution.py:222
  66.1 7.1 %collective-permute-start.16 = (bf16[256,384]{1,0:T(8,128)(2,1)S(1)}, bf16[256,384]{1,0:T(8,128)(2,1)S(1)}, u32[]{:S(2)}, u32[]{:S(2)}) collective-permute-start(bf16[256,384]{1,0:T(8,128)(2,1)S(1)} %get-tuple-element.60), channel_id=1, source_target_pairs={{0,224},{32,0},{64,32},{96,64},{128,96},{160,128},{192,160},{224,1... | collective-permute-start | bytes 589832 | tf_op jit(solution)/shard_map/ppermute | solution.py:222
  69.5 7.7 %collective-permute-start.10 = (bf16[128,256]{1,0:T(8,128)(2,1)S(1)}, bf16[128,256]{1,0:T(8,128)(2,1)S(1)}, u32[]{:S(2)}, u32[]{:S(2)}) collective-permute-start(bf16[128,256]{1,0:T(8,128)(2,1)S(1)} %get-tuple-element.53), channel_id=1, source_target_pairs={{0,24},{8,0},{16,8},{24,16},{1,25},{9,1},{17,9},{25,17},{2,26},{10... | collective-permute-start | bytes 196616 | tf_op jit(solution)/shard_map/ppermute | solution.py:226
  71.3 5.9 %collective-permute-start.9 = (bf16[128,256]{1,0:T(8,128)(2,1)S(1)}, bf16[128,256]{1,0:T(8,128)(2,1)S(1)}, u32[]{:S(2)}, u32[]{:S(2)}) collective-permute-start(bf16[128,256]{1,0:T(8,128)(2,1)S(1)} %get-tuple-element.52), channel_id=1, source_target_pairs={{0,8},{8,16},{16,24},{24,0},{1,9},{9,17},{17,25},{25,1},{2,10},{10... | collective-permute-start | bytes 196616 | tf_op jit(solution)/shard_map/ppermute | solution.py:226
  71.8 11.7 %collective-permute-start.7 = (bf16[256,384]{1,0:T(8,128)(2,1)S(1)}, bf16[256,384]{1,0:T(8,128)(2,1)S(1)}, u32[]{:S(2)}, u32[]{:S(2)}) collective-permute-start(bf16[256,384]{1,0:T(8,128)(2,1)S(1)} %get-tuple-element.46), channel_id=1, source_target_pairs={{0,4},{4,0},{1,5},{5,1},{2,6},{6,2},{3,7},{7,3},{8,12},{12,8},{9,1... | collective-permute-start | bytes 589832 | tf_op jit(solution)/shard_map/ppermute | solution.py:264
  74.0 16.2 %collective-permute-start.17 = (bf16[256,384]{1,0:T(8,128)(2,1)}, bf16[256,384]{1,0:T(8,128)(2,1)}, u32[]{:S(2)}, u32[]{:S(2)}) collective-permute-start(bf16[256,384]{1,0:T(8,128)(2,1)} %get-tuple-element.61), channel_id=1, source_target_pairs={{0,32},{32,64},{64,96},{96,128},{128,160},{160,192},{192,224},{224... | collective-permute-start | bytes 589832 | tf_op jit(solution)/shard_map/ppermute | solution.py:222
  76.8 13.4 %collective-permute-start.18 = (bf16[256,384]{1,0:T(8,128)(2,1)}, bf16[256,384]{1,0:T(8,128)(2,1)}, u32[]{:S(2)}, u32[]{:S(2)}) collective-permute-start(bf16[256,384]{1,0:T(8,128)(2,1)} %get-tuple-element.62), channel_id=1, source_target_pairs={{0,224},{32,0},{64,32},{96,64},{128,96},{160,128},{192,160},{224,1... | collective-permute-start | bytes 589832 | tf_op jit(solution)/shard_map/ppermute | solution.py:222
  77.3 6.3 %collective-permute-start.11 = (bf16[256,256]{1,0:T(8,128)(2,1)S(1)}, bf16[256,256]{1,0:T(8,128)(2,1)S(1)}, u32[]{:S(2)}, u32[]{:S(2)}) collective-permute-start(bf16[256,256]{1,0:T(8,128)(2,1)S(1)} %get-tuple-element.54), channel_id=1, source_target_pairs={{0,8},{8,16},{16,24},{24,0},{1,9},{9,17},{17,25},{25,1},{2,10},{10... | collective-permute-start | bytes 393224 | tf_op jit(solution)/shard_map/ppermute | solution.py:226
  77.6 5.9 %collective-permute-start.12 = (bf16[256,256]{1,0:T(8,128)(2,1)S(1)}, bf16[256,256]{1,0:T(8,128)(2,1)S(1)}, u32[]{:S(2)}, u32[]{:S(2)}) collective-permute-start(bf16[256,256]{1,0:T(8,128)(2,1)S(1)} %get-tuple-element.55), channel_id=1, source_target_pairs={{0,24},{8,0},{16,8},{24,16},{1,25},{9,1},{17,9},{25,17},{2,26},{10... | collective-permute-start | bytes 393224 | tf_op jit(solution)/shard_map/ppermute | solution.py:226
  84.3 28.9 %all-to-all-start = ((bf16[8,32,640]{2,1,0:T(8,128)(2,1)}), bf16[8,32,640]{2,1,0:T(8,128)(2,1)S(1)}, u32[]{:S(2)}, u32[]{:S(2)}) async-start(bf16[8,32,640]{2,1,0:T(8,128)(2,1)} %copy-done.1), calls=%async_computation | async-start | bytes 655360 | tf_op jit(solution)/shard_map/all_to_all | solution.py:218
  90.2 20.9 %copy-start.7 = (bf16[32,768]{1,0:T(8,128)(2,1)S(1)}, bf16[32,768]{1,0:T(8,128)(2,1)}, u32[]{:S(2)}) copy-start(bf16[32,768]{1,0:T(8,128)(2,1)} %param.8) | copy-start | bytes 147460
  91.3 9.6 %collective-permute-start.19 = (bf16[256,384]{1,0:T(8,128)(2,1)S(1)}, bf16[256,384]{1,0:T(8,128)(2,1)S(1)}, u32[]{:S(2)}, u32[]{:S(2)}) collective-permute-start(bf16[256,384]{1,0:T(8,128)(2,1)S(1)} %get-tuple-element.63), channel_id=1, source_target_pairs={{0,32},{32,64},{64,96},{96,128},{128,160},{160,192},{192,224},{224... | collective-permute-start | bytes 589832 | tf_op jit(solution)/shard_map/ppermute | solution.py:222
  93.4 7.5 %collective-permute-start.20 = (bf16[256,384]{1,0:T(8,128)(2,1)S(1)}, bf16[256,384]{1,0:T(8,128)(2,1)S(1)}, u32[]{:S(2)}, u32[]{:S(2)}) collective-permute-start(bf16[256,384]{1,0:T(8,128)(2,1)S(1)} %get-tuple-element.64), channel_id=1, source_target_pairs={{0,224},{32,0},{64,32},{96,64},{128,96},{160,128},{192,160},{224,1... | collective-permute-start | bytes 589832 | tf_op jit(solution)/shard_map/ppermute | solution.py:222
  101.0 5.4 %collective-permute-start.21 = (bf16[2,32,384]{2,1,0:T(8,128)(2,1)S(1)}, bf16[2,32,384]{2,1,0:T(8,128)(2,1)S(1)}, u32[]{:S(2)}, u32[]{:S(2)}) collective-permute-start(bf16[2,32,384]{2,1,0:T(8,128)(2,1)S(1)} %get-tuple-element.66), channel_id=1, source_target_pairs={{0,8},{8,16},{16,24},{24,0},{1,9},{9,17},{17,25},{25,1},{2,10},{10... | collective-permute-start | bytes 147464 | tf_op jit(solution)/shard_map/ppermute | solution.py:226
  102.2 5.6 %collective-permute-start.22 = (bf16[2,32,384]{2,1,0:T(8,128)(2,1)S(1)}, bf16[2,32,384]{2,1,0:T(8,128)(2,1)S(1)}, u32[]{:S(2)}, u32[]{:S(2)}) collective-permute-start(bf16[2,32,384]{2,1,0:T(8,128)(2,1)S(1)} %get-tuple-element.67), channel_id=1, source_target_pairs={{0,16},{8,24},{16,0},{24,8},{1,17},{9,25},{17,1},{25,9},{2,18},{10... | collective-permute-start | bytes 147464 | tf_op jit(solution)/shard_map/ppermute | solution.py:226
  105.2 4.1 %collective-permute-start.23 = (bf16[2,32,384]{2,1,0:T(8,128)(2,1)S(1)}, bf16[2,32,384]{2,1,0:T(8,128)(2,1)S(1)}, u32[]{:S(2)}, u32[]{:S(2)}) collective-permute-start(bf16[2,32,384]{2,1,0:T(8,128)(2,1)S(1)} %get-tuple-element.68), channel_id=1, source_target_pairs={{0,24},{8,0},{16,8},{24,16},{1,25},{9,1},{17,9},{25,17},{2,26},{10... | collective-permute-start | bytes 147464 | tf_op jit(solution)/shard_map/ppermute | solution.py:226
  109.3 3.9 %collective-permute-start.24 = (bf16[32,384]{1,0:T(8,128)(2,1)S(1)}, bf16[32,384]{1,0:T(8,128)(2,1)S(1)}, u32[]{:S(2)}, u32[]{:S(2)}) collective-permute-start(bf16[32,384]{1,0:T(8,128)(2,1)S(1)} %get-tuple-element.70), channel_id=1, source_target_pairs={{0,4},{4,0},{1,5},{5,1},{2,6},{6,2},{3,7},{7,3},{8,12},{12,8},{9,1... | collective-permute-start | bytes 73736 | tf_op jit(solution)/shard_map/ppermute | solution.py:272
  (4 other events, 7.8 us)

commit v5 on v4

--- a/solution.py
+++ b/solution.py
@@ -22,14 +22,14 @@
 
 
 def transform_rows(f_ref, w_ref, t_ref, base):
-    def step(i, _):
-        h = i // REL
-        r = i - h * REL
-        y = jnp.dot(f_ref[pl.ds(h * 2 * BLK, 2 * BLK), :], w_ref[r], preferred_element_type=F32)
-        t_ref[pl.ds(base + i * 2, 2)] = y.astype(BF16).reshape(2, BLK, HID)
+    n = f_ref.shape[0] // BLK
+
+    def step(r, _):
+        y = jnp.dot(f_ref[...], w_ref[r], preferred_element_type=F32)
+        t_ref[pl.ds(base + r * n, n)] = y.astype(BF16).reshape(n, BLK, HID)
         return 0
 
-    lax.fori_loop(0, f_ref.shape[0] // (2 * BLK) * REL, step, 0)
+    lax.fori_loop(0, REL, step, 0)
 
 
 def transform_kernel(f_ref, w_ref, t_ref):
@@ -55,10 +55,10 @@
         v = src_ref[k, t]
         r = lax.shift_right_logical(v, 4)
         j = lax.bitwise_and(v, 15)
-        half = lax.bitwise_xor(lax.shift_right_logical(j, 1), me * 2)
+        q = lax.bitwise_xor(lax.shift_right_logical(j, 2), me)
         w = adj_ref[t, k]
         weights.append(jnp.where(k < cnt_ref[0, t], w, jnp.zeros_like(w)))
-        picked.append(t_ref[half * 6 + r * 2 + lax.bitwise_and(j, 1)])
+        picked.append(t_ref[q * 12 + r * 4 + lax.bitwise_and(j, 3)])
     return jnp.dot(
         jnp.concatenate(weights, axis=1), jnp.concatenate(picked, axis=0), preferred_element_type=F32
     ).astype(BF16)
@@ -66,7 +66,7 @@
 
 def aggregate_kernel(src_ref, cnt_ref, f_ref, w_ref, adj_ref, *refs):
     n = len(PLACE)
-    parts, (a_ref, low, high), b_refs = refs[:n], refs[n : n + 3], refs[n + 3 : -5]
+    parts, a_refs, b_refs = refs[:n], refs[n : n + NZ + 1], refs[n + NZ + 1 : -5]
     c_refs, (both, t_ref, sems) = refs[-5:-3], refs[-3:]
     copies = []
     for q, part in enumerate(parts):
@@ -84,11 +84,14 @@
         z = lax.bitwise_and(z0 + d, NZ - 1)
         for odd in range(2):
             got = weighted_sum(z * 2 + odd, src_ref, cnt_ref, me, adj_ref, t_ref)
-            a_ref[d, odd * BLK : (odd + 1) * BLK, :] = got[:, :HA]
-
-            @pl.when(d == NZ // 2)
-            def _():
-                (low, high)[odd][...] = got[:, :HA]
+            for away in range(NZ):
+
+                @pl.when(d == away)
+                def _():
+                    if away == NZ // 2:
+                        a_refs[away + odd * (NZ // 2)][...] = got[:, :HA]
+                    else:
+                        a_refs[away][odd * BLK : (odd + 1) * BLK, :] = got[:, :HA]
 
             both[odd * BLK : (odd + 1) * BLK, :] = got[:, HA:]
         at = pl.ds(pl.multiple_of(z * ROWS, ROWS), ROWS)
@@ -107,7 +110,8 @@
 
 
 def aggregate(src, cnt, feat, weight, adj, parts):
-    shapes = [(NZ, 256, HA), (BLK, HA), (BLK, HA)] + [(NY, 256, HB)] * 3 + [(256, HB)] * 2 + [(NX, 256, HC)] * 2
+    shapes = [(BLK if away in (NZ // 2, NZ) else 256, HA) for away in range(NZ + 1)]
+    shapes += [(NY, 256, HB)] * 3 + [(256, HB)] * 2 + [(NX, 256, HC)] * 2
     return pl.pallas_call(
         aggregate_kernel,
         out_shape=tuple(jax.ShapeDtypeStruct(shape, BF16) for shape in shapes),
@@ -149,19 +153,15 @@
     return total.astype(BF16)
 
 
-def a_relay(away):
-    def kernel(a, left, right, up, down):
-        if left.shape[0] < up.shape[0]:
-            half = left.shape[0]
-            up[:half] = add(a[away, :half], left[...])
-            up[half:] = a[away, half:]
-            down[:half] = a[NZ - away, :half]
-            down[half:] = add(a[NZ - away, half:], right[...])
-        else:
-            up[...] = add(a[away], left[...])
-            down[...] = add(a[NZ - away], right[...])
-
-    return kernel
+def a_relay(a_up, a_down, left, right, up, down):
+    half = left.shape[0]
+    up[:half] = add(a_up[:half], left[...])
+    if half < up.shape[0]:
+        up[half:] = a_up[half:]
+        down[:half] = a_down[:half]
+        down[half:] = add(a_down[half:], right[...])
+    else:
+        down[...] = add(a_down[...], right[...])
 
 
 def a_sum(a, left, right, *outs):
@@ -170,7 +170,7 @@
         for dy in range(NY):
             to = lax.bitwise_and(x0 + dx, NX - 1) * NY + lax.bitwise_xor(y0, dy)
             rows = pl.ds(pl.multiple_of(to * ROWS, ROWS), ROWS)
-            out[dy] = add(a[0, rows, :], left[rows, :], right[rows, :])
+            out[dy] = add(a[rows, :], left[rows, :], right[rows, :])
 
 
 def a_meet(s0, s1, s2, s3, keep, send):
@@ -241,7 +241,7 @@
         t_far.append(transform(f, rel_weight))
     for f in diag[:-1]:
         t_diag.append(transform(f, rel_weight))
-    a, low, high, b0, b1, b3, b20, b21, c0, c1 = aggregate(
+    got = aggregate(
         jnp.transpose(adj_source[0]),
         adj_count,
         diag[-1],
@@ -249,11 +249,12 @@
         adj_weight[0],
         [t_own, t_near] + t_far + t_diag,
     )
-    a_left, a_right = along_z(low, 1), along_z(high, -1)
+    a, (b0, b1, b3, b20, b21, c0, c1) = got[: NZ + 1], got[NZ + 1 :]
+    a_left, a_right = along_z(a[NZ // 2], 1), along_z(a[NZ], -1)
     b_left, b_right = along_x(b20, 1), along_x(b21, -1)
     c_other = lax.ppermute(c1, "yl", swap)
     for away in (3, 2, 1):
-        up, down = local(a_relay(away), [(256, HA)] * 2, a, a_left, a_right)
+        up, down = local(a_relay, [(256, HA)] * 2, a[away], a[NZ - away], a_left, a_right)
         a_left, a_right = along_z(up, 1), along_z(down, -1)
     b_up, b_down = local(b_relay, [(NY, 256, HB)] * 2, b1, b3, b_left, b_right)
     b_left, b_right = along_x(b_up, 1), along_x(b_down, -1)
@@ -264,8 +265,9 @@
     b_other = lax.ppermute(b_send, "yl", swap)
     c_up, c_down = local(c_relay, [(256, HC)] * 2, c_up, c_down, c_left, c_right)
     c_left, c_right = along_x(c_up, 1), along_x(c_down, -1)
-    s0, s1, s2, s3 = local(a_sum, [(NY, ROWS, HA)] * NX, a, a_left, a_right)
-    s1, s2, s3 = along_x(s1, 1), along_x(s2, 2), along_x(s3, 3)
+    s0, s1, s2, s3 = local(a_sum, [(NY, ROWS, HA)] * NX, a[0], a_left, a_right)
+    s2 = along_x(s2, 2)
+    s1, s3 = along_x(s1, 1), along_x(s3, 3)
     (joined,) = local(join, [(NZ, ROWS, HB + HC)], b_keep, b_other, c_own, c_left, c_right)
     last_b = exchange(joined, "z")
     a_keep, a_send = local(a_meet, [(ROWS, HA)] * 2, s0, s1, s2, s3)

time: 115 us -> 112 us (0.974)
  Pallas kernels: 24.1 us -> 21.5 us
  waiting for transfers between devices: 39.4 us -> 41 us
    pallas_call x3, Pallas kernels: 10.5 us -> 8.85 us  [transform(): pl.pallas_call(transform_kernel, out_shape=jax.ShapeDtypeStruct((REL * fe...]
    unnamed x20 -> x16, local copies, waits for them, and re-layouts: 4.23 us -> 3.5 us
  transfers between devices with their start and end apart: 26 -> 26, of which waited for: 8 -> 9; matrix products, arithmetic and copies ran while one was open for 0% -> 0% of each run, Pallas kernels for 11% -> 9%
where the time goes in v5:
time: 112 us
  starting transfers between devices  45.5 us (41%)
  waiting for transfers between devices  41 us (37%)
  Pallas kernels  21.5 us (19%)
  local copies, waits for them, and re-layouts  3.5 us (3%)
    ppermute x1, waiting for transfers between devices, layer(): far.append(lax.ppermute(f, 'yh', swap))  18.9 us
    ppermute x11, starting transfers between devices, along_x(): return lax.ppermute(x, 'x', [(i, (i + d) % NX) for i in range(NX)])  17.6 us
    ppermute x8, starting transfers between devices, along_z(): return lax.ppermute(x, 'z', [(i, (i + d) % NZ) for i in range(NZ)])  15.9 us
    ppermute x11, waiting for transfers between devices, along_x(): return lax.ppermute(x, 'x', [(i, (i + d) % NX) for i in range(NX)])  10.4 us
    pallas_call x1, Pallas kernels, aggregate(): pl.pallas_call(aggregate_kernel, out_shape=tuple((jax.ShapeDtypeStruct(sh...  10.3 us
    ppermute x8, waiting for transfers between devices, along_z(): return lax.ppermute(x, 'z', [(i, (i + d) % NZ) for i in range(NZ)])  9.53 us
    pallas_call x3, Pallas kernels, transform(): pl.pallas_call(transform_kernel, out_shape=jax.ShapeDtypeStruct((REL * fe...  8.85 us
    all_to_all x1, starting transfers between devices, exchange(): return lax.all_to_all(x, axes, 0, 0, tiled=True)  5.84 us
  transfers between devices with their start and end apart: 26, of which 9 were waited for; matrix products, arithmetic and copies ran while one was open for 0% of the time, Pallas kernels for 9%

profile of v5, /device:TPU:16, one launch (start us, length us, event | category | flops | bytes accessed | tf_op | source)
XLA Modules:
  0.0 112.1 jit_solution(8723075165327080615)
XLA Ops:
  0.0 2.0 %collective-permute-start = (bf16[512,768]{1,0:T(8,128)(2,1)}, bf16[512,768]{1,0:T(8,128)(2,1)S(1)}, u32[]{:S(2)}, u32[]{:S(2)}) collective-permute-start(bf16[512,768]{1,0:T(8,128)(2,1)} %f_ref.1), channel_id=1, source_target_pairs={{0,2},{2,0},{1,3},{3,1},{4,6},{6,4},{5,7},{7,5},{8,10},{10,8},{9,1... | collective-permute-start | bytes 2359304 | tf_op jit(solution)/shard_map/ppermute | solution.py:233
  2.0 18.9 %collective-permute-done.f_ref = bf16[512,768]{1,0:T(8,128)(2,1)S(1)} collective-permute-done((bf16[512,768]{1,0:T(8,128)(2,1)}, bf16[512,768]{1,0:T(8,128)(2,1)S(1)}, u32[]{:S(2)}, u32[]{:S(2)}) %collective-permute-start) | collective-permute-done | bytes 786464 | tf_op jit(solution)/shard_map/ppermute | solution.py:233
  21.0 2.3 %copy-done.1 = bf16[3,768,1024]{2,1,0:T(8,128)(2,1)S(1)} copy-done((bf16[3,768,1024]{2,1,0:T(8,128)(2,1)S(1)}, bf16[3,768,1024]{2,1,0:T(8,128)(2,1)}, u32[]{:S(2)}) %copy-start.1) | copy-done | bytes 4718616
  23.3 1.1 %copy-done.4 = bf16[512,768]{1,0:T(8,128)(2,1)S(1)} copy-done((bf16[512,768]{1,0:T(8,128)(2,1)S(1)}, bf16[512,768]{1,0:T(8,128)(2,1)}, u32[]{:S(2)}) %copy-start.4) | copy-done | bytes 786456
  24.5 2.9 %shard_map.73.refs_0_ = bf16[12,128,1024]{2,1,0:T(8,128)(2,1)S(1)} custom-call(bf16[512,768]{1,0:T(8,128)(2,1)S(1)} %copy-done.4, bf16[3,768,1024]{2,1,0:T(8,128)(2,1)S(1)} %copy-done.1), custom_call_target="tpu_custom_call" | custom-call | flops 2415919104 | bytes 8388608 | tf_op jit(solution)/shard_map/pallas_call | solution.py:40
  27.4 3.0 %shard_map.75.refs_2_ = bf16[12,128,1024]{2,1,0:T(8,128)(2,1)S(1)} custom-call(bf16[512,768]{1,0:T(8,128)(2,1)S(1)} %collective-permute-done.f_ref, bf16[3,768,1024]{2,1,0:T(8,128)(2,1)S(1)} %copy-done.2), custom_call_target="tpu_custom_call" | custom-call | flops 2415919104 | bytes 8388608 | tf_op jit(solution)/shard_map/pallas_call | solution.py:40
  30.4 3.0 %shard_map.74.refs_1_ = bf16[12,128,1024]{2,1,0:T(8,128)(2,1)S(1)} custom-call(bf16[512,768]{1,0:T(8,128)(2,1)S(1)} %collective-permute-done.2.f_ref, bf16[3,768,1024]{2,1,0:T(8,128)(2,1)S(1)} %copy-done.2), custom_call_target="tpu_custom_call" | custom-call | flops 2415919104 | bytes 8388608 | tf_op jit(solution)/shard_map/pallas_call | solution.py:40
  33.4 10.3 %shard_map.76 = (bf16[256,384]{1,0:T(8,128)(2,1)S(1)}, bf16[256,384]{1,0:T(8,128)(2,1)S(1)}, bf16[256,384]{1,0:T(8,128)(2,1)S(1)}, bf16[256,384]{1,0:T(8,128)(2,...) custom-call(s32[4,16]{1,0:T(4,128)S(1)} %bitcast.7, ...), custom_call_target="tpu_custom_call" | custom-call | flops 6442450944 | bytes 20971520 | tf_op jit(solution)/shard_map/pallas_call | solution.py:115
  43.8 1.6 %collective-permute-start.3 = (bf16[256,384]{1,0:T(8,128)(2,1)S(1)}, bf16[256,384]{1,0:T(8,128)(2,1)S(1)}, u32[]{:S(2)}, u32[]{:S(2)}) collective-permute-start(bf16[256,384]{1,0:T(8,128)(2,1)S(1)} %get-tuple-element.47), channel_id=1, source_target_pairs={{0,8},{8,16},{16,24},{24,0},{1,9},{9,17},{17,25},{25,1},{2,10},{10... | collective-permute-start | bytes 589832 | tf_op jit(solution)/shard_map/ppermute | solution.py:226
  45.4 1.7 %collective-permute-start.4 = (bf16[256,384]{1,0:T(8,128)(2,1)S(1)}, bf16[256,384]{1,0:T(8,128)(2,1)S(1)}, u32[]{:S(2)}, u32[]{:S(2)}) collective-permute-start(bf16[256,384]{1,0:T(8,128)(2,1)S(1)} %get-tuple-element.48), channel_id=1, source_target_pairs={{0,24},{8,0},{16,8},{24,16},{1,25},{9,1},{17,9},{25,17},{2,26},{10... | collective-permute-start | bytes 589832 | tf_op jit(solution)/shard_map/ppermute | solution.py:226
  47.1 1.3 %collective-permute-start.8 = (bf16[4,256,256]{2,1,0:T(8,128)(2,1)S(1)}, bf16[4,256,256]{2,1,0:T(8,128)(2,1)S(1)}, u32[]{:S(2)}, u32[]{:S(2)}) collective-permute-start(bf16[4,256,256]{2,1,0:T(8,128)(2,1)S(1)} %get-tuple-element.54), channel_id=1, source_target_pairs={{0,4},{4,0},{1,5},{5,1},{2,6},{6,2},{3,7},{7,3},{8,12},{12,8},{9,1... | collective-permute-start | bytes 1572872 | tf_op jit(solution)/shard_map/ppermute | solution.py:255
  48.4 4.0 %collective-permute-done.3.left = bf16[256,384]{1,0:T(8,128)(2,1)S(1)} collective-permute-done((bf16[256,384]{1,0:T(8,128)(2,1)S(1)}, bf16[256,384]{1,0:T(8,128)(2,1)S(1)}, u32[]{:S(2)}, u32[]{:S(2)}) %collective-permute-start.3) | collective-permute-done | bytes 196640 | tf_op jit(solution)/shard_map/ppermute | solution.py:226
  52.5 1.6 %collective-permute-start.5 = (bf16[2,256,384]{2,1,0:T(8,128)(2,1)S(1)}, bf16[2,256,384]{2,1,0:T(8,128)(2,1)S(1)}, u32[]{:S(2)}, u32[]{:S(2)}) collective-permute-start(bf16[2,256,384]{2,1,0:T(8,128)(2,1)S(1)} %get-tuple-element.49), channel_id=1, source_target_pairs={{0,8},{8,16},{16,24},{24,0},{1,9},{9,17},{17,25},{25,1},{2,10},{10... | collective-permute-start | bytes 1179656 | tf_op jit(solution)/shard_map/ppermute | solution.py:226
  54.1 1.8 %collective-permute-start.6 = (bf16[2,256,384]{2,1,0:T(8,128)(2,1)S(1)}, bf16[2,256,384]{2,1,0:T(8,128)(2,1)S(1)}, u32[]{:S(2)}, u32[]{:S(2)}) collective-permute-start(bf16[2,256,384]{2,1,0:T(8,128)(2,1)S(1)} %get-tuple-element.50), channel_id=1, source_target_pairs={{0,24},{8,0},{16,8},{24,16},{1,25},{9,1},{17,9},{25,17},{2,26},{10... | collective-permute-start | bytes 1179656 | tf_op jit(solution)/shard_map/ppermute | solution.py:226
  55.8 1.9 %collective-permute-start.13 = (bf16[128,384]{1,0:T(8,128)(2,1)S(1)}, bf16[128,384]{1,0:T(8,128)(2,1)S(1)}, u32[]{:S(2)}, u32[]{:S(2)}) collective-permute-start(bf16[128,384]{1,0:T(8,128)(2,1)S(1)} %get-tuple-element.69), channel_id=1, source_target_pairs={{0,32},{32,64},{64,96},{96,128},{128,160},{160,192},{192,224},{224... | collective-permute-start | bytes 294920 | tf_op jit(solution)/shard_map/ppermute | solution.py:222
  57.7 3.9 %collective-permute-start.14 = (bf16[128,384]{1,0:T(8,128)(2,1)S(1)}, bf16[128,384]{1,0:T(8,128)(2,1)S(1)}, u32[]{:S(2)}, u32[]{:S(2)}) collective-permute-start(bf16[128,384]{1,0:T(8,128)(2,1)S(1)} %get-tuple-element.70), channel_id=1, source_target_pairs={{0,224},{32,0},{64,32},{96,64},{128,96},{160,128},{192,160},{224,1... | collective-permute-start | bytes 294920 | tf_op jit(solution)/shard_map/ppermute | solution.py:222
  61.7 2.6 %collective-permute-done.13.left = bf16[128,384]{1,0:T(8,128)(2,1)S(1)} collective-permute-done((bf16[128,384]{1,0:T(8,128)(2,1)S(1)}, bf16[128,384]{1,0:T(8,128)(2,1)S(1)}, u32[]{:S(2)}, u32[]{:S(2)}) %collective-permute-start.13) | collective-permute-done | bytes 98336 | tf_op jit(solution)/shard_map/ppermute | solution.py:222
  64.4 3.3 %collective-permute-start.16 = (bf16[256,384]{1,0:T(8,128)(2,1)S(1)}, bf16[256,384]{1,0:T(8,128)(2,1)S(1)}, u32[]{:S(2)}, u32[]{:S(2)}) collective-permute-start(bf16[256,384]{1,0:T(8,128)(2,1)S(1)} %get-tuple-element.72), channel_id=1, source_target_pairs={{0,224},{32,0},{64,32},{96,64},{128,96},{160,128},{192,160},{224,1... | collective-permute-start | bytes 589832 | tf_op jit(solution)/shard_map/ppermute | solution.py:222
  67.8 2.0 %collective-permute-start.10 = (bf16[128,256]{1,0:T(8,128)(2,1)S(1)}, bf16[128,256]{1,0:T(8,128)(2,1)S(1)}, u32[]{:S(2)}, u32[]{:S(2)}) collective-permute-start(bf16[128,256]{1,0:T(8,128)(2,1)S(1)} %get-tuple-element.59), channel_id=1, source_target_pairs={{0,24},{8,0},{16,8},{24,16},{1,25},{9,1},{17,9},{25,17},{2,26},{10... | collective-permute-start | bytes 196616 | tf_op jit(solution)/shard_map/ppermute | solution.py:226
  70.3 1.4 %collective-permute-start.7 = (bf16[256,384]{1,0:T(8,128)(2,1)S(1)}, bf16[256,384]{1,0:T(8,128)(2,1)S(1)}, u32[]{:S(2)}, u32[]{:S(2)}) collective-permute-start(bf16[256,384]{1,0:T(8,128)(2,1)S(1)} %get-tuple-element.52), channel_id=1, source_target_pairs={{0,4},{4,0},{1,5},{5,1},{2,6},{6,2},{3,7},{7,3},{8,12},{12,8},{9,1... | collective-permute-start | bytes 589832 | tf_op jit(solution)/shard_map/ppermute | solution.py:265
  71.8 2.7 %collective-permute-start.17 = (bf16[256,384]{1,0:T(8,128)(2,1)S(1)}, bf16[256,384]{1,0:T(8,128)(2,1)S(1)}, u32[]{:S(2)}, u32[]{:S(2)}) collective-permute-start(bf16[256,384]{1,0:T(8,128)(2,1)S(1)} %get-tuple-element.73), channel_id=1, source_target_pairs={{0,32},{32,64},{64,96},{96,128},{128,160},{160,192},{192,224},{224... | collective-permute-start | bytes 589832 | tf_op jit(solution)/shard_map/ppermute | solution.py:222
  75.5 3.2 %collective-permute-start.12 = (bf16[256,256]{1,0:T(8,128)(2,1)S(1)}, bf16[256,256]{1,0:T(8,128)(2,1)S(1)}, u32[]{:S(2)}, u32[]{:S(2)}) collective-permute-start(bf16[256,256]{1,0:T(8,128)(2,1)S(1)} %get-tuple-element.61), channel_id=1, source_target_pairs={{0,24},{8,0},{16,8},{24,16},{1,25},{9,1},{17,9},{25,17},{2,26},{10... | collective-permute-start | bytes 393224 | tf_op jit(solution)/shard_map/ppermute | solution.py:226
  78.7 2.9 %collective-permute-done.11.left = bf16[256,256]{1,0:T(8,128)(2,1)S(1)} collective-permute-done((bf16[256,256]{1,0:T(8,128)(2,1)S(1)}, bf16[256,256]{1,0:T(8,128)(2,1)S(1)}, u32[]{:S(2)}, u32[]{:S(2)}) %collective-permute-start.11) | collective-permute-done | bytes 131104 | tf_op jit(solution)/shard_map/ppermute | solution.py:226
  82.5 5.8 %all-to-all-start = ((bf16[8,32,640]{2,1,0:T(8,128)(2,1)}), bf16[8,32,640]{2,1,0:T(8,128)(2,1)S(1)}, u32[]{:S(2)}, u32[]{:S(2)}) async-start(bf16[8,32,640]{2,1,0:T(8,128)(2,1)} %shard_map.81), calls=%async_computation | async-start | bytes 655360 | tf_op jit(solution)/shard_map/all_to_all | solution.py:218
  88.4 2.1 %collective-permute-start.19 = (bf16[256,384]{1,0:T(8,128)(2,1)S(1)}, bf16[256,384]{1,0:T(8,128)(2,1)S(1)}, u32[]{:S(2)}, u32[]{:S(2)}) collective-permute-start(bf16[256,384]{1,0:T(8,128)(2,1)S(1)} %get-tuple-element.75), channel_id=1, source_target_pairs={{0,32},{32,64},{64,96},{96,128},{128,160},{160,192},{192,224},{224... | collective-permute-start | bytes 589832 | tf_op jit(solution)/shard_map/ppermute | solution.py:222
  90.5 1.3 %collective-permute-start.20 = (bf16[256,384]{1,0:T(8,128)(2,1)S(1)}, bf16[256,384]{1,0:T(8,128)(2,1)S(1)}, u32[]{:S(2)}, u32[]{:S(2)}) collective-permute-start(bf16[256,384]{1,0:T(8,128)(2,1)S(1)} %get-tuple-element.76), channel_id=1, source_target_pairs={{0,224},{32,0},{64,32},{96,64},{128,96},{160,128},{192,160},{224,1... | collective-permute-start | bytes 589832 | tf_op jit(solution)/shard_map/ppermute | solution.py:222
  91.8 6.9 %collective-permute-done.19.left = bf16[256,384]{1,0:T(8,128)(2,1)S(1)} collective-permute-done((bf16[256,384]{1,0:T(8,128)(2,1)S(1)}, bf16[256,384]{1,0:T(8,128)(2,1)S(1)}, u32[]{:S(2)}, u32[]{:S(2)}) %collective-permute-start.19) | collective-permute-done | bytes 196640 | tf_op jit(solution)/shard_map/ppermute | solution.py:222
  99.7 3.6 %collective-permute-start.22 = (bf16[2,32,384]{2,1,0:T(8,128)(2,1)S(1)}, bf16[2,32,384]{2,1,0:T(8,128)(2,1)S(1)}, u32[]{:S(2)}, u32[]{:S(2)}) collective-permute-start(bf16[2,32,384]{2,1,0:T(8,128)(2,1)S(1)} %get-tuple-element.79), channel_id=1, source_target_pairs={{0,16},{8,24},{16,0},{24,8},{1,17},{9,25},{17,1},{25,9},{2,18},{10... | collective-permute-start | bytes 147464 | tf_op jit(solution)/shard_map/ppermute | solution.py:226
  104.2 1.7 %collective-permute-done.22.s2 = bf16[2,32,384]{2,1,0:T(8,128)(2,1)S(1)} collective-permute-done((bf16[2,32,384]{2,1,0:T(8,128)(2,1)S(1)}, bf16[2,32,384]{2,1,0:T(8,128)(2,1)S(1)}, u32[]{:S(2)}, u32[]{:S(2)}) %collective-permute-start.22) | collective-permute-done | bytes 49184 | tf_op jit(solution)/shard_map/ppermute | solution.py:226
  105.9 1.5 %collective-permute-done.23.s3 = bf16[2,32,384]{2,1,0:T(8,128)(2,1)S(1)} collective-permute-done((bf16[2,32,384]{2,1,0:T(8,128)(2,1)S(1)}, bf16[2,32,384]{2,1,0:T(8,128)(2,1)S(1)}, u32[]{:S(2)}, u32[]{:S(2)}) %collective-permute-start.23) | collective-permute-done | bytes 49184 | tf_op jit(solution)/shard_map/ppermute | solution.py:226
  107.4 1.4 %collective-permute-start.24 = (bf16[32,384]{1,0:T(8,128)(2,1)S(1)}, bf16[32,384]{1,0:T(8,128)(2,1)S(1)}, u32[]{:S(2)}, u32[]{:S(2)}) collective-permute-start(bf16[32,384]{1,0:T(8,128)(2,1)S(1)} %get-tuple-element.82), channel_id=1, source_target_pairs={{0,4},{4,0},{1,5},{5,1},{2,6},{6,2},{3,7},{7,3},{8,12},{12,8},{9,1... | collective-permute-start | bytes 73736 | tf_op jit(solution)/shard_map/ppermute | solution.py:274
  109.2 2.2 %collective-permute-done.24.other = bf16[32,384]{1,0:T(8,128)(2,1)S(1)} collective-permute-done((bf16[32,384]{1,0:T(8,128)(2,1)S(1)}, bf16[32,384]{1,0:T(8,128)(2,1)S(1)}, u32[]{:S(2)}, u32[]{:S(2)}) %collective-permute-start.24) | collective-permute-done | bytes 24608 | tf_op jit(solution)/shard_map/ppermute | solution.py:274
  (52 shorter events, 5.9 us)
Async XLA Ops:
  0.0 108.8 %copy-start = (bf16[768,1024]{1,0:T(8,128)(2,1)S(1)}, bf16[768,1024]{1,0:T(8,128)(2,1)}, u32[]{:S(2)}) copy-start(bf16[768,1024]{1,0:T(8,128)(2,1)} %param.10) | copy-start | bytes 4718596
  0.0 21.0 %collective-permute-start = (bf16[512,768]{1,0:T(8,128)(2,1)}, bf16[512,768]{1,0:T(8,128)(2,1)S(1)}, u32[]{:S(2)}, u32[]{:S(2)}) collective-permute-start(bf16[512,768]{1,0:T(8,128)(2,1)} %f_ref.1), channel_id=1, source_target_pairs={{0,2},{2,0},{1,3},{3,1},{4,6},{6,4},{5,7},{7,5},{8,10},{10,8},{9,1... | collective-permute-start | bytes 2359304 | tf_op jit(solution)/shard_map/ppermute | solution.py:233
  2.0 28.4 %collective-permute-start.2 = (bf16[512,768]{1,0:T(8,128)(2,1)}, bf16[512,768]{1,0:T(8,128)(2,1)S(1)}, u32[]{:S(2)}, u32[]{:S(2)}) collective-permute-start(bf16[512,768]{1,0:T(8,128)(2,1)} %f_ref.1), channel_id=1, source_target_pairs={{0,1},{1,0},{2,3},{3,2},{4,5},{5,4},{6,7},{7,6},{8,9},{9,8},{10,11... | collective-permute-start | bytes 2359304 | tf_op jit(solution)/shard_map/ppermute | solution.py:234
  21.0 12.4 %collective-permute-start.1 = (bf16[512,768]{1,0:T(8,128)(2,1)S(1)}, bf16[512,768]{1,0:T(8,128)(2,1)S(1)}, u32[]{:S(2)}, u32[]{:S(2)}) collective-permute-start(bf16[512,768]{1,0:T(8,128)(2,1)S(1)} %collective-permute-done.f_ref), channel_id=1, source_target_pairs={{0,1},{1,0},{2,3},{3,2},{4,5},{5,4},{6,7},{7,6},{8,9},{9,8},{10,11... | collective-permute-start | bytes 2359304 | tf_op jit(solution)/shard_map/ppermute | solution.py:240
  24.5 3.0 %copy-start.2 = (bf16[3,768,1024]{2,1,0:T(8,128)(2,1)S(1)}, bf16[3,768,1024]{2,1,0:T(8,128)(2,1)}, u32[]{:S(2)}) copy-start(bf16[3,768,1024]{2,1,0:T(8,128)(2,1)} %w_ref.7) | copy-start | bytes 14155780
  30.4 3.0 %copy-start.3 = (bf16[1,16,4,128,128]{4,3,2,1,0:T(8,128)(2,1)S(1)}, bf16[1,16,4,128,128]{4,3,2,1,0:T(8,128)(2,1)}, u32[]{:S(2)}) copy-start(bf16[1,16,4,128,128]{4,3,2,1,0:T(8,128)(2,1)} %param.11) | copy-start | bytes 6291460
  30.4 3.0 %copy-start.5 = (s32[1,16,4]{1,2,0:T(4,128)S(1)}, s32[1,16,4]{1,2,0:T(4,128)}, u32[]{:S(2)}) copy-start(s32[1,16,4]{1,2,0:T(4,128)} %param.12) | copy-start | bytes 772
  30.4 3.0 %copy-start.6 = (s32[1,16]{1,0:T(1,128)S(1)}, s32[1,16]{1,0:T(1,128)}, u32[]{:S(2)}) copy-start(s32[1,16]{1,0:T(1,128)} %cnt_ref.1) | copy-start | bytes 196
  43.8 8.6 %collective-permute-start.3 = (bf16[256,384]{1,0:T(8,128)(2,1)S(1)}, bf16[256,384]{1,0:T(8,128)(2,1)S(1)}, u32[]{:S(2)}, u32[]{:S(2)}) collective-permute-start(bf16[256,384]{1,0:T(8,128)(2,1)S(1)} %get-tuple-element.47), channel_id=1, source_target_pairs={{0,8},{8,16},{16,24},{24,0},{1,9},{9,17},{17,25},{25,1},{2,10},{10... | collective-permute-start | bytes 589832 | tf_op jit(solution)/shard_map/ppermute | solution.py:226
  45.4 7.0 %collective-permute-start.4 = (bf16[256,384]{1,0:T(8,128)(2,1)S(1)}, bf16[256,384]{1,0:T(8,128)(2,1)S(1)}, u32[]{:S(2)}, u32[]{:S(2)}) collective-permute-start(bf16[256,384]{1,0:T(8,128)(2,1)S(1)} %get-tuple-element.48), channel_id=1, source_target_pairs={{0,24},{8,0},{16,8},{24,16},{1,25},{9,1},{17,9},{25,17},{2,26},{10... | collective-permute-start | bytes 589832 | tf_op jit(solution)/shard_map/ppermute | solution.py:226
  47.1 20.6 %collective-permute-start.8 = (bf16[4,256,256]{2,1,0:T(8,128)(2,1)S(1)}, bf16[4,256,256]{2,1,0:T(8,128)(2,1)S(1)}, u32[]{:S(2)}, u32[]{:S(2)}) collective-permute-start(bf16[4,256,256]{2,1,0:T(8,128)(2,1)S(1)} %get-tuple-element.54), channel_id=1, source_target_pairs={{0,4},{4,0},{1,5},{5,1},{2,6},{6,2},{3,7},{7,3},{8,12},{12,8},{9,1... | collective-permute-start | bytes 1572872 | tf_op jit(solution)/shard_map/ppermute | solution.py:255
  52.5 17.4 %collective-permute-start.5 = (bf16[2,256,384]{2,1,0:T(8,128)(2,1)S(1)}, bf16[2,256,384]{2,1,0:T(8,128)(2,1)S(1)}, u32[]{:S(2)}, u32[]{:S(2)}) collective-permute-start(bf16[2,256,384]{2,1,0:T(8,128)(2,1)S(1)} %get-tuple-element.49), channel_id=1, source_target_pairs={{0,8},{8,16},{16,24},{24,0},{1,9},{9,17},{17,25},{25,1},{2,10},{10... | collective-permute-start | bytes 1179656 | tf_op jit(solution)/shard_map/ppermute | solution.py:226
  54.1 16.1 %collective-permute-start.6 = (bf16[2,256,384]{2,1,0:T(8,128)(2,1)S(1)}, bf16[2,256,384]{2,1,0:T(8,128)(2,1)S(1)}, u32[]{:S(2)}, u32[]{:S(2)}) collective-permute-start(bf16[2,256,384]{2,1,0:T(8,128)(2,1)S(1)} %get-tuple-element.50), channel_id=1, source_target_pairs={{0,24},{8,0},{16,8},{24,16},{1,25},{9,1},{17,9},{25,17},{2,26},{10... | collective-permute-start | bytes 1179656 | tf_op jit(solution)/shard_map/ppermute | solution.py:226
  55.8 8.4 %collective-permute-start.13 = (bf16[128,384]{1,0:T(8,128)(2,1)S(1)}, bf16[128,384]{1,0:T(8,128)(2,1)S(1)}, u32[]{:S(2)}, u32[]{:S(2)}) collective-permute-start(bf16[128,384]{1,0:T(8,128)(2,1)S(1)} %get-tuple-element.69), channel_id=1, source_target_pairs={{0,32},{32,64},{64,96},{96,128},{128,160},{160,192},{192,224},{224... | collective-permute-start | bytes 294920 | tf_op jit(solution)/shard_map/ppermute | solution.py:222
  57.7 6.5 %collective-permute-start.14 = (bf16[128,384]{1,0:T(8,128)(2,1)S(1)}, bf16[128,384]{1,0:T(8,128)(2,1)S(1)}, u32[]{:S(2)}, u32[]{:S(2)}) collective-permute-start(bf16[128,384]{1,0:T(8,128)(2,1)S(1)} %get-tuple-element.70), channel_id=1, source_target_pairs={{0,224},{32,0},{64,32},{96,64},{128,96},{160,128},{192,160},{224,1... | collective-permute-start | bytes 294920 | tf_op jit(solution)/shard_map/ppermute | solution.py:222
  64.3 7.3 %collective-permute-start.15 = (bf16[256,384]{1,0:T(8,128)(2,1)S(1)}, bf16[256,384]{1,0:T(8,128)(2,1)S(1)}, u32[]{:S(2)}, u32[]{:S(2)}) collective-permute-start(bf16[256,384]{1,0:T(8,128)(2,1)S(1)} %get-tuple-element.71), channel_id=1, source_target_pairs={{0,32},{32,64},{64,96},{96,128},{128,160},{160,192},{192,224},{224... | collective-permute-start | bytes 589832 | tf_op jit(solution)/shard_map/ppermute | solution.py:222
  64.4 7.3 %collective-permute-start.16 = (bf16[256,384]{1,0:T(8,128)(2,1)S(1)}, bf16[256,384]{1,0:T(8,128)(2,1)S(1)}, u32[]{:S(2)}, u32[]{:S(2)}) collective-permute-start(bf16[256,384]{1,0:T(8,128)(2,1)S(1)} %get-tuple-element.72), channel_id=1, source_target_pairs={{0,224},{32,0},{64,32},{96,64},{128,96},{160,128},{192,160},{224,1... | collective-permute-start | bytes 589832 | tf_op jit(solution)/shard_map/ppermute | solution.py:222
  67.8 7.2 %collective-permute-start.10 = (bf16[128,256]{1,0:T(8,128)(2,1)S(1)}, bf16[128,256]{1,0:T(8,128)(2,1)S(1)}, u32[]{:S(2)}, u32[]{:S(2)}) collective-permute-start(bf16[128,256]{1,0:T(8,128)(2,1)S(1)} %get-tuple-element.59), channel_id=1, source_target_pairs={{0,24},{8,0},{16,8},{24,16},{1,25},{9,1},{17,9},{25,17},{2,26},{10... | collective-permute-start | bytes 196616 | tf_op jit(solution)/shard_map/ppermute | solution.py:226
  69.9 5.5 %collective-permute-start.9 = (bf16[128,256]{1,0:T(8,128)(2,1)S(1)}, bf16[128,256]{1,0:T(8,128)(2,1)S(1)}, u32[]{:S(2)}, u32[]{:S(2)}) collective-permute-start(bf16[128,256]{1,0:T(8,128)(2,1)S(1)} %get-tuple-element.58), channel_id=1, source_target_pairs={{0,8},{8,16},{16,24},{24,0},{1,9},{9,17},{17,25},{25,1},{2,10},{10... | collective-permute-start | bytes 196616 | tf_op jit(solution)/shard_map/ppermute | solution.py:226
  70.3 11.3 %collective-permute-start.7 = (bf16[256,384]{1,0:T(8,128)(2,1)S(1)}, bf16[256,384]{1,0:T(8,128)(2,1)S(1)}, u32[]{:S(2)}, u32[]{:S(2)}) collective-permute-start(bf16[256,384]{1,0:T(8,128)(2,1)S(1)} %get-tuple-element.52), channel_id=1, source_target_pairs={{0,4},{4,0},{1,5},{5,1},{2,6},{6,2},{3,7},{7,3},{8,12},{12,8},{9,1... | collective-permute-start | bytes 589832 | tf_op jit(solution)/shard_map/ppermute | solution.py:265
  71.7 37.1 %copy-start.7 = (bf16[32,768]{1,0:T(8,128)(2,1)S(1)}, bf16[32,768]{1,0:T(8,128)(2,1)}, u32[]{:S(2)}) copy-start(bf16[32,768]{1,0:T(8,128)(2,1)} %param.8) | copy-start | bytes 147460
  71.8 16.5 %collective-permute-start.17 = (bf16[256,384]{1,0:T(8,128)(2,1)S(1)}, bf16[256,384]{1,0:T(8,128)(2,1)S(1)}, u32[]{:S(2)}, u32[]{:S(2)}) collective-permute-start(bf16[256,384]{1,0:T(8,128)(2,1)S(1)} %get-tuple-element.73), channel_id=1, source_target_pairs={{0,32},{32,64},{64,96},{96,128},{128,160},{160,192},{192,224},{224... | collective-permute-start | bytes 589832 | tf_op jit(solution)/shard_map/ppermute | solution.py:222
  74.5 13.8 %collective-permute-start.18 = (bf16[256,384]{1,0:T(8,128)(2,1)S(1)}, bf16[256,384]{1,0:T(8,128)(2,1)S(1)}, u32[]{:S(2)}, u32[]{:S(2)}) collective-permute-start(bf16[256,384]{1,0:T(8,128)(2,1)S(1)} %get-tuple-element.74), channel_id=1, source_target_pairs={{0,224},{32,0},{64,32},{96,64},{128,96},{160,128},{192,160},{224,1... | collective-permute-start | bytes 589832 | tf_op jit(solution)/shard_map/ppermute | solution.py:222
  75.4 6.3 %collective-permute-start.11 = (bf16[256,256]{1,0:T(8,128)(2,1)S(1)}, bf16[256,256]{1,0:T(8,128)(2,1)S(1)}, u32[]{:S(2)}, u32[]{:S(2)}) collective-permute-start(bf16[256,256]{1,0:T(8,128)(2,1)S(1)} %get-tuple-element.60), channel_id=1, source_target_pairs={{0,8},{8,16},{16,24},{24,0},{1,9},{9,17},{17,25},{25,1},{2,10},{10... | collective-permute-start | bytes 393224 | tf_op jit(solution)/shard_map/ppermute | solution.py:226
  75.5 6.1 %collective-permute-start.12 = (bf16[256,256]{1,0:T(8,128)(2,1)S(1)}, bf16[256,256]{1,0:T(8,128)(2,1)S(1)}, u32[]{:S(2)}, u32[]{:S(2)}) collective-permute-start(bf16[256,256]{1,0:T(8,128)(2,1)S(1)} %get-tuple-element.61), channel_id=1, source_target_pairs={{0,24},{8,0},{16,8},{24,16},{1,25},{9,1},{17,9},{25,17},{2,26},{10... | collective-permute-start | bytes 393224 | tf_op jit(solution)/shard_map/ppermute | solution.py:226
  82.5 28.9 %all-to-all-start = ((bf16[8,32,640]{2,1,0:T(8,128)(2,1)}), bf16[8,32,640]{2,1,0:T(8,128)(2,1)S(1)}, u32[]{:S(2)}, u32[]{:S(2)}) async-start(bf16[8,32,640]{2,1,0:T(8,128)(2,1)} %shard_map.81), calls=%async_computation | async-start | bytes 655360 | tf_op jit(solution)/shard_map/all_to_all | solution.py:218
  88.4 10.3 %collective-permute-start.19 = (bf16[256,384]{1,0:T(8,128)(2,1)S(1)}, bf16[256,384]{1,0:T(8,128)(2,1)S(1)}, u32[]{:S(2)}, u32[]{:S(2)}) collective-permute-start(bf16[256,384]{1,0:T(8,128)(2,1)S(1)} %get-tuple-element.75), channel_id=1, source_target_pairs={{0,32},{32,64},{64,96},{96,128},{128,160},{160,192},{192,224},{224... | collective-permute-start | bytes 589832 | tf_op jit(solution)/shard_map/ppermute | solution.py:222
  90.5 8.2 %collective-permute-start.20 = (bf16[256,384]{1,0:T(8,128)(2,1)S(1)}, bf16[256,384]{1,0:T(8,128)(2,1)S(1)}, u32[]{:S(2)}, u32[]{:S(2)}) collective-permute-start(bf16[256,384]{1,0:T(8,128)(2,1)S(1)} %get-tuple-element.76), channel_id=1, source_target_pairs={{0,224},{32,0},{64,32},{96,64},{128,96},{160,128},{192,160},{224,1... | collective-permute-start | bytes 589832 | tf_op jit(solution)/shard_map/ppermute | solution.py:222
  98.8 5.4 %collective-permute-start.21 = (bf16[2,32,384]{2,1,0:T(8,128)(2,1)S(1)}, bf16[2,32,384]{2,1,0:T(8,128)(2,1)S(1)}, u32[]{:S(2)}, u32[]{:S(2)}) collective-permute-start(bf16[2,32,384]{2,1,0:T(8,128)(2,1)S(1)} %get-tuple-element.78), channel_id=1, source_target_pairs={{0,8},{8,16},{16,24},{24,0},{1,9},{9,17},{17,25},{25,1},{2,10},{10... | collective-permute-start | bytes 147464 | tf_op jit(solution)/shard_map/ppermute | solution.py:226
  99.7 6.2 %collective-permute-start.22 = (bf16[2,32,384]{2,1,0:T(8,128)(2,1)S(1)}, bf16[2,32,384]{2,1,0:T(8,128)(2,1)S(1)}, u32[]{:S(2)}, u32[]{:S(2)}) collective-permute-start(bf16[2,32,384]{2,1,0:T(8,128)(2,1)S(1)} %get-tuple-element.79), channel_id=1, source_target_pairs={{0,16},{8,24},{16,0},{24,8},{1,17},{9,25},{17,1},{25,9},{2,18},{10... | collective-permute-start | bytes 147464 | tf_op jit(solution)/shard_map/ppermute | solution.py:226
  103.3 4.1 %collective-permute-start.23 = (bf16[2,32,384]{2,1,0:T(8,128)(2,1)S(1)}, bf16[2,32,384]{2,1,0:T(8,128)(2,1)S(1)}, u32[]{:S(2)}, u32[]{:S(2)}) collective-permute-start(bf16[2,32,384]{2,1,0:T(8,128)(2,1)S(1)} %get-tuple-element.80), channel_id=1, source_target_pairs={{0,24},{8,0},{16,8},{24,16},{1,25},{9,1},{17,9},{25,17},{2,26},{10... | collective-permute-start | bytes 147464 | tf_op jit(solution)/shard_map/ppermute | solution.py:226
  107.4 3.9 %collective-permute-start.24 = (bf16[32,384]{1,0:T(8,128)(2,1)S(1)}, bf16[32,384]{1,0:T(8,128)(2,1)S(1)}, u32[]{:S(2)}, u32[]{:S(2)}) collective-permute-start(bf16[32,384]{1,0:T(8,128)(2,1)S(1)} %get-tuple-element.82), channel_id=1, source_target_pairs={{0,4},{4,0},{1,5},{5,1},{2,6},{6,2},{3,7},{7,3},{8,12},{12,8},{9,1... | collective-permute-start | bytes 73736 | tf_op jit(solution)/shard_map/ppermute | solution.py:274
  (2 other events, 3.5 us)
